TPU v7x, 32 devices: a whole 2x2x4 slice. The times are simulated.
32 devices in a mesh: row: 8 (over y, x, core), col: 4 (over z).
Axes of the slice: x: 2, y: 2, z: 4, core: 2. Of those that a mesh axis runs over, the one named last changes fastest.
Arguments:
- features: bfloat16 [512, 16384], P('col', 'row'), may hold values from -6 to 6
- weight: bfloat16 [512, 512], replicated, may hold values from -0.25 to 0.25
- tile_cols: int32 [8, 256], P('row'), may hold values from 0 to 127, as said below
- tile_rows: int32 [8, 256], P('row'), may hold values from 0 to 15
- tile_count: int32 [8], P('row'), may hold values from 1 to 256, as said below
- tile_values: bfloat16 [2048, 128, 128], P('row'), may hold values from 0 to 0.049804688
- out_grad: bfloat16 [512, 16384], P('col', 'row'), may hold values from -6 to 6
Outputs:
- output: bfloat16 [512, 16384], P('col', 'row')
- input_grad: bfloat16 [512, 16384], P('col', 'row')
- weight_grad: float32 [512, 512], P(None, 'col')
Inputs may be any that keep to these rules, and one draw needn't show every extreme that they name: `tile_cols`: the column tiles used by the slots t < tile_count[r] of row index r that lie in the range of one other row index s (tiles s * 16 to s * 16 + 15) are at most 4 distinct ones, and some pair r, s has exactly 4. Slots past tile_count[r] hold in-range entries that are not used. `tile_count`: some row index uses all 256 slots.
All inputs are finite; a program needn't handle non-finite values.
Results may differ from a plain program's by a relative error of at most 0.0061.
Values may be sent and summed in bfloat16 or wider, within the bound.
No kernel may reach another device: no remote copies, remote signals or barrier semaphores. Data moves between devices by JAX's collectives and lax.ppermute only.
A program may use at most 128 MiB of HBM per device.

v0:
```python
import jax
import jax.numpy as jnp
from jax import lax
from jax.sharding import PartitionSpec as P

TILE = 128


def shards(features, weight, tile_cols, tile_rows, tile_count, tile_values, out_grad):
    n_row = lax.axis_size("row")
    col_self = lax.axis_index("col")
    f_loc, nodes_loc = features.shape
    h_loc = out_grad.shape[0]
    row_tiles = nodes_loc // TILE
    max_tiles = tile_cols.shape[1]
    col_ids = tile_cols[0]
    row_ids = tile_rows[0]
    slot_ids = jnp.arange(max_tiles, dtype=jnp.int32)
    in_use = slot_ids < tile_count[0]
    all_feats = lax.all_gather(features, "col", axis=0, tiled=True)
    w_mine = lax.dynamic_slice_in_dim(weight, col_self * h_loc, h_loc, 1)
    projected = jnp.einsum("fh,fn->hn", w_mine, all_feats, preferred_element_type=jnp.float32)
    projected = projected.astype(jnp.bfloat16).reshape(h_loc, row_tiles, TILE)
    sources_table = lax.all_gather(projected, "row", axis=1, tiled=True)
    picked = jnp.take(sources_table, col_ids, axis=1)
    products = jnp.einsum("htm,tnm->thn", picked, tile_values, preferred_element_type=jnp.float32)
    placing = (
        (row_ids[:, None] == jnp.arange(row_tiles, dtype=jnp.int32)[None, :]) & in_use[:, None]
    ).astype(jnp.float32)
    preact = jnp.einsum("ti,thn->hin", placing, products, precision=lax.Precision.HIGHEST)
    logistic = jax.nn.sigmoid(preact)
    output = (preact * logistic).astype(jnp.bfloat16)
    slope_v = logistic * (1.0 + preact * (1.0 - logistic))
    z_grad = (out_grad.reshape(h_loc, row_tiles, TILE).astype(jnp.float32) * slope_v).astype(
        jnp.bfloat16
    )
    picked_z = jnp.take(z_grad, row_ids, axis=1)
    back_terms = jnp.einsum(
        "htn,tnm->thm", picked_z, tile_values, preferred_element_type=jnp.float32
    )
    back_terms = back_terms * in_use.astype(jnp.float32)[:, None, None]
    spread = jax.ops.segment_sum(back_terms, col_ids, num_segments=n_row * row_tiles)
    summed = lax.psum_scatter(spread, "row", scatter_dimension=0, tiled=True)
    p_grad = summed.astype(jnp.bfloat16)
    w_term = jnp.einsum(
        "fbn,bhn->fh",
        all_feats.reshape(all_feats.shape[0], row_tiles, TILE),
        p_grad,
        preferred_element_type=jnp.float32,
    )
    weight_grad = lax.psum(w_term, "row") * float(nodes_loc * n_row) ** (-0.5)
    w_rows = lax.dynamic_slice_in_dim(weight, col_self * f_loc, f_loc, 0)
    grad_sum = jnp.einsum(
        "fh,bhn->fbn",
        w_rows,
        lax.all_gather(p_grad, "col", axis=1, tiled=True),
        preferred_element_type=jnp.float32,
    )
    input_grad = grad_sum.astype(jnp.bfloat16).reshape(f_loc, nodes_loc)
    return (output.reshape(h_loc, nodes_loc), input_grad, weight_grad)


def solution(mesh):
    return jax.shard_map(
        shards,
        mesh=mesh,
        in_specs=(
            P("col", "row"),
            P(),
            P("row", None),
            P("row", None),
            P("row"),
            P("row", None, None),
            P("col", "row"),
        ),
        out_specs=(P("col", "row"), P("col", "row"), P(None, "col")),
        check_vma=False,
    )
```

profile of v0, /device:TPU:0, one launch (start us, length us, event | category | flops | bytes accessed | tf_op | source)
XLA Modules:
  0.0 408.7 jit_solution(3409858486664761841)
XLA Ops:
  7.2 2.1 copy.22
  9.4 49.7 %all-gather.4.cloned.1.call-done = bf16[512,2048]{0,1:T(8,128)(2,1)} async-done(((bf16[128,2048]{0,1:T(8,128)(2,1)}), bf16[512,2048]{0,1:T(8,128)(2,1)}) %all-gather.4.cloned.1.call-update) | async-done | bytes 2097168 | tf_op jit(solution)/shard_map/all_gather | solution.py:20
  59.1 2.4 fusion.14
  61.6 0.9 copy.45
  63.2 1.1 convert_bitcast_fusion
  64.7 33.0 %all-gather.6.cloned.1.call-done = bf16[128,128,128]{2,0,1:T(8,128)(2,1)} async-done(((bf16[128,16,128]{2,0,1:T(8,128)(2,1)}), bf16[128,128,128]{2,0,1:T(8,128)(2,1)}) %all-gather.6.cloned.1.call-update) | async-done | bytes 4194320 | tf_op jit(solution)/shard_map/all_gather | solution.py:24
  97.6 10.8 %gather_fusion = bf16[256,128,128]{2,1,0:T(8,128)(2,1)} fusion(bf16[128,128,128]{2,0,1:T(8,128)(2,1)} %all-gather.6.cloned.1.call-done, s32[1024]{0:T(1024)S(1)} %pad_clamp_fusion.1), kind=kCustom, calls=%fused_computation | custom fusion | bytes 16778240 | tf_op jit(solution)/shard_map/jit(_take)/gather | solution.py:25
  108.4 12.8 %fusion.3 = f32[256,128,128]{2,1,0:T(8,128)} fusion(bf16[256,128,128]{2,1,0:T(8,128)(2,1)} %param.12, bf16[256,128,128]{2,1,0:T(8,128)(2,1)} %gather_fusion, pred[256]{0:T(512)(128)(4,1)S(1)} %compare_and_fusion.1), kind=kOutput, calls=%fused_computation.7 | convolution fusion | flops 1077936128 | bytes 33554688 | tf_op jit(solution)/shard_map/htm,tnm->thn/dot_general | solution.py:26
  121.2 14.1 %fusion.15 = (bf16[128,16,128]{2,1,0:T(8,128)(2,1)S(1)}, bf16[128,16,128]{2,1,0:T(8,128)(2,1)}) fusion(f32[16,8,16,128]{3,2,1,0:T(8,128)S(1)} %copy.35, s32[256]{0:T(256)S(1)} %bitcast.63, pred[256]{0:T(512)(128)(4,1)S(1)} %iota_compare_fusion.1, f32[256,128,128]{2,1,0:T(8,128)} %fusion.3), kind=kOutput, calls=%fused_computation.20 | convolution fusion | flops 808198144 | bytes 18875648 | tf_op jit(solution)/shard_map/ti,thn->hin/dot_general | solution.py:30
  135.4 8.6 %gather_fusion.1 = bf16[256,128,128]{2,1,0:T(8,128)(2,1)} fusion(bf16[128,16,128]{2,0,1:T(8,128)(2,1)S(1)} %copy.25, s32[1024]{0:T(1024)S(1)} %pad_clamp_fusion), kind=kCustom, calls=%fused_computation.1 | custom fusion | bytes 16778240 | tf_op jit(solution)/shard_map/jit(_take)/gather | solution.py:37
  144.0 14.0 %convolution_multiply_fusion = f32[256,128,128]{2,1,0:T(8,128)} fusion(bf16[256,128,128]{2,1,0:T(8,128)(2,1)} %param.12, bf16[256,128,128]{2,1,0:T(8,128)(2,1)} %gather_fusion.1, f32[256]{0:T(256)S(1)} %get-tuple-element.15, pred[256]{0:T(512)(128)(4,1)S(1)} %get-tuple-element.14), kind=kOutput, calls=%fused_computation.5 | convolution fusion | flops 1082130432 | bytes 33555712 | tf_op jit(solution)/shard_map/htn,tnm->thm/dot_general | solution.py:38
  158.1 4.3 %broadcast_in_dim.26 = f32[128,128,128]{2,1,0:T(8,128)} broadcast(f32[]{:T(128)} %constant.40.clone.1), dimensions={} | broadcast | bytes 8388612 | tf_op jit(solution)/shard_map/broadcast_in_dim | solution.py:42
  162.3 51.1 %scatter_fusion = f32[128,128,128]{2,1,0:T(8,128)} fusion(f32[128,128,128]{2,1,0:T(8,128)} %broadcast_in_dim.26, s32[256]{0:T(256)S(1)} %bitcast.65, f32[256,128,128]{2,1,0:T(8,128)} %convolution_multiply_fusion), kind=kCustom, calls=%fused_computation.2 | custom fusion | flops 4194304 | bytes 50332672 | tf_op jit(solution)/shard_map/scatter-add | solution.py:42
  213.5 9.0 %copy.26 = f32[128,128,128]{1,2,0:T(8,128)} copy(f32[128,128,128]{2,1,0:T(8,128)} %scatter_fusion) | data formatting | bytes 16777216 | tf_op jit(solution)/shard_map/scatter-add | solution.py:42
  222.6 71.8 %reduce-scatter.2.cloned.1.call-done = f32[16,128,128]{1,2,0:T(8,128)} async-done(((f32[128,128,128]{1,2,0:T(8,128)}), f32[16,128,128]{1,2,0:T(8,128)}) %reduce-scatter.2.cloned.1.call-update) | async-done | bytes 1048592 | tf_op jit(solution)/shard_map/reduce_scatter | solution.py:43
  294.3 1.3 convert_element_type.35
  295.6 1.2 convolution_bitcast_fusion
  297.4 2.0 copy.44
  299.4 52.2 %all-reduce.2.cloned.1.call-done = f32[512,128]{0,1:T(8,128)} async-done(((f32[512,128]{0,1:T(8,128)}), f32[512,128]{0,1:T(8,128)}) %all-reduce.2.cloned.1.call-update) | async-done | bytes 262160 | tf_op jit(solution)/shard_map/psum | solution.py:51
  351.7 1.0 broadcast_multiply_fusion
  352.6 0.8 copy.30
  353.5 45.3 %all-gather.8.cloned.1.call-done = bf16[16,512,128]{1,2,0:T(8,128)(2,1)} async-done(((bf16[16,128,128]{1,2,0:T(8,128)(2,1)}), bf16[16,512,128]{1,2,0:T(8,128)(2,1)}) %all-gather.8.cloned.1.call-update) | async-done | bytes 2097168 | tf_op jit(solution)/shard_map/all_gather | solution.py:56
  398.7 2.3 fusion.16
  401.1 1.0 copy.29
  (30 shorter events, 1.3 us)
Async XLA Ops:
  7.2 52.0 %copy-start = (bf16[512,512]{1,0:T(8,128)(2,1)S(1)}, bf16[512,512]{1,0:T(8,128)(2,1)}, u32[]{:S(2)}) copy-start(bf16[512,512]{1,0:T(8,128)(2,1)} %param.8) | copy-start | bytes 1572868
  7.2 57.4 %copy-start.3 = (s32[1,256]{1,0:T(1,128)S(1)}, s32[1,256]{1,0:T(1,128)}, u32[]{:S(2)}) copy-start(s32[1,256]{1,0:T(1,128)} %param.10) | copy-start | bytes 3076
  7.2 57.4 %copy-start.4 = (s32[1,256]{1,0:T(1,128)S(1)}, s32[1,256]{1,0:T(1,128)}, u32[]{:S(2)}) copy-start(s32[1,256]{1,0:T(1,128)} %param.9) | copy-start | bytes 3076
  7.2 51.9 %all-gather.4.cloned.1.call-start = ((), (), s32[]{:S(2)}) async-start(), calls=%async_computation.1 | async-start | bytes 2621440 | tf_op jit(solution)/shard_map/all_gather | solution.py:20
  9.4 88.3 %all-gather.6.cloned.1.call-start = ((), (), s32[]{:S(2)}) async-start(), calls=%async_computation.2 | async-start | bytes 4718592 | tf_op jit(solution)/shard_map/all_gather | solution.py:24
  62.5 231.8 %reduce-scatter.2.cloned.1.call-start = ((), (), s32[]{:S(2)}) async-start(), calls=%async_computation.3 | async-start | bytes 9437184 | tf_op jit(solution)/shard_map/reduce_scatter | solution.py:43
  222.5 73.2 %copy-start.1 = (bf16[512,2048]{0,1:T(8,128)(2,1)S(1)}, bf16[512,2048]{0,1:T(8,128)(2,1)}, u32[]{:S(2)}) copy-start(bf16[512,2048]{0,1:T(8,128)(2,1)} %all-gather.4.cloned.1.call-done) | copy-start | bytes 6291460
  222.5 129.2 %all-reduce.2.cloned.1.call-start = ((), (), s32[]{:S(2)}) async-start(), calls=%async_computation.5 | async-start | bytes 524288 | tf_op jit(solution)/shard_map/psum | solution.py:51
  295.6 1.3 copy-start.2
  296.8 101.9 %all-gather.8.cloned.1.call-start = ((), (), s32[]{:S(2)}) async-start(), calls=%async_computation.4 | async-start | bytes 2621440 | tf_op jit(solution)/shard_map/all_gather | solution.py:56
Sparse Core Ops, SparseCore 0:
  10.2 48.9 all-gather.3
  62.6 34.9 all-gather.5
  222.6 71.6 reduce-scatter.1
  298.1 53.5 all-reduce.1
  353.1 45.6 all-gather.7
where the time goes:
time: 410 us; the launch traced here: 409 us
  waiting for transfers between devices  253 us (62%)
  other arithmetic  54.7 us (13%)
  matrix products  46.8 us (11%)
  local copies, waits for them, and re-layouts  39.9 us (10%)
  between operations  14.6 us (4%)
    reduce_scatter x1, waiting for transfers between devices, shards(): summed = lax.psum_scatter(spread, 'row', scatter_dimension=0, tiled=True)  71.8 us
    psum x1, waiting for transfers between devices, shards(): weight_grad = lax.psum(w_term, 'row') * float(nodes_loc * n_row) ** (-0.5)  52.2 us
    scatter-add x1, other arithmetic, shards(): jax.ops.segment_sum(back_terms, col_ids, num_segments=n_row * row_tiles)  51.1 us
    all_gather x1, waiting for transfers between devices, shards(): all_feats = lax.all_gather(features, 'col', axis=0, tiled=True)  49.7 us
    all_gather x1, waiting for transfers between devices, shards(): lax.all_gather(p_grad, 'col', axis=1, tiled=True)  45.3 us
    all_gather x1, waiting for transfers between devices, shards(): sources_table = lax.all_gather(projected, 'row', axis=1, tiled=True)  33 us
    dot_general x1, matrix products, shards(): jnp.einsum('ti,thn->hin', placing, products, precision=lax.Precision.HIGH...  14.1 us
    dot_general x1, matrix products, shards(): jnp.einsum('htn,tnm->thm', picked_z, tile_values, preferred_element_type=...  14 us
  transfers between devices with their start and end apart: 5, of which 5 were waited for; matrix products, arithmetic and copies ran while one was open for 1% of the time, Pallas kernels for 0%

commit v1 on v0

v1 whole, which is shorter than its diff:
```python
import functools

import jax
import jax.numpy as jnp
from jax import lax
from jax.experimental import pallas as pl
from jax.experimental.pallas import tpu as pltpu
from jax.sharding import PartitionSpec as P

TILE = 128
SLOT = 4
UNROLL = 4
BF = jnp.bfloat16
F32 = jnp.float32
VM = pl.BlockSpec(memory_space=pltpu.VMEM)
SM = pl.BlockSpec(memory_space=pltpu.SMEM)


def call(kernel, outs, scratch, smem, vmem, flops=0, nbytes=0, limit=32):
    return pl.pallas_call(
        kernel,
        out_shape=outs,
        in_specs=[SM] * len(smem) + [VM] * len(vmem),
        out_specs=jax.tree.map(lambda _: VM, outs),
        scratch_shapes=scratch,
        compiler_params=pltpu.CompilerParams(vmem_limit_bytes=limit << 20),
        cost_estimate=pl.CostEstimate(flops=flops, bytes_accessed=nbytes, transcendentals=0),
    )(*smem, *vmem)


def swap(x, axis, n, k):
    return lax.ppermute(x, axis, [(i, i ^ k) for i in range(n)])


def tile_list(key, valid, groups, source, blank):
    slots = key.shape[0]
    ids = jnp.arange(slots, dtype=jnp.int32)
    gids = jnp.arange(groups, dtype=jnp.int32)
    key = jnp.where(valid, key, -1)
    count = jnp.sum((key[None, :] == gids[:, None]).astype(jnp.int32), axis=1)
    even = (count + 1) & ~1
    start = jnp.sum(jnp.where(gids[None, :] < gids[:, None], even[None, :], 0), axis=1)
    rank = jnp.sum(
        ((key[None, :] == key[:, None]) & (ids[None, :] < ids[:, None])).astype(jnp.int32), axis=1
    )
    first = jnp.sum(jnp.where(key[:, None] == gids[None, :], start[None, :], 0), axis=1)
    place = jnp.where(valid, first + rank, -1)
    word = ids | (source << 10) | (key << 20)
    pad = blank << 10
    length = -(-(slots + groups) // (2 * UNROLL)) * 2 * UNROLL
    places = jnp.arange(length, dtype=jnp.int32)
    hit = places[:, None] == place[None, :]
    words = jnp.sum(jnp.where(hit, word[None, :] - pad, 0), axis=1) + pad
    pairs = jnp.sum(even) // 2
    return words, ((pairs + UNROLL - 1) // UNROLL).reshape(1)


def sparse_loop(list_ref, steps_ref, x_ref, tiles_ref, acc_ref, forward):
    def step(s, carry):
        for u in range(UNROLL):
            w0 = list_ref[(s * UNROLL + u) * 2]
            w1 = list_ref[(s * UNROLL + u) * 2 + 1]
            x = jnp.concatenate([x_ref[(w0 >> 10) & 1023], x_ref[(w1 >> 10) & 1023]], axis=1)
            t0, t1 = tiles_ref[w0 & 1023], tiles_ref[w1 & 1023]
            if forward:
                part = lax.dot_general(
                    x,
                    jnp.concatenate([t0, t1], axis=1),
                    (((1,), (1,)), ((), ())),
                    preferred_element_type=F32,
                )
            else:
                part = jnp.dot(x, jnp.concatenate([t0, t1], axis=0), preferred_element_type=F32)
            acc_ref[w0 >> 20] += part
        return carry

    lax.fori_loop(0, steps_ref[0], step, 0)


def send_kernel(peers, want_ref, me_ref, feat_ref, *out_refs):
    for d, out in enumerate(out_refs):
        peer = me_ref[0] ^ (d + 1)
        for j in range(SLOT):
            col = pl.multiple_of(want_ref[peer * SLOT + j] * TILE, TILE)
            out[j] = feat_ref[:, pl.ds(col, TILE)]


def fill_from_wide(x_ref, wide_ref, count):
    for k in range(count):
        x_ref[k] = wide_ref[:, k * TILE : (k + 1) * TILE]
    x_ref[count] = jnp.zeros_like(x_ref[count])


def local_kernel(forward, list_ref, steps_ref, wide_ref, tiles_ref, acc_ref, x_ref):
    fill_from_wide(x_ref, wide_ref, x_ref.shape[0] - 1)
    acc_ref[...] = jnp.zeros_like(acc_ref)
    sparse_loop(list_ref, steps_ref, x_ref, tiles_ref, acc_ref, forward)


def remote_fwd_kernel(n_in, list_ref, steps_ref, me_ref, *refs):
    ins, (tiles_ref, base_ref), rest = refs[:n_in], refs[n_in : n_in + 2], refs[n_in + 2 :]
    outs, (x_ref, acc_ref) = rest[:-2], rest[-2:]
    for d, r in enumerate(ins):
        x_ref[d * SLOT : (d + 1) * SLOT] = r[...]
    x_ref[n_in * SLOT] = jnp.zeros_like(x_ref[0])
    acc_ref[...] = base_ref[...]
    sparse_loop(list_ref, steps_ref, x_ref, tiles_ref, acc_ref, True)
    per = acc_ref.shape[0] // len(outs)
    for k, out in enumerate(outs):
        block = me_ref[0] ^ k
        for i in range(per):
            out[:, i * TILE : (i + 1) * TILE] = acc_ref[block * per + i].astype(BF)


def dense_kernel(n_col, me_ref, wt_ref, w_ref, *refs):
    s_refs, g_refs = refs[:n_col], refs[n_col : 2 * n_col]
    o_refs, y_refs = refs[2 * n_col : 3 * n_col], refs[3 * n_col : 4 * n_col]
    z_ref, s_ref = refs[4 * n_col], refs[4 * n_col + 1]
    f_loc = s_refs[0].shape[0]
    me = me_ref[0]
    for k in range(n_col):
        s_ref[pl.ds(pl.multiple_of((me ^ k) * f_loc, f_loc), f_loc), :] = s_refs[k][...]
    s_all = s_ref[...]
    for k in range(n_col):
        rows = pl.ds(pl.multiple_of((me ^ k) * f_loc, f_loc), f_loc)
        pre = jnp.dot(wt_ref[rows, :], s_all, preferred_element_type=F32)
        sig = 1.0 / (1.0 + jnp.exp(-pre))
        o_refs[k][...] = (pre * sig).astype(BF)
        slope = sig * (1.0 + pre * (1.0 - sig))
        z_ref[rows, :] = (g_refs[k][...].astype(F32) * slope).astype(BF)
    z_all = z_ref[...]
    for k in range(n_col):
        rows = pl.ds(pl.multiple_of((me ^ k) * f_loc, f_loc), f_loc)
        y_refs[k][...] = jnp.dot(w_ref[rows, :], z_all, preferred_element_type=F32).astype(BF)


def weight_kernel(me_ref, s_ref, z_ref, own_ref, *outs):
    per = own_ref.shape[0]
    z = z_ref[...]
    for d in range(len(outs) + 1):
        rows = pl.ds(pl.multiple_of((me_ref[0] ^ d) * per, per), per)
        part = lax.dot_general(
            s_ref[rows, :], z, (((1,), (1,)), ((), ())), preferred_element_type=F32
        )
        if d == 0:
            own_ref[...] = part
        else:
            outs[d - 1][...] = part.astype(BF)


def gather_blocks(wide_ref, me, refs):
    width = refs[0].shape[1]
    for k, r in enumerate(refs):
        wide_ref[:, pl.ds(pl.multiple_of((me ^ k) * width, width), width)] = r[...]


def remote_bwd_kernel(n_col, list_ref, steps_ref, me_ref, *refs):
    ins, tiles_ref, rest = refs[:n_col], refs[n_col], refs[n_col + 1 :]
    wide_ref, (x_ref, acc_ref) = rest[0], rest[-2:]
    outs = rest[1:-2]
    gather_blocks(wide_ref, me_ref[0], ins)
    fill_from_wide(x_ref, wide_ref, x_ref.shape[0] - 1)
    acc_ref[...] = jnp.zeros_like(acc_ref)
    sparse_loop(list_ref, steps_ref, x_ref, tiles_ref, acc_ref, False)
    for d, out in enumerate(outs):
        out[...] = acc_ref[d * SLOT : (d + 1) * SLOT].astype(BF)


def join_kernel(want_ref, me_ref, base_ref, *refs):
    ins, out_ref, acc_ref = refs[:-2], refs[-2], refs[-1]
    acc_ref[...] = base_ref[...]
    for d, r in enumerate(ins):
        peer = me_ref[0] ^ (d + 1)
        for j in range(SLOT):
            acc_ref[want_ref[peer * SLOT + j]] += r[j].astype(F32)
    for k in range(acc_ref.shape[0]):
        out_ref[:, k * TILE : (k + 1) * TILE] = acc_ref[k].astype(BF)


def place_kernel(me_ref, *refs):
    gather_blocks(refs[-1], me_ref[0], refs[:-1])


def shards(features, weight, tile_cols, tile_rows, tile_count, tile_values, out_grad):
    n_row, n_col = lax.axis_size("row"), lax.axis_size("col")
    me_r, me_c = lax.axis_index("row").astype(jnp.int32), lax.axis_index("col").astype(jnp.int32)
    mer, mec = me_r.reshape(1), me_c.reshape(1)
    f_loc, nodes = features.shape
    h_loc = out_grad.shape[0]
    n_f, n_h = weight.shape
    row_tiles = nodes // TILE
    part = nodes // n_col
    slots = tile_cols.shape[1]
    cols, rows = tile_cols[0], tile_rows[0]
    valid = jnp.arange(slots, dtype=jnp.int32) < tile_count[0]

    blocks = jnp.arange(n_row * row_tiles, dtype=jnp.int32)
    seen = jnp.any((cols[None, :] == blocks[:, None]) & valid[None, :], axis=1)
    seen = seen.reshape(n_row, row_tiles)
    inner = jnp.arange(row_tiles, dtype=jnp.int32)
    below = inner[None, :] < inner[:, None]
    rank = jnp.sum((seen[:, None, :] & below[None]).astype(jnp.int32), axis=2)
    slot_ids = jnp.arange(SLOT, dtype=jnp.int32)
    chosen = seen[:, None, :] & (rank[:, None, :] == slot_ids[None, :, None])
    need = jnp.sum(jnp.where(chosen, inner[None, None, :], 0), axis=2)
    want = lax.all_to_all(need, "row", 0, 0, tiled=True).reshape(n_row * SLOT)

    owner, inside = cols // row_tiles, cols % row_tiles
    slot_of = jnp.sum(
        jnp.where(cols[:, None] == blocks[None, :], rank.reshape(-1)[None, :], 0), axis=1
    )
    away = ((owner ^ me_r) - 1) * SLOT + slot_of
    mine, far = valid & (owner == me_r), valid & (owner != me_r)
    n_away = (n_row - 1) * SLOT
    list_fl, steps_fl = tile_list(rows, mine, row_tiles, inside, row_tiles)
    list_fr, steps_fr = tile_list(rows, far, row_tiles, away, n_away)
    list_br, steps_br = tile_list(away, far, n_away, rows, row_tiles)
    list_bl, steps_bl = tile_list(inside, mine, row_tiles, rows, row_tiles)

    block = (SLOT, f_loc, TILE)
    sds = jax.ShapeDtypeStruct
    tile_flops = 2 * f_loc * TILE * TILE
    tile_bytes = slots * TILE * TILE * 2

    sends = call(
        functools.partial(send_kernel, n_row - 1),
        [sds(block, BF)] * (n_row - 1),
        [],
        (want, mer),
        (features,),
        nbytes=2 * n_away * f_loc * TILE * 2,
    )
    got = [swap(x, "row", n_row, d + 1) for d, x in enumerate(sends)]

    def split_cols(x):
        return [lax.dynamic_slice_in_dim(x, (me_c ^ k) * part, part, 1) for k in range(n_col)]

    grads = [g if k == 0 else swap(g, "col", n_col, k) for k, g in enumerate(split_cols(out_grad))]

    acc = call(
        functools.partial(local_kernel, True),
        sds((row_tiles, f_loc, TILE), F32),
        [pltpu.VMEM((row_tiles + 1, f_loc, TILE), BF)],
        (list_fl, steps_fl),
        (features, tile_values),
        flops=tile_flops * slots,
        nbytes=tile_bytes,
    )
    s_parts = call(
        functools.partial(remote_fwd_kernel, n_row - 1),
        [sds((f_loc, part), BF)] * n_col,
        [pltpu.VMEM((n_away + 1, f_loc, TILE), BF), pltpu.VMEM((row_tiles, f_loc, TILE), F32)],
        (list_fr, steps_fr, mec),
        (*got, tile_values, acc),
        flops=tile_flops * slots,
        nbytes=tile_bytes,
    )
    s_got = [s if k == 0 else swap(s, "col", n_col, k) for k, s in enumerate(s_parts)]

    res = call(
        functools.partial(dense_kernel, n_col),
        [sds((h_loc, part), BF)] * n_col
        + [sds((f_loc, part), BF)] * n_col
        + [sds((n_h, part), BF), sds((n_f, part), BF)],
        [],
        (mec,),
        (weight.T, weight, *s_got, *grads),
        flops=4 * n_f * n_h * part,
        nbytes=n_f * part * 8,
    )
    o_parts, y_parts, z_all, s_all = res[:n_col], res[n_col : 2 * n_col], res[-2], res[-1]
    y_got = [y if k == 0 else swap(y, "col", n_col, k) for k, y in enumerate(y_parts)]

    w_rows = n_f // n_row
    w_parts = call(
        weight_kernel,
        [sds((w_rows, n_h), F32)] + [sds((w_rows, n_h), BF)] * (n_row - 1),
        [],
        (mer,),
        (s_all, z_all),
        flops=2 * n_f * n_h * part,
        nbytes=n_f * part * 8,
    )
    w_sum = w_parts[0]
    for d in range(1, n_row):
        w_sum = w_sum + swap(w_parts[d], "row", n_row, d).astype(F32)

    back = call(
        functools.partial(remote_bwd_kernel, n_col),
        [sds((f_loc, nodes), BF)] + [sds(block, BF)] * (n_row - 1),
        [pltpu.VMEM((row_tiles + 1, f_loc, TILE), BF), pltpu.VMEM((n_away, f_loc, TILE), F32)],
        (list_br, steps_br, mec),
        (*y_got, tile_values),
        flops=tile_flops * slots,
        nbytes=tile_bytes,
    )
    y_wide, contribs = back[0], back[1:]
    returned = [swap(x, "row", n_row, d + 1) for d, x in enumerate(contribs)]

    o_got = [o if k == 0 else swap(o, "col", n_col, k) for k, o in enumerate(o_parts)]
    w_cols = [
        lax.dynamic_slice_in_dim(w_sum, (me_c ^ k) * h_loc, h_loc, 1) for k in range(n_col)
    ]
    w_mine = w_cols[0]
    for k in range(1, n_col):
        w_mine = w_mine + swap(w_cols[k], "col", n_col, k)
    w_mine = w_mine * float(nodes * n_row) ** (-0.5)
    weight_grad = lax.all_gather(w_mine, "row", axis=0, tiled=True)

    acc_b = call(
        functools.partial(local_kernel, False),
        sds((row_tiles, f_loc, TILE), F32),
        [pltpu.VMEM((row_tiles + 1, f_loc, TILE), BF)],
        (list_bl, steps_bl),
        (y_wide, tile_values),
        flops=tile_flops * slots,
        nbytes=tile_bytes,
    )
    input_grad = call(
        join_kernel,
        sds((f_loc, nodes), BF),
        [pltpu.VMEM((row_tiles, f_loc, TILE), F32)],
        (want, mer),
        (acc_b, *returned),
        nbytes=f_loc * nodes * 8,
    )
    output = call(
        place_kernel, sds((h_loc, nodes), BF), [], (mec,), tuple(o_got), nbytes=h_loc * nodes * 4
    )
    return output, input_grad, weight_grad


def solution(mesh):
    return jax.shard_map(
        shards,
        mesh=mesh,
        in_specs=(
            P("col", "row"),
            P(),
            P("row", None),
            P("row", None),
            P("row"),
            P("row", None, None),
            P("col", "row"),
        ),
        out_specs=(P("col", "row"), P("col", "row"), P(None, "col")),
        check_vma=False,
    )
```

time: 410 us -> 145 us (0.35)
  the two profiles are of different devices: /device:TPU:0 before, /device:TPU:13 now
where the time goes in v1:
time: 145 us; the launch traced here: 143 us
  starting transfers between devices  51.7 us (36%)
  local copies, waits for them, and re-layouts  19.8 us (14%)
  Pallas kernels  17.4 us (12%)
  waiting for transfers between devices  16.3 us (11%)
  blocking collectives  13.7 us (9%)
  other arithmetic  12.7 us (9%)
  between operations  11.5 us (8%)
    ppermute x36, starting transfers between devices, swap(): return lax.ppermute(x, axis, [(i, i ^ k) for i in range(n)])  47.2 us
    pallas_call x9, Pallas kernels, call(): pl.pallas_call(kernel, out_shape=outs, in_specs=[SM] * len(smem) + [VM] *...  17.4 us
    unnamed x16, local copies, waits for them, and re-layouts  16.5 us
    ppermute x36, waiting for transfers between devices, swap(): return lax.ppermute(x, axis, [(i, i ^ k) for i in range(n)])  16.3 us
    all_gather x1, blocking collectives, shards(): weight_grad = lax.all_gather(w_mine, 'row', axis=0, tiled=True)  13.7 us
    all_to_all x1, starting transfers between devices, shards(): want = lax.all_to_all(need, 'row', 0, 0, tiled=True).reshape(n_row * SLOT)  4.54 us
  transfers between devices with their start and end apart: 37, of which 5 were waited for; matrix products, arithmetic and copies ran while one was open for 9% of the time, Pallas kernels for 8%

profile of v1, /device:TPU:13, one launch (start us, length us, event | category | flops | bytes accessed | tf_op | source)
XLA Modules:
  0.0 143.1 jit_solution(8375610285104598765)
XLA Ops:
  3.3 4.5 %all-to-all-start = ((s32[8,1,4]{2,1,0:T(1,128)}), s32[8,1,4]{2,1,0:T(1,128)S(1)}, u32[]{:S(2)}, u32[]{:S(2)}) async-start(s32[8,1,4]{2,1,0:T(1,128)} %copy.17), calls=%async_computation | async-start | bytes 8192 | tf_op jit(solution)/shard_map/all_to_all | solution.py:206
  23.7 1.8 %constant_dynamic-slice_fusion.1 = (bf16[128,512]{1,0:T(8,128)(2,1)}, bf16[128,512]{1,0:T(8,128)(2,1)}, bf16[128,512]{1,0:T(8,128)(2,1)S(1)}, bf16[128,512]{1,0:T(8,128)(2,1)}) fusion(bf16[128,2048]{1,0:T(8,128)(2,1)} %param.13, s32[]{:T(128)S(6)} %select_n.232, s32[]{:T(128)S(6)} %select_n.230, s32[]{:T(128)S(6)} %select_n.229, s32[]{:T(128)S(6)} %select_n.231), kind=kLoop, calls=%fused_computation.58 | loop fusion | bytes 1048592 | tf_op jit(solution)/shard_map/dynamic_slice | solution.py:236
  32.8 3.4 %copy-done = bf16[256,128,128]{2,1,0:T(8,128)(2,1)S(1)} copy-done((bf16[256,128,128]{2,1,0:T(8,128)(2,1)S(1)}, bf16[256,128,128]{2,1,0:T(8,128)(2,1)}, u32[]{:S(2)}) %copy-start) | copy-done | bytes 8388632
  37.3 3.1 %shard_map.95.refs_8_ = f32[16,128,128]{2,1,0:T(8,128)S(1)} custom-call(s32[272]{0:T(512)S(1)} %broadcast_add_fusion.2.list_ref, s32[1]{0:T(128)} %bitcast.17.steps_ref, bf16[128,2048]{1,0:T(8,128)(2,1)S(1)} %copy-done.5, bf16[256,128,128]{2,1,0:T(8,128)(2,1)S(1)} %copy-done), custom_call_target="tpu_custom_call" | custom-call | flops 1073741824 | bytes 8388608 | tf_op jit(solution)/shard_map/pallas_call | solution.py:20
  42.9 2.4 %collective-permute-start.11 = (bf16[128,512]{1,0:T(8,128)(2,1)}, bf16[128,512]{1,0:T(8,128)(2,1)S(1)}, u32[]{:S(2)}, u32[]{:S(2)}) collective-permute-start(bf16[128,512]{1,0:T(8,128)(2,1)} %get-tuple-element.97), channel_id=1, source_target_pairs={{0,2},{1,3},{2,0},{3,1},{4,6},{5,7},{6,4},{7,5},{8,10},{9,11},{10,... | collective-permute-start | bytes 393224 | tf_op jit(solution)/shard_map/ppermute | solution.py:32
  45.5 3.4 %copy-done.1 = bf16[256,128,128]{2,1,0:T(8,128)(2,1)S(1)} copy-done((bf16[256,128,128]{2,1,0:T(8,128)(2,1)S(1)}, bf16[256,128,128]{2,1,0:T(8,128)(2,1)}, u32[]{:S(2)}) %copy-start.1) | copy-done | bytes 8388632
  48.9 2.4 %shard_map.96 = (bf16[128,512]{1,0:T(8,128)(2,1)S(1)}, bf16[128,512]{1,0:T(8,128)(2,1)S(1)}, bf16[128,512]{1,0:T(8,128)(2,1)S(1)}, bf16[128,512]{1,0:T(8,128)(2,1)S(1)}) custom-call(s32[272]{0:T(512)S(1)} %broadcast_add_fusion.3.list_ref, s32[1]{0:T(128)} %bitcast.10.steps_ref, s32[1]{0:T(128)} %bitcast.me_ref, ...), custom_call_target="tpu_custom_call" | custom-call | flops 1073741824 | bytes 8388608 | tf_op jit(solution)/shard_map/pallas_call | solution.py:20
  52.5 2.1 %collective-permute-start.8 = (bf16[128,512]{1,0:T(8,128)(2,1)S(1)}, bf16[128,512]{1,0:T(8,128)(2,1)S(1)}, u32[]{:S(2)}, u32[]{:S(2)}) collective-permute-start(bf16[128,512]{1,0:T(8,128)(2,1)S(1)} %get-tuple-element.49), channel_id=1, source_target_pairs={{0,2},{1,3},{2,0},{3,1},{4,6},{5,7},{6,4},{7,5},{8,10},{9,11},{10,... | collective-permute-start | bytes 393224 | tf_op jit(solution)/shard_map/ppermute | solution.py:32
  54.9 8.0 %collective-permute-done.12.refs_7_ = bf16[128,512]{1,0:T(8,128)(2,1)S(1)} collective-permute-done((bf16[128,512]{1,0:T(8,128)(2,1)}, bf16[128,512]{1,0:T(8,128)(2,1)S(1)}, u32[]{:S(2)}, u32[]{:S(2)}) %collective-permute-start.12) | collective-permute-done | bytes 131104 | tf_op jit(solution)/shard_map/ppermute | solution.py:32
  62.9 2.7 %collective-permute-done.8.refs_2_ = bf16[128,512]{1,0:T(8,128)(2,1)S(1)} collective-permute-done((bf16[128,512]{1,0:T(8,128)(2,1)S(1)}, bf16[128,512]{1,0:T(8,128)(2,1)S(1)}, u32[]{:S(2)}, u32[]{:S(2)}) %collective-permute-start.8) | collective-permute-done | bytes 131104 | tf_op jit(solution)/shard_map/ppermute | solution.py:32
  65.6 3.2 %collective-permute-done.9.refs_3_ = bf16[128,512]{1,0:T(8,128)(2,1)S(1)} collective-permute-done((bf16[128,512]{1,0:T(8,128)(2,1)S(1)}, bf16[128,512]{1,0:T(8,128)(2,1)S(1)}, u32[]{:S(2)}, u32[]{:S(2)}) %collective-permute-start.9) | collective-permute-done | bytes 131104 | tf_op jit(solution)/shard_map/ppermute | solution.py:32
  74.5 1.8 %collective-permute-start.30 = (bf16[64,512]{1,0:T(8,128)(2,1)S(1)}, bf16[64,512]{1,0:T(8,128)(2,1)S(1)}, u32[]{:S(2)}, u32[]{:S(2)}) collective-permute-start(bf16[64,512]{1,0:T(8,128)(2,1)S(1)} %get-tuple-element.74), channel_id=1, source_target_pairs={{0,20},{4,16},{8,28},{12,24},{16,4},{20,0},{24,12},{28,8},{1,21},{... | collective-permute-start | bytes 196616 | tf_op jit(solution)/shard_map/ppermute | solution.py:32
  84.0 2.3 %collective-permute-start.17 = (bf16[128,512]{1,0:T(8,128)(2,1)S(1)}, bf16[128,512]{1,0:T(8,128)(2,1)S(1)}, u32[]{:S(2)}, u32[]{:S(2)}) collective-permute-start(bf16[128,512]{1,0:T(8,128)(2,1)S(1)} %get-tuple-element.57), channel_id=1, source_target_pairs={{0,2},{1,3},{2,0},{3,1},{4,6},{5,7},{6,4},{7,5},{8,10},{9,11},{10,... | collective-permute-start | bytes 393224 | tf_op jit(solution)/shard_map/ppermute | solution.py:32
  89.1 2.1 %collective-permute-start.33 = (f32[64,128]{1,0:T(8,128)S(1)}, f32[64,128]{1,0:T(8,128)S(1)}, u32[]{:S(2)}, u32[]{:S(2)}) collective-permute-start(f32[64,128]{1,0:T(8,128)S(1)} %get-tuple-element.98), channel_id=1, source_target_pairs={{0,1},{1,0},{2,3},{3,2},{4,5},{5,4},{6,7},{7,6},{8,9},{9,8},{10,11... | collective-permute-start | bytes 98312 | tf_op jit(solution)/shard_map/ppermute | solution.py:32
  92.8 4.8 %collective-permute-start.34 = (f32[64,128]{1,0:T(8,128)S(1)}, f32[64,128]{1,0:T(8,128)S(1)}, u32[]{:S(2)}, u32[]{:S(2)}) collective-permute-start(f32[64,128]{1,0:T(8,128)S(1)} %get-tuple-element.100), channel_id=1, source_target_pairs={{0,2},{1,3},{2,0},{3,1},{4,6},{5,7},{6,4},{7,5},{8,10},{9,11},{10,... | collective-permute-start | bytes 98312 | tf_op jit(solution)/shard_map/ppermute | solution.py:32
  98.3 4.4 %collective-permute-start.35 = (f32[64,128]{1,0:T(8,128)S(1)}, f32[64,128]{1,0:T(8,128)S(1)}, u32[]{:S(2)}, u32[]{:S(2)}) collective-permute-start(f32[64,128]{1,0:T(8,128)S(1)} %get-tuple-element.99), channel_id=1, source_target_pairs={{0,3},{1,2},{2,1},{3,0},{4,7},{5,6},{6,5},{7,4},{8,11},{9,10},{10,... | collective-permute-start | bytes 98312 | tf_op jit(solution)/shard_map/ppermute | solution.py:32
  102.7 3.4 %copy-done.2 = bf16[256,128,128]{2,1,0:T(8,128)(2,1)S(1)} copy-done((bf16[256,128,128]{2,1,0:T(8,128)(2,1)S(1)}, bf16[256,128,128]{2,1,0:T(8,128)(2,1)}, u32[]{:S(2)}) %copy-start.2) | copy-done | bytes 8388632
  106.1 2.5 %shard_map.99 = (bf16[128,2048]{1,0:T(8,128)(2,1)S(1)}, bf16[4,128,128]{2,1,0:T(8,128)(2,1)S(1)}, bf16[4,128,128]{2,1,0:T(8,128)(2,1)S(1)}, bf16[4,128,128]{2,1,...) custom-call(s32[288]{0:T(512)S(1)} %broadcast_add_fusion.list_ref, ...), custom_call_target="tpu_custom_call" | custom-call | flops 1073741824 | bytes 8388608 | tf_op jit(solution)/shard_map/pallas_call | solution.py:20
  108.7 3.8 %collective-permute-start.19 = (bf16[4,128,128]{2,1,0:T(8,128)(2,1)S(1)}, bf16[4,128,128]{2,1,0:T(8,128)(2,1)S(1)}, u32[]{:S(2)}, u32[]{:S(2)}) collective-permute-start(bf16[4,128,128]{2,1,0:T(8,128)(2,1)S(1)} %get-tuple-element.60), channel_id=1, source_target_pairs={{0,4},{4,0},{8,12},{12,8},{16,20},{20,16},{24,28},{28,24},{1,5},{5... | collective-permute-start | bytes 393224 | tf_op jit(solution)/shard_map/ppermute | solution.py:32
  114.3 2.1 %collective-permute-start.23 = (bf16[4,128,128]{2,1,0:T(8,128)(2,1)S(1)}, bf16[4,128,128]{2,1,0:T(8,128)(2,1)S(1)}, u32[]{:S(2)}, u32[]{:S(2)}) collective-permute-start(bf16[4,128,128]{2,1,0:T(8,128)(2,1)S(1)} %get-tuple-element.64), channel_id=1, source_target_pairs={{0,20},{4,16},{8,28},{12,24},{16,4},{20,0},{24,12},{28,8},{1,21},{... | collective-permute-start | bytes 393224 | tf_op jit(solution)/shard_map/ppermute | solution.py:32
  116.5 2.5 %collective-permute-start.24 = (bf16[4,128,128]{2,1,0:T(8,128)(2,1)S(1)}, bf16[4,128,128]{2,1,0:T(8,128)(2,1)S(1)}, u32[]{:S(2)}, u32[]{:S(2)}) collective-permute-start(bf16[4,128,128]{2,1,0:T(8,128)(2,1)S(1)} %get-tuple-element.65), channel_id=1, source_target_pairs={{0,24},{4,28},{8,16},{12,20},{16,8},{20,12},{24,0},{28,4},{1,25},{... | collective-permute-start | bytes 393224 | tf_op jit(solution)/shard_map/ppermute | solution.py:32
  119.9 13.7 %all_gather.3 = f32[512,128]{1,0:T(8,128)S(1)} all-gather(f32[64,128]{1,0:T(8,128)S(1)} %add_multiply_fusion), channel_id=1, replica_groups=mesh['row'=8,'col'=4] {'row'}, dimensions={0}, use_global_device_ids=true | all-gather | bytes 294912 | tf_op jit(solution)/shard_map/all_gather | solution.py:308
  134.4 3.4 %copy-done.3 = bf16[256,128,128]{2,1,0:T(8,128)(2,1)S(1)} copy-done((bf16[256,128,128]{2,1,0:T(8,128)(2,1)S(1)}, bf16[256,128,128]{2,1,0:T(8,128)(2,1)}, u32[]{:S(2)}) %copy-start.3) | copy-done | bytes 8388632
  137.8 2.8 %shard_map.100.base_ref = f32[16,128,128]{2,1,0:T(8,128)S(1)} custom-call(s32[272]{0:T(512)S(1)} %broadcast_add_fusion.1.list_ref, s32[1]{0:T(128)} %bitcast.22.steps_ref, bf16[128,2048]{1,0:T(8,128)(2,1)S(1)} %get-tuple-element.59.wide_ref, bf16[256,128,128]{2,1,0:T(8,128)(2,1)S(1)} %copy-done.3), custom_call_target="tpu_custom_call" | custom-call | flops 1073741824 | bytes 8388608 | tf_op jit(solution)/shard_map/pallas_call | solution.py:20
  (130 shorter events, 44.9 us)
Async XLA Ops:
  3.3 14.5 %all-to-all-start = ((s32[8,1,4]{2,1,0:T(1,128)}), s32[8,1,4]{2,1,0:T(1,128)S(1)}, u32[]{:S(2)}, u32[]{:S(2)}) async-start(s32[8,1,4]{2,1,0:T(1,128)} %copy.17), calls=%async_computation | async-start | bytes 8192 | tf_op jit(solution)/shard_map/all_to_all | solution.py:206
  25.5 17.4 %collective-permute-start.3 = (bf16[4,128,128]{2,1,0:T(8,128)(2,1)}, bf16[4,128,128]{2,1,0:T(8,128)(2,1)S(1)}, u32[]{:S(2)}, u32[]{:S(2)}) collective-permute-start(bf16[4,128,128]{2,1,0:T(8,128)(2,1)} %get-tuple-element.43), channel_id=1, source_target_pairs={{0,16},{4,20},{8,24},{12,28},{16,0},{20,4},{24,8},{28,12},{1,17},{... | collective-permute-start | bytes 393224 | tf_op jit(solution)/shard_map/ppermute | solution.py:32
  25.6 19.7 %collective-permute-start.4 = (bf16[4,128,128]{2,1,0:T(8,128)(2,1)}, bf16[4,128,128]{2,1,0:T(8,128)(2,1)S(1)}, u32[]{:S(2)}, u32[]{:S(2)}) collective-permute-start(bf16[4,128,128]{2,1,0:T(8,128)(2,1)} %get-tuple-element.44), channel_id=1, source_target_pairs={{0,20},{4,16},{8,28},{12,24},{16,4},{20,0},{24,12},{28,8},{1,21},{... | collective-permute-start | bytes 393224 | tf_op jit(solution)/shard_map/ppermute | solution.py:32
  27.2 18.3 %collective-permute-start.5 = (bf16[4,128,128]{2,1,0:T(8,128)(2,1)S(1)}, bf16[4,128,128]{2,1,0:T(8,128)(2,1)S(1)}, u32[]{:S(2)}, u32[]{:S(2)}) collective-permute-start(bf16[4,128,128]{2,1,0:T(8,128)(2,1)S(1)} %get-tuple-element.45), channel_id=1, source_target_pairs={{0,24},{4,28},{8,16},{12,20},{16,8},{20,12},{24,0},{28,4},{1,25},{... | collective-permute-start | bytes 393224 | tf_op jit(solution)/shard_map/ppermute | solution.py:32
  28.4 17.1 %collective-permute-start.6 = (bf16[4,128,128]{2,1,0:T(8,128)(2,1)S(1)}, bf16[4,128,128]{2,1,0:T(8,128)(2,1)S(1)}, u32[]{:S(2)}, u32[]{:S(2)}) collective-permute-start(bf16[4,128,128]{2,1,0:T(8,128)(2,1)S(1)} %get-tuple-element.46), channel_id=1, source_target_pairs={{0,28},{4,24},{8,20},{12,16},{16,12},{20,8},{24,4},{28,0},{1,29},{... | collective-permute-start | bytes 393224 | tf_op jit(solution)/shard_map/ppermute | solution.py:32
  32.6 22.0 %collective-permute-start.10 = (bf16[128,512]{1,0:T(8,128)(2,1)}, bf16[128,512]{1,0:T(8,128)(2,1)S(1)}, u32[]{:S(2)}, u32[]{:S(2)}) collective-permute-start(bf16[128,512]{1,0:T(8,128)(2,1)} %get-tuple-element.95), channel_id=1, source_target_pairs={{0,1},{1,0},{2,3},{3,2},{4,5},{5,4},{6,7},{7,6},{8,9},{9,8},{10,11... | collective-permute-start | bytes 393224 | tf_op jit(solution)/shard_map/ppermute | solution.py:32
  42.9 11.9 %collective-permute-start.11 = (bf16[128,512]{1,0:T(8,128)(2,1)}, bf16[128,512]{1,0:T(8,128)(2,1)S(1)}, u32[]{:S(2)}, u32[]{:S(2)}) collective-permute-start(bf16[128,512]{1,0:T(8,128)(2,1)} %get-tuple-element.97), channel_id=1, source_target_pairs={{0,2},{1,3},{2,0},{3,1},{4,6},{5,7},{6,4},{7,5},{8,10},{9,11},{10,... | collective-permute-start | bytes 393224 | tf_op jit(solution)/shard_map/ppermute | solution.py:32
  45.3 17.6 %collective-permute-start.12 = (bf16[128,512]{1,0:T(8,128)(2,1)}, bf16[128,512]{1,0:T(8,128)(2,1)S(1)}, u32[]{:S(2)}, u32[]{:S(2)}) collective-permute-start(bf16[128,512]{1,0:T(8,128)(2,1)} %get-tuple-element.94), channel_id=1, source_target_pairs={{0,3},{1,2},{2,1},{3,0},{4,7},{5,6},{6,5},{7,4},{8,11},{9,10},{10,... | collective-permute-start | bytes 393224 | tf_op jit(solution)/shard_map/ppermute | solution.py:32
  51.3 11.6 %collective-permute-start.7 = (bf16[128,512]{1,0:T(8,128)(2,1)S(1)}, bf16[128,512]{1,0:T(8,128)(2,1)S(1)}, u32[]{:S(2)}, u32[]{:S(2)}) collective-permute-start(bf16[128,512]{1,0:T(8,128)(2,1)S(1)} %get-tuple-element.48), channel_id=1, source_target_pairs={{0,1},{1,0},{2,3},{3,2},{4,5},{5,4},{6,7},{7,6},{8,9},{9,8},{10,11... | collective-permute-start | bytes 393224 | tf_op jit(solution)/shard_map/ppermute | solution.py:32
  52.5 13.1 %collective-permute-start.8 = (bf16[128,512]{1,0:T(8,128)(2,1)S(1)}, bf16[128,512]{1,0:T(8,128)(2,1)S(1)}, u32[]{:S(2)}, u32[]{:S(2)}) collective-permute-start(bf16[128,512]{1,0:T(8,128)(2,1)S(1)} %get-tuple-element.49), channel_id=1, source_target_pairs={{0,2},{1,3},{2,0},{3,1},{4,6},{5,7},{6,4},{7,5},{8,10},{9,11},{10,... | collective-permute-start | bytes 393224 | tf_op jit(solution)/shard_map/ppermute | solution.py:32
  54.6 14.2 %collective-permute-start.9 = (bf16[128,512]{1,0:T(8,128)(2,1)S(1)}, bf16[128,512]{1,0:T(8,128)(2,1)S(1)}, u32[]{:S(2)}, u32[]{:S(2)}) collective-permute-start(bf16[128,512]{1,0:T(8,128)(2,1)S(1)} %get-tuple-element.50), channel_id=1, source_target_pairs={{0,3},{1,2},{2,1},{3,0},{4,7},{5,6},{6,5},{7,4},{8,11},{9,10},{10,... | collective-permute-start | bytes 393224 | tf_op jit(solution)/shard_map/ppermute | solution.py:32
  73.1 10.9 %collective-permute-start.28 = (bf16[64,512]{1,0:T(8,128)(2,1)S(1)}, bf16[64,512]{1,0:T(8,128)(2,1)S(1)}, u32[]{:S(2)}, u32[]{:S(2)}) collective-permute-start(bf16[64,512]{1,0:T(8,128)(2,1)S(1)} %get-tuple-element.72), channel_id=1, source_target_pairs={{0,12},{4,8},{8,4},{12,0},{16,28},{20,24},{24,20},{28,16},{1,13},{... | collective-permute-start | bytes 196616 | tf_op jit(solution)/shard_map/ppermute | solution.py:32
  74.5 11.9 %collective-permute-start.30 = (bf16[64,512]{1,0:T(8,128)(2,1)S(1)}, bf16[64,512]{1,0:T(8,128)(2,1)S(1)}, u32[]{:S(2)}, u32[]{:S(2)}) collective-permute-start(bf16[64,512]{1,0:T(8,128)(2,1)S(1)} %get-tuple-element.74), channel_id=1, source_target_pairs={{0,20},{4,16},{8,28},{12,24},{16,4},{20,0},{24,12},{28,8},{1,21},{... | collective-permute-start | bytes 196616 | tf_op jit(solution)/shard_map/ppermute | solution.py:32
  86.4 11.9 %collective-permute-start.18 = (bf16[128,512]{1,0:T(8,128)(2,1)S(1)}, bf16[128,512]{1,0:T(8,128)(2,1)S(1)}, u32[]{:S(2)}, u32[]{:S(2)}) collective-permute-start(bf16[128,512]{1,0:T(8,128)(2,1)S(1)} %get-tuple-element.58), channel_id=1, source_target_pairs={{0,3},{1,2},{2,1},{3,0},{4,7},{5,6},{6,5},{7,4},{8,11},{9,10},{10,... | collective-permute-start | bytes 393224 | tf_op jit(solution)/shard_map/ppermute | solution.py:32
  86.7 27.3 %collective-permute-start.13 = (bf16[128,512]{1,0:T(8,128)(2,1)S(1)}, bf16[128,512]{1,0:T(8,128)(2,1)S(1)}, u32[]{:S(2)}, u32[]{:S(2)}) collective-permute-start(bf16[128,512]{1,0:T(8,128)(2,1)S(1)} %get-tuple-element.52), channel_id=1, source_target_pairs={{0,1},{1,0},{2,3},{3,2},{4,5},{5,4},{6,7},{7,6},{8,9},{9,8},{10,11... | collective-permute-start | bytes 393224 | tf_op jit(solution)/shard_map/ppermute | solution.py:32
  87.7 26.7 %collective-permute-start.14 = (bf16[128,512]{1,0:T(8,128)(2,1)S(1)}, bf16[128,512]{1,0:T(8,128)(2,1)S(1)}, u32[]{:S(2)}, u32[]{:S(2)}) collective-permute-start(bf16[128,512]{1,0:T(8,128)(2,1)S(1)} %get-tuple-element.53), channel_id=1, source_target_pairs={{0,2},{1,3},{2,0},{3,1},{4,6},{5,7},{6,4},{7,5},{8,10},{9,11},{10,... | collective-permute-start | bytes 393224 | tf_op jit(solution)/shard_map/ppermute | solution.py:32
  89.1 19.4 %collective-permute-start.33 = (f32[64,128]{1,0:T(8,128)S(1)}, f32[64,128]{1,0:T(8,128)S(1)}, u32[]{:S(2)}, u32[]{:S(2)}) collective-permute-start(f32[64,128]{1,0:T(8,128)S(1)} %get-tuple-element.98), channel_id=1, source_target_pairs={{0,1},{1,0},{2,3},{3,2},{4,5},{5,4},{6,7},{7,6},{8,9},{9,8},{10,11... | collective-permute-start | bytes 98312 | tf_op jit(solution)/shard_map/ppermute | solution.py:32
  92.8 15.8 %collective-permute-start.34 = (f32[64,128]{1,0:T(8,128)S(1)}, f32[64,128]{1,0:T(8,128)S(1)}, u32[]{:S(2)}, u32[]{:S(2)}) collective-permute-start(f32[64,128]{1,0:T(8,128)S(1)} %get-tuple-element.100), channel_id=1, source_target_pairs={{0,2},{1,3},{2,0},{3,1},{4,6},{5,7},{6,4},{7,5},{8,10},{9,11},{10,... | collective-permute-start | bytes 98312 | tf_op jit(solution)/shard_map/ppermute | solution.py:32
  98.3 14.1 %collective-permute-start.35 = (f32[64,128]{1,0:T(8,128)S(1)}, f32[64,128]{1,0:T(8,128)S(1)}, u32[]{:S(2)}, u32[]{:S(2)}) collective-permute-start(f32[64,128]{1,0:T(8,128)S(1)} %get-tuple-element.99), channel_id=1, source_target_pairs={{0,3},{1,2},{2,1},{3,0},{4,7},{5,6},{6,5},{7,4},{8,11},{9,10},{10,... | collective-permute-start | bytes 98312 | tf_op jit(solution)/shard_map/ppermute | solution.py:32
  113.9 26.6 %collective-permute-start.21 = (bf16[4,128,128]{2,1,0:T(8,128)(2,1)S(1)}, bf16[4,128,128]{2,1,0:T(8,128)(2,1)S(1)}, u32[]{:S(2)}, u32[]{:S(2)}) collective-permute-start(bf16[4,128,128]{2,1,0:T(8,128)(2,1)S(1)} %get-tuple-element.62), channel_id=1, source_target_pairs={{0,12},{4,8},{8,4},{12,0},{16,28},{20,24},{24,20},{28,16},{1,13},{... | collective-permute-start | bytes 393224 | tf_op jit(solution)/shard_map/ppermute | solution.py:32
  114.3 26.3 %collective-permute-start.22 = (bf16[4,128,128]{2,1,0:T(8,128)(2,1)S(1)}, bf16[4,128,128]{2,1,0:T(8,128)(2,1)S(1)}, u32[]{:S(2)}, u32[]{:S(2)}) collective-permute-start(bf16[4,128,128]{2,1,0:T(8,128)(2,1)S(1)} %get-tuple-element.63), channel_id=1, source_target_pairs={{0,16},{4,20},{8,24},{12,28},{16,0},{20,4},{24,8},{28,12},{1,17},{... | collective-permute-start | bytes 393224 | tf_op jit(solution)/shard_map/ppermute | solution.py:32
  114.3 26.3 %collective-permute-start.23 = (bf16[4,128,128]{2,1,0:T(8,128)(2,1)S(1)}, bf16[4,128,128]{2,1,0:T(8,128)(2,1)S(1)}, u32[]{:S(2)}, u32[]{:S(2)}) collective-permute-start(bf16[4,128,128]{2,1,0:T(8,128)(2,1)S(1)} %get-tuple-element.64), channel_id=1, source_target_pairs={{0,20},{4,16},{8,28},{12,24},{16,4},{20,0},{24,12},{28,8},{1,21},{... | collective-permute-start | bytes 393224 | tf_op jit(solution)/shard_map/ppermute | solution.py:32
  116.5 24.1 %collective-permute-start.24 = (bf16[4,128,128]{2,1,0:T(8,128)(2,1)S(1)}, bf16[4,128,128]{2,1,0:T(8,128)(2,1)S(1)}, u32[]{:S(2)}, u32[]{:S(2)}) collective-permute-start(bf16[4,128,128]{2,1,0:T(8,128)(2,1)S(1)} %get-tuple-element.65), channel_id=1, source_target_pairs={{0,24},{4,28},{8,16},{12,20},{16,8},{20,12},{24,0},{28,4},{1,25},{... | collective-permute-start | bytes 393224 | tf_op jit(solution)/shard_map/ppermute | solution.py:32
  119.0 21.7 %collective-permute-start.25 = (bf16[4,128,128]{2,1,0:T(8,128)(2,1)S(1)}, bf16[4,128,128]{2,1,0:T(8,128)(2,1)S(1)}, u32[]{:S(2)}, u32[]{:S(2)}) collective-permute-start(bf16[4,128,128]{2,1,0:T(8,128)(2,1)S(1)} %get-tuple-element.66), channel_id=1, source_target_pairs={{0,28},{4,24},{8,20},{12,16},{16,12},{20,8},{24,4},{28,0},{1,29},{... | collective-permute-start | bytes 393224 | tf_op jit(solution)/shard_map/ppermute | solution.py:32
  (20 other events, 134.7 us)

commit v2 on v1

v2 whole, which is shorter than its diff:
```python
import functools

import jax
import jax.numpy as jnp
from jax import lax
from jax.experimental import pallas as pl
from jax.experimental.pallas import tpu as pltpu
from jax.sharding import PartitionSpec as P

TILE = 128
SLOT = 4
UNROLL = 4
LOADS = 8
BF = jnp.bfloat16
F32 = jnp.float32
VM = pl.BlockSpec(memory_space=pltpu.VMEM)
SM = pl.BlockSpec(memory_space=pltpu.SMEM)


def call(kernel, outs, scratch, smem, vmem, held=(), flops=0, nbytes=0, limit=24):
    return pl.pallas_call(
        kernel,
        out_shape=outs,
        in_specs=[SM] * len(smem) + [VM] * len(held) + [VM] * len(vmem),
        out_specs=jax.tree.map(lambda _: VM, outs),
        scratch_shapes=scratch,
        compiler_params=pltpu.CompilerParams(vmem_limit_bytes=limit << 20),
        cost_estimate=pl.CostEstimate(flops=flops, bytes_accessed=nbytes, transcendentals=0),
    )(*[pltpu.with_memory_space_constraint(x, pltpu.SMEM) for x in smem], *held, *vmem)


def swap(x, axis, n, k):
    return lax.ppermute(x, axis, [(i, i ^ k) for i in range(n)])


def flip(x, n):
    i = lax.broadcasted_iota(jnp.int32, (n, n), 0)
    j = lax.broadcasted_iota(jnp.int32, (n, n), 1)
    return jnp.sum(jnp.where(i == j, x, 0), axis=1 if x.shape[0] == 1 else 0, keepdims=True)


def iota(n, axis):
    return lax.broadcasted_iota(jnp.int32, (n, 1) if axis == 0 else (1, n), axis)


def ranks(cols, valid, blocks, row_tiles):
    b_col, b_row = iota(blocks, 0), iota(blocks, 1)
    hit = jnp.where((cols == b_col) & valid, 1, 0)
    used_col = jnp.max(hit, axis=1, keepdims=True)
    used_row = flip(used_col, blocks)
    same = (b_col // row_tiles) == (b_row // row_tiles)
    rank_row = jnp.sum(jnp.where(same & (b_col < b_row), used_col, 0), axis=0, keepdims=True)
    rank_col = jnp.sum(jnp.where(same & (b_row < b_col), used_row, 0), axis=1, keepdims=True)
    return used_row, rank_row, rank_col


def need_kernel(n_row, row_tiles, count_ref, cols_ref, need_ref):
    cols = cols_ref[...]
    blocks = n_row * row_tiles
    valid = iota(cols.shape[1], 1) < count_ref[0]
    used, rank, _ = ranks(cols, valid, blocks, row_tiles)
    b = iota(blocks, 1)
    owner = (b // row_tiles) == iota(n_row, 0)
    lane = iota(128, 1)
    total = jnp.zeros((n_row, 128), jnp.int32)
    for j in range(SLOT):
        pick = jnp.where((used > 0) & (rank == j), b % row_tiles, 0)
        total += jnp.where(
            lane == j, jnp.sum(jnp.where(owner, pick, 0), axis=1, keepdims=True), 0
        )
    need_ref[...] = total


def write_list(out_ref, which, key_row, key_col, valid_row, valid_col, groups, source, blank):
    slots, length = key_row.shape[1], out_ref.shape[1]
    t_row, t_col = iota(slots, 1), iota(slots, 0)
    key_row, key_col = jnp.where(valid_row, key_row, -1), jnp.where(valid_col, key_col, -1)
    g_col, g_row = iota(groups, 0), iota(128, 1)
    count = jnp.sum(jnp.where(key_row == g_col, 1, 0), axis=1, keepdims=True)
    even = ((count + 1) >> 1) << 1
    start = jnp.sum(jnp.where(g_col < g_row, even, 0), axis=0, keepdims=True)
    first = jnp.sum(jnp.where(key_col == g_row, start, 0), axis=1, keepdims=True)
    rank = jnp.sum(jnp.where((key_row == key_col) & (t_row < t_col), 1, 0), axis=1, keepdims=True)
    place = jnp.where(valid_col, first + rank, -1)
    word = t_col | (source << 10) | (key_col << 20)
    pad = blank << 10
    words = jnp.sum(jnp.where(place == iota(length, 1), word - pad, 0), axis=0, keepdims=True) + pad
    out_ref[which : which + 1, :] = words
    total = jnp.sum(even, axis=0, keepdims=True)
    steps = (total + (2 * UNROLL - 1)) // (2 * UNROLL)
    out_ref[4 + which : 5 + which, :] = jnp.broadcast_to(steps, (1, length))


def lists_kernel(n_row, row_tiles, count_ref, me_ref, cols_ref, rows_ref, out_ref):
    cols, rows = cols_ref[...], rows_ref[...]
    slots = cols.shape[1]
    blocks = n_row * row_tiles
    me, n_chip = me_ref[0], n_row // 2
    valid = iota(slots, 1) < count_ref[0]
    _, rank_row, rank_col = ranks(cols, valid, blocks, row_tiles)
    cols_c, rows_c = flip(cols, slots), flip(rows, slots)
    valid_c = iota(slots, 0) < count_ref[0]
    slot_c = jnp.sum(jnp.where(cols_c == iota(blocks, 1), rank_row, 0), axis=1, keepdims=True)
    slot_r = jnp.sum(jnp.where(cols == iota(blocks, 0), rank_col, 0), axis=0, keepdims=True)

    def away(c, s):
        owner = c // row_tiles
        return ((owner >> 1) ^ (me >> 1)) * (2 * SLOT) + (owner & 1) * SLOT + s

    away_r, away_c = away(cols, slot_r), away(cols_c, slot_c)
    per = 2 * SLOT
    chip, chip_c = cols // row_tiles >> 1 == me >> 1, cols_c // row_tiles >> 1 == me >> 1
    near, near_c = valid & chip, valid_c & chip_c
    far, far_c = valid & ~chip, valid_c & ~chip_c
    write_list(
        out_ref, 0, rows, rows_c, near, near_c, row_tiles, cols_c % (2 * row_tiles), 2 * row_tiles
    )
    write_list(
        out_ref, 1, rows, rows_c, far, far_c, row_tiles, away_c - per, (n_chip - 1) * per
    )
    own, own_c = valid & (cols // row_tiles == me), valid_c & (cols_c // row_tiles == me)
    other, other_c = valid & (cols // row_tiles != me), valid_c & (cols_c // row_tiles != me)
    write_list(out_ref, 2, away_r, away_c, other, other_c, n_chip * per, rows_c, row_tiles)
    write_list(
        out_ref, 3, cols % row_tiles, cols_c % row_tiles, own, own_c, row_tiles, rows_c, row_tiles
    )


def sparse_loop(list_ref, which, x_ref, tiles_ref, acc_ref, forward):
    def step(s, carry):
        for u in range(UNROLL):
            p = 2 * (s * UNROLL + u)
            w0 = list_ref[which, p]
            w1 = list_ref[which, p + 1]
            x = jnp.concatenate([x_ref[(w0 >> 10) & 1023], x_ref[(w1 >> 10) & 1023]], axis=1)
            t0, t1 = tiles_ref[w0 & 1023], tiles_ref[w1 & 1023]
            if forward:
                part = lax.dot_general(
                    x,
                    jnp.concatenate([t0, t1], axis=1),
                    (((1,), (1,)), ((), ())),
                    preferred_element_type=F32,
                )
            else:
                part = jnp.dot(x, jnp.concatenate([t0, t1], axis=0), preferred_element_type=F32)
            acc_ref[w0 >> 20] += part
        return carry

    lax.fori_loop(0, list_ref[4 + which, 0], step, 0)


def load_kernel(in_ref, out_ref, sems):
    n = in_ref.shape[0] // LOADS
    copies = [
        pltpu.make_async_copy(
            in_ref.at[pl.ds(i * n, n)], out_ref.at[pl.ds(i * n, n)], sems.at[i]
        )
        for i in range(LOADS)
    ]
    for c in copies:
        c.start()
    for c in copies:
        c.wait()


def pack_kernel(me_ref, feat_ref, sib_ref, out_ref):
    tiles = feat_ref.shape[1] // TILE
    base = (me_ref[0] & 1) * tiles
    for k in range(tiles):
        out_ref[base + k] = feat_ref[:, k * TILE : (k + 1) * TILE]
        out_ref[tiles - base + k] = sib_ref[:, k * TILE : (k + 1) * TILE]
    out_ref[2 * tiles] = jnp.zeros_like(out_ref[0])


def send_kernel(n_chip, row_tiles, me_ref, *refs):
    need_refs, x_ref, outs = refs[: n_chip - 1], refs[n_chip - 1], refs[n_chip:]
    for need_ref, out in zip(need_refs, outs):
        for q in range(2):
            for j in range(SLOT):
                out[q * SLOT + j] = x_ref[
                    q * row_tiles + need_ref[((me_ref[0] >> 1) << 1) + q, j]
                ]


def fill_from_wide(x_ref, wide_ref, count):
    for k in range(count):
        x_ref[k] = wide_ref[:, k * TILE : (k + 1) * TILE]
    x_ref[count] = jnp.zeros_like(x_ref[count])


def near_fwd_kernel(list_ref, tiles_ref, x_ref, acc_ref):
    acc_ref[...] = jnp.zeros_like(acc_ref)
    sparse_loop(list_ref, 0, x_ref, tiles_ref, acc_ref, True)


def own_bwd_kernel(list_ref, tiles_ref, wide_ref, acc_ref, x_ref):
    fill_from_wide(x_ref, wide_ref, x_ref.shape[0] - 1)
    acc_ref[...] = jnp.zeros_like(acc_ref)
    sparse_loop(list_ref, 3, x_ref, tiles_ref, acc_ref, False)


def far_fwd_kernel(n_in, list_ref, me_ref, tiles_ref, *refs):
    ins, base_ref, rest = refs[:n_in], refs[n_in], refs[n_in + 1 :]
    outs, (x_ref, acc_ref) = rest[:-2], rest[-2:]
    per = 2 * SLOT
    for d, r in enumerate(ins):
        x_ref[d * per : (d + 1) * per] = r[...]
    x_ref[n_in * per] = jnp.zeros_like(x_ref[0])
    acc_ref[...] = base_ref[...]
    sparse_loop(list_ref, 1, x_ref, tiles_ref, acc_ref, True)
    per = acc_ref.shape[0] // len(outs)
    for k, out in enumerate(outs):
        block = me_ref[0] ^ k
        for i in range(per):
            out[:, i * TILE : (i + 1) * TILE] = acc_ref[block * per + i].astype(BF)


def weight_kernel(me_ref, s_ref, z_ref, own_ref, sib_ref):
    n_chip, per, _ = own_ref.shape
    z = z_ref[...]
    for q, out in enumerate((own_ref, sib_ref)):
        core = (me_ref[0] & 1) ^ q
        for c in range(n_chip):
            rows = pl.ds(pl.multiple_of((2 * c + core) * per, per), per)
            out[c] = lax.dot_general(
                s_ref[rows, :], z, (((1,), (1,)), ((), ())), preferred_element_type=F32
            ).astype(out.dtype)


def weight_pair_kernel(me_ref, own_ref, got_ref, keep_ref, *outs):
    for e in range(len(outs) + 1):
        c = (me_ref[0] >> 1) ^ e
        total = own_ref[c] + got_ref[c].astype(F32)
        if e == 0:
            keep_ref[...] = total
        else:
            outs[e - 1][...] = total.astype(BF)


def far_bwd_kernel(n_col, list_ref, mec_ref, mer_ref, tiles_ref, *refs):
    ins, rest = refs[:n_col], refs[n_col:]
    wide_ref, sib_ref, (x_ref, acc_ref) = rest[0], rest[1], rest[-2:]
    outs = rest[2:-2]
    per = 2 * SLOT
    gather_blocks(wide_ref, mec_ref[0], ins)
    fill_from_wide(x_ref, wide_ref, x_ref.shape[0] - 1)
    acc_ref[...] = jnp.zeros_like(acc_ref)
    sparse_loop(list_ref, 2, x_ref, tiles_ref, acc_ref, False)
    for e, out in enumerate(outs):
        out[...] = acc_ref[(e + 1) * per : (e + 2) * per].astype(BF)
    other = 1 - (mer_ref[0] & 1)
    for j in range(SLOT):
        sib_ref[j] = acc_ref[other * SLOT + j].astype(BF)


def forward_kernel(me_ref, *refs):
    other = 1 - (me_ref[0] & 1)
    for e, r in enumerate(refs[:-1]):
        for j in range(SLOT):
            refs[-1][e * SLOT + j] = r[other * SLOT + j]


def join_kernel(n_chip, me_ref, table_ref, base_ref, sib_ref, fwd_ref, *refs):
    ins, (out_ref, acc_ref) = refs[:-2], refs[-2:]
    me = me_ref[0]
    core = me & 1
    n_row = 2 * n_chip

    def tile(e, j, other):
        return table_ref[(other * n_chip + e) * n_row + me, j]

    acc_ref[...] = base_ref[...]
    for j in range(SLOT):
        acc_ref[tile(0, j, 1)] += sib_ref[j].astype(F32)
        for e, r in enumerate(ins):
            acc_ref[tile(e + 1, j, 0)] += r[core * SLOT + j].astype(F32)
            acc_ref[tile(e + 1, j, 1)] += fwd_ref[e * SLOT + j].astype(F32)
    for k in range(acc_ref.shape[0]):
        out_ref[:, k * TILE : (k + 1) * TILE] = acc_ref[k].astype(BF)


def pair_kernel(me_ref, own_ref, sib_ref, out_ref):
    core = me_ref[0] & 1
    out_ref[core] = own_ref[...]
    out_ref[1 - core] = sib_ref[...]


def weight_place_kernel(me_ref, *refs):
    out_ref = refs[-1]
    per = refs[0].shape[1]
    for e, r in enumerate(refs[:-1]):
        for q in range(2):
            row = (((me_ref[0] >> 1) ^ e) << 1) + q
            out_ref[pl.ds(pl.multiple_of(row * per, per), per), :] = r[q]


def dense_kernel(n_col, me_ref, wt_ref, w_ref, *refs):
    s_refs, g_refs = refs[:n_col], refs[n_col : 2 * n_col]
    o_refs, y_refs = refs[2 * n_col : 3 * n_col], refs[3 * n_col : 4 * n_col]
    z_ref, s_ref = refs[4 * n_col], refs[4 * n_col + 1]
    f_loc = s_refs[0].shape[0]
    me = me_ref[0]
    for k in range(n_col):
        s_ref[pl.ds(pl.multiple_of((me ^ k) * f_loc, f_loc), f_loc), :] = s_refs[k][...]
    s_all = s_ref[...]
    for k in range(n_col):
        rows = pl.ds(pl.multiple_of((me ^ k) * f_loc, f_loc), f_loc)
        pre = jnp.dot(wt_ref[rows, :], s_all, preferred_element_type=F32)
        sig = 1.0 / (1.0 + jnp.exp(-pre))
        o_refs[k][...] = (pre * sig).astype(BF)
        slope = sig * (1.0 + pre * (1.0 - sig))
        z_ref[rows, :] = (g_refs[k][...].astype(F32) * slope).astype(BF)
    z_all = z_ref[...]
    for k in range(n_col):
        rows = pl.ds(pl.multiple_of((me ^ k) * f_loc, f_loc), f_loc)
        y_refs[k][...] = jnp.dot(w_ref[rows, :], z_all, preferred_element_type=F32).astype(BF)


def gather_blocks(wide_ref, me, refs):
    width = refs[0].shape[1]
    for k, r in enumerate(refs):
        wide_ref[:, pl.ds(pl.multiple_of((me ^ k) * width, width), width)] = r[...]


def place_kernel(me_ref, *refs):
    wide_ref = refs[-1]
    width = refs[0].shape[1]
    for k, r in enumerate(refs[:-1]):
        at = pl.multiple_of((me_ref[0] ^ k) * width, width)
        wide_ref[:, pl.ds(at, width)] = r[: wide_ref.shape[0], :]


def split_kernel(me_ref, x_ref, *outs):
    width = outs[0].shape[1]
    for k, out in enumerate(outs):
        out[...] = x_ref[:, pl.ds(pl.multiple_of((me_ref[0] ^ k) * width, width), width)]


def weight_cols_kernel(n_chip, me_ref, *refs):
    n_col = (len(refs) - n_chip - 2) // 2
    ins, o_refs = refs[:n_chip], refs[n_chip : n_chip + n_col]
    outs, own_ref, sum_ref = refs[n_chip + n_col : -2], refs[-2], refs[-1]
    total = ins[0][...]
    for r in ins[1:]:
        total += r[...].astype(F32)
    sum_ref[...] = total
    h_loc, part = o_refs[0].shape
    rows = total.shape[0] * h_loc // part
    for k, out in enumerate(outs):
        if k:
            out[:h_loc, :] = o_refs[k][...]
        for c in range(n_col):

            @pl.when(me_ref[0] ^ k == c)
            def _():
                mine = sum_ref[:, c * h_loc : (c + 1) * h_loc]
                if k == 0:
                    own_ref[...] = mine
                else:
                    for i in range(part // h_loc):
                        out[h_loc : h_loc + rows, i * h_loc : (i + 1) * h_loc] = mine[
                            i * rows : (i + 1) * rows
                        ].astype(BF)


def weight_scale_kernel(scale, own_ref, *refs):
    out_ref = refs[-1]
    n_rows, h_loc = own_ref.shape
    rows = n_rows * h_loc // refs[0].shape[1]
    for i in range(n_rows // rows):
        total = own_ref[i * rows : (i + 1) * rows, :]
        for r in refs[:-1]:
            total += r[h_loc : h_loc + rows, i * h_loc : (i + 1) * h_loc].astype(F32)
        out_ref[i * rows : (i + 1) * rows, :] = total * scale


def shards(features, weight, tile_cols, tile_rows, tile_count, tile_values, out_grad):
    n_row, n_col = lax.axis_size("row"), lax.axis_size("col")
    n_chip = n_row // 2
    me_r, me_c = lax.axis_index("row").astype(jnp.int32), lax.axis_index("col").astype(jnp.int32)
    mer, mec = me_r.reshape(1), me_c.reshape(1)
    f_loc, nodes = features.shape
    h_loc = out_grad.shape[0]
    n_f, n_h = weight.shape
    row_tiles = nodes // TILE
    part = nodes // n_col
    slots = tile_cols.shape[1]
    per = 2 * SLOT
    sds = jax.ShapeDtypeStruct
    tile_flops = 2 * f_loc * TILE * TILE
    tile_bytes = slots * TILE * TILE * 2

    tile_values, mer, mec, weight_t = lax.optimization_barrier(
        (tile_values, mer, mec, weight.T)
    )
    tile_values = pl.pallas_call(
        load_kernel,
        out_shape=sds(tile_values.shape, BF),
        in_specs=[pl.BlockSpec(memory_space=pltpu.HBM)],
        out_specs=VM,
        scratch_shapes=[pltpu.SemaphoreType.DMA((LOADS,))],
        compiler_params=pltpu.CompilerParams(vmem_limit_bytes=24 << 20),
        cost_estimate=pl.CostEstimate(flops=0, bytes_accessed=tile_bytes, transcendentals=0),
    )(pltpu.with_memory_space_constraint(tile_values, pltpu.HBM))

    def over_chips(x):
        return swap(x, "row", n_row, 1)

    sib_feat = over_chips(features)
    need = call(
        functools.partial(need_kernel, n_row, row_tiles),
        sds((n_row, 128), jnp.int32),
        [],
        (tile_count,),
        (tile_cols,),
    )
    needs = [need] + [swap(need, "row", n_row, 2 * e) for e in range(1, n_chip)]
    length = -(-(slots + n_chip * per + 2 * UNROLL) // 128) * 128
    lists = call(
        functools.partial(lists_kernel, n_row, row_tiles),
        sds((8, length), jnp.int32),
        [],
        (tile_count, mer),
        (tile_cols, tile_rows),
    )
    x_near = call(
        pack_kernel,
        sds((2 * row_tiles + 1, f_loc, TILE), BF),
        [],
        (mer,),
        (features, sib_feat),
        nbytes=f_loc * nodes * 8,
    )
    g_parts = call(
        split_kernel,
        [sds((h_loc, part), BF)] * n_col,
        [],
        (mec,),
        (out_grad,),
        nbytes=h_loc * nodes * 4,
    )
    needs, x_near, lists, tile_values, g_parts = lax.optimization_barrier(
        (needs, x_near, lists, tile_values, g_parts)
    )
    sends = call(
        functools.partial(send_kernel, n_chip, row_tiles),
        [sds((per, f_loc, TILE), BF)] * (n_chip - 1),
        [],
        (mer, *needs[1:]),
        (x_near,),
        nbytes=4 * n_chip * per * f_loc * TILE,
    )
    got = [swap(x, "row", n_row, 2 * (e + 1)) for e, x in enumerate(sends)]
    table = jnp.concatenate(needs, axis=0)
    table = jnp.concatenate([table, over_chips(table)], axis=0)
    got, table = lax.optimization_barrier((got, table))

    grads = [g if k == 0 else swap(g, "col", n_col, k) for k, g in enumerate(g_parts)]

    acc = call(
        near_fwd_kernel,
        sds((row_tiles, f_loc, TILE), F32),
        [],
        (lists,),
        (x_near,),
        (tile_values,),
        flops=tile_flops * slots,
        nbytes=tile_bytes,
    )
    s_parts = call(
        functools.partial(far_fwd_kernel, n_chip - 1),
        [sds((f_loc, part), BF)] * n_col,
        [
            pltpu.VMEM(((n_chip - 1) * per + 1, f_loc, TILE), BF),
            pltpu.VMEM((row_tiles, f_loc, TILE), F32),
        ],
        (lists, mec),
        (*got, acc),
        (tile_values,),
        flops=tile_flops * slots,
        nbytes=tile_bytes,
    )
    s_got = [s if k == 0 else swap(s, "col", n_col, k) for k, s in enumerate(s_parts)]

    res = call(
        functools.partial(dense_kernel, n_col),
        [sds((h_loc, part), BF)] * n_col
        + [sds((f_loc, part), BF)] * n_col
        + [sds((n_h, part), BF), sds((n_f, part), BF)],
        [],
        (mec,),
        (weight_t, weight, *s_got, *grads),
        flops=4 * n_f * n_h * part,
        nbytes=n_f * part * 8,
    )
    o_parts, y_parts, z_all, s_all = res[:n_col], res[n_col : 2 * n_col], res[-2], res[-1]
    y_got = [y if k == 0 else swap(y, "col", n_col, k) for k, y in enumerate(y_parts)]

    w_rows = n_f // n_row
    w_own, w_sib = call(
        weight_kernel,
        [sds((n_chip, w_rows, n_h), F32), sds((n_chip, w_rows, n_h), BF)],
        [],
        (mer,),
        (s_all, z_all),
        flops=2 * n_f * n_h * part,
        nbytes=n_f * part * 8,
    )
    w_parts = call(
        weight_pair_kernel,
        [sds((w_rows, n_h), F32)] + [sds((w_rows, n_h), BF)] * (n_chip - 1),
        [],
        (mer,),
        (w_own, over_chips(w_sib)),
        nbytes=n_f * n_h * 4,
    )
    w_chips = [w if e == 0 else swap(w, "row", n_row, 2 * e) for e, w in enumerate(w_parts)]
    more = -(-(w_rows * h_loc // part) // 16) * 16
    mixed = call(
        functools.partial(weight_cols_kernel, n_chip),
        [sds((h_loc + more, part), BF)] * n_col + [sds((w_rows, h_loc), F32)],
        [pltpu.VMEM((w_rows, n_h), F32)],
        (mec,),
        (*w_chips, *o_parts),
        nbytes=n_h * part * 4,
    )
    w_own_cols = mixed[-1]
    mixed = [m if k == 0 else swap(m, "col", n_col, k) for k, m in enumerate(mixed[:-1])]

    y_got, w_chips = lax.optimization_barrier((y_got, w_chips))
    back = call(
        functools.partial(far_bwd_kernel, n_col),
        [sds((f_loc, nodes), BF), sds((SLOT, f_loc, TILE), BF)]
        + [sds((per, f_loc, TILE), BF)] * (n_chip - 1),
        [
            pltpu.VMEM((row_tiles + 1, f_loc, TILE), BF),
            pltpu.VMEM((n_chip * per, f_loc, TILE), F32),
        ],
        (lists, mec, mer),
        tuple(y_got),
        (tile_values,),
        flops=tile_flops * slots,
        nbytes=tile_bytes,
    )
    y_wide, to_sib, contribs = back[0], back[1], back[2:]
    returned = [swap(x, "row", n_row, 2 * (e + 1)) for e, x in enumerate(contribs)]
    from_sib = over_chips(to_sib)

    w_mine = call(
        functools.partial(weight_scale_kernel, float(nodes * n_row) ** (-0.5)),
        sds((w_rows, h_loc), F32),
        [],
        (),
        (w_own_cols, *mixed[1:]),
    )

    w_mine = call(
        functools.partial(weight_scale_kernel, float(nodes * n_row) ** (-0.5)),
        sds((w_rows, h_loc), F32),
        [],
        (),
        (w_own_cols, *mixed[1:]),
    )

    o_parts, _ = lax.optimization_barrier((o_parts, to_sib))
    o_got = [o if k == 0 else swap(o, "col", n_col, k) for k, o in enumerate(o_parts)]
    acc_b = call(
        own_bwd_kernel,
        sds((row_tiles, f_loc, TILE), F32),
        [pltpu.VMEM((row_tiles + 1, f_loc, TILE), BF)],
        (lists,),
        (y_wide,),
        (tile_values,),
        flops=tile_flops * slots,
        nbytes=tile_bytes,
    )
    returned, acc_b, w_mine = lax.optimization_barrier((returned, acc_b, w_mine))
    passed = call(
        forward_kernel,
        sds(((n_chip - 1) * SLOT, f_loc, TILE), BF),
        [],
        (mer,),
        tuple(returned),
    )
    w_pair = call(
        pair_kernel, sds((2, w_rows, h_loc), F32), [], (mer,), (w_mine, over_chips(w_mine))
    )
    w_chips = [w_pair] + [swap(w_pair, "row", n_row, 2 * e) for e in range(1, n_chip)]
    weight_grad = call(
        weight_place_kernel,
        sds((n_f, h_loc), F32),
        [],
        (mer,),
        tuple(w_chips),
        nbytes=n_f * h_loc * 8,
    )

    input_grad = call(
        functools.partial(join_kernel, n_chip),
        sds((f_loc, nodes), BF),
        [pltpu.VMEM((row_tiles, f_loc, TILE), F32)],
        (mer, table),
        (acc_b, from_sib, over_chips(passed), *returned),
        nbytes=f_loc * nodes * 8,
    )
    output = call(
        place_kernel, sds((h_loc, nodes), BF), [], (mec,), (o_parts[0], *mixed[1:]), nbytes=h_loc * nodes * 4
    )
    return output, input_grad, weight_grad


def solution(mesh):
    return jax.shard_map(
        shards,
        mesh=mesh,
        in_specs=(
            P("col", "row"),
            P(),
            P("row", None),
            P("row", None),
            P("row"),
            P("row", None, None),
            P("col", "row"),
        ),
        out_specs=(P("col", "row"), P("col", "row"), P(None, "col")),
        check_vma=False,
    )
```

time: 145 us -> 100 us (0.69)
  the two profiles are of different devices: /device:TPU:13 before, /device:TPU:0 now
where the time goes in v2:
time: 100 us; the launch traced here: 101 us
  starting transfers between devices  44.1 us (44%)
  waiting for transfers between devices  31.3 us (31%)
  Pallas kernels  21.7 us (22%)
  local copies, waits for them, and re-layouts  1.97 us (2%)
  between operations  1.6 us (2%)
    ppermute x33, starting transfers between devices, swap(): return lax.ppermute(x, axis, [(i, i ^ k) for i in range(n)])  44.1 us
    ppermute x33, waiting for transfers between devices, swap(): return lax.ppermute(x, axis, [(i, i ^ k) for i in range(n)])  31.3 us
    pallas_call x19, Pallas kernels, call(): pl.pallas_call(kernel, out_shape=outs, in_specs=[SM] * len(smem) + [VM] *...  18.1 us
    pallas_call x1, Pallas kernels, shards(): pl.pallas_call(load_kernel, out_shape=sds(tile_values.shape, BF), in_spec...  3.56 us
  transfers between devices with their start and end apart: 33, of which 10 were waited for; matrix products, arithmetic and copies ran while one was open for 1% of the time, Pallas kernels for 16%

profile of v2, /device:TPU:0, one launch (start us, length us, event | category | flops | bytes accessed | tf_op | source)
XLA Modules:
  0.0 100.7 jit_solution(647774460873562316)
XLA Ops:
  2.8 3.5 %collective-permute-start.2 = (s32[8,128]{1,0:T(8,128)S(1)}, s32[8,128]{1,0:T(8,128)S(1)}, u32[]{:S(2)}, u32[]{:S(2)}) collective-permute-start(s32[8,128]{1,0:T(8,128)S(1)} %shard_map.94), channel_id=1, source_target_pairs={{0,24},{4,28},{8,16},{12,20},{16,8},{20,12},{24,0},{28,4},{1,25},{... | collective-permute-start | bytes 12296 | tf_op jit(solution)/shard_map/ppermute | solution.py:33
  8.2 3.6 %shard_map.97.tiles_ref = bf16[256,128,128]{2,1,0:T(8,128)(2,1)S(1)} custom-call(bf16[256,128,128]{2,1,0:T(8,128)(2,1)} %in_ref), custom_call_target="tpu_custom_call" | custom-call | bytes 8388608 | tf_op jit(solution)/shard_map/pallas_call | solution.py:396
  14.6 2.0 %collective-permute-start.4 = (bf16[8,128,128]{2,1,0:T(8,128)(2,1)S(1)}, bf16[8,128,128]{2,1,0:T(8,128)(2,1)S(1)}, u32[]{:S(2)}, u32[]{:S(2)}) collective-permute-start(bf16[8,128,128]{2,1,0:T(8,128)(2,1)S(1)} %get-tuple-element.82), channel_id=1, source_target_pairs={{0,8},{4,12},{8,0},{12,4},{16,24},{20,28},{24,16},{28,20},{1,9},{5... | collective-permute-start | bytes 786440 | tf_op jit(solution)/shard_map/ppermute | solution.py:33
  18.1 2.0 %collective-permute-start.11 = (bf16[128,512]{1,0:T(8,128)(2,1)S(1)}, bf16[128,512]{1,0:T(8,128)(2,1)S(1)}, u32[]{:S(2)}, u32[]{:S(2)}) collective-permute-start(bf16[128,512]{1,0:T(8,128)(2,1)S(1)} %get-tuple-element.94), channel_id=1, source_target_pairs={{0,1},{1,0},{2,3},{3,2},{4,5},{5,4},{6,7},{7,6},{8,9},{9,8},{10,11... | collective-permute-start | bytes 393224 | tf_op jit(solution)/shard_map/ppermute | solution.py:33
  20.1 2.0 %shard_map.100.refs_3_ = f32[16,128,128]{2,1,0:T(8,128)S(1)} custom-call(s32[8,384]{1,0:T(8,128)S(1)} %shard_map.96.list_ref, bf16[256,128,128]{2,1,0:T(8,128)(2,1)S(1)} %shard_map.97.tiles_ref, bf16[33,128,128]{2,1,0:T(8,128)(2,1)S(1)} %shard_map.95.refs_3_.x_ref), custom_call_target="tpu_custom_call" | custom-call | flops 1073741824 | bytes 8388608 | tf_op jit(solution)/shard_map/pallas_call | solution.py:21
  22.1 2.7 %collective-permute-start.12 = (bf16[128,512]{1,0:T(8,128)(2,1)S(1)}, bf16[128,512]{1,0:T(8,128)(2,1)S(1)}, u32[]{:S(2)}, u32[]{:S(2)}) collective-permute-start(bf16[128,512]{1,0:T(8,128)(2,1)S(1)} %get-tuple-element.95), channel_id=1, source_target_pairs={{0,2},{1,3},{2,0},{3,1},{4,6},{5,7},{6,4},{7,5},{8,10},{9,11},{10,... | collective-permute-start | bytes 393224 | tf_op jit(solution)/shard_map/ppermute | solution.py:33
  24.8 3.0 %collective-permute-start.13 = (bf16[128,512]{1,0:T(8,128)(2,1)S(1)}, bf16[128,512]{1,0:T(8,128)(2,1)S(1)}, u32[]{:S(2)}, u32[]{:S(2)}) collective-permute-start(bf16[128,512]{1,0:T(8,128)(2,1)S(1)} %get-tuple-element.96), channel_id=1, source_target_pairs={{0,3},{1,2},{2,1},{3,0},{4,7},{5,6},{6,5},{7,4},{8,11},{9,10},{10,... | collective-permute-start | bytes 393224 | tf_op jit(solution)/shard_map/ppermute | solution.py:33
  27.8 2.8 %collective-permute-done.5.refs_1_ = bf16[8,128,128]{2,1,0:T(8,128)(2,1)S(1)} collective-permute-done((bf16[8,128,128]{2,1,0:T(8,128)(2,1)S(1)}, bf16[8,128,128]{2,1,0:T(8,128)(2,1)S(1)}, u32[]{:S(2)}, u32[]{:S(2)}) %collective-permute-start.5) | collective-permute-done | bytes 262176 | tf_op jit(solution)/shard_map/ppermute | solution.py:33
  30.6 1.9 %shard_map.101 = (bf16[128,512]{1,0:T(8,128)(2,1)S(1)}, bf16[128,512]{1,0:T(8,128)(2,1)S(1)}, bf16[128,512]{1,0:T(8,128)(2,1)S(1)}, bf16[128,512]{1,0:T(8,128)(2,1)S(1)}) custom-call(s32[8,384]{1,0:T(8,128)S(1)} %shard_map.96.list_ref, s32[1]{0:T(128)} %bitcast.1.me_ref.mec_ref, bf16[256,128,128]{2,1,0:T(8,128)(2,1)S(1)} %shard_map.97.tiles_ref, ...), custom_call_target="tpu_custom_call" | custom-call | flops 1073741824 | bytes 8388608 | tf_op jit(solution)/shard_map/pallas_call | solution.py:21
  32.5 1.6 %collective-permute-start.8 = (bf16[128,512]{1,0:T(8,128)(2,1)S(1)}, bf16[128,512]{1,0:T(8,128)(2,1)S(1)}, u32[]{:S(2)}, u32[]{:S(2)}) collective-permute-start(bf16[128,512]{1,0:T(8,128)(2,1)S(1)} %get-tuple-element.90), channel_id=1, source_target_pairs={{0,1},{1,0},{2,3},{3,2},{4,5},{5,4},{6,7},{7,6},{8,9},{9,8},{10,11... | collective-permute-start | bytes 393224 | tf_op jit(solution)/shard_map/ppermute | solution.py:33
  34.1 2.6 %collective-permute-start.9 = (bf16[128,512]{1,0:T(8,128)(2,1)S(1)}, bf16[128,512]{1,0:T(8,128)(2,1)S(1)}, u32[]{:S(2)}, u32[]{:S(2)}) collective-permute-start(bf16[128,512]{1,0:T(8,128)(2,1)S(1)} %get-tuple-element.91), channel_id=1, source_target_pairs={{0,2},{1,3},{2,0},{3,1},{4,6},{5,7},{6,4},{7,5},{8,10},{9,11},{10,... | collective-permute-start | bytes 393224 | tf_op jit(solution)/shard_map/ppermute | solution.py:33
  36.9 3.2 %collective-permute-done.8.refs_1_ = bf16[128,512]{1,0:T(8,128)(2,1)S(1)} collective-permute-done((bf16[128,512]{1,0:T(8,128)(2,1)S(1)}, bf16[128,512]{1,0:T(8,128)(2,1)S(1)}, u32[]{:S(2)}, u32[]{:S(2)}) %collective-permute-start.8) | collective-permute-done | bytes 131104 | tf_op jit(solution)/shard_map/ppermute | solution.py:33
  40.1 6.9 %collective-permute-done.9.refs_2_ = bf16[128,512]{1,0:T(8,128)(2,1)S(1)} collective-permute-done((bf16[128,512]{1,0:T(8,128)(2,1)S(1)}, bf16[128,512]{1,0:T(8,128)(2,1)S(1)}, u32[]{:S(2)}, u32[]{:S(2)}) %collective-permute-start.9) | collective-permute-done | bytes 131104 | tf_op jit(solution)/shard_map/ppermute | solution.py:33
  49.7 2.4 %collective-permute-start.14 = (bf16[128,512]{1,0:T(8,128)(2,1)S(1)}, bf16[128,512]{1,0:T(8,128)(2,1)S(1)}, u32[]{:S(2)}, u32[]{:S(2)}) collective-permute-start(bf16[128,512]{1,0:T(8,128)(2,1)S(1)} %get-tuple-element.102), channel_id=1, source_target_pairs={{0,1},{1,0},{2,3},{3,2},{4,5},{5,4},{6,7},{7,6},{8,9},{9,8},{10,11... | collective-permute-start | bytes 393224 | tf_op jit(solution)/shard_map/ppermute | solution.py:33
  54.6 2.3 %collective-permute-start.18 = (bf16[64,512]{1,0:T(8,128)(2,1)S(1)}, bf16[64,512]{1,0:T(8,128)(2,1)S(1)}, u32[]{:S(2)}, u32[]{:S(2)}) collective-permute-start(bf16[64,512]{1,0:T(8,128)(2,1)S(1)} %get-tuple-element.110), channel_id=1, source_target_pairs={{0,8},{4,12},{8,0},{12,4},{16,24},{20,28},{24,16},{28,20},{1,9},{5... | collective-permute-start | bytes 196616 | tf_op jit(solution)/shard_map/ppermute | solution.py:33
  58.4 2.5 %collective-permute-start.20 = (bf16[64,512]{1,0:T(8,128)(2,1)S(1)}, bf16[64,512]{1,0:T(8,128)(2,1)S(1)}, u32[]{:S(2)}, u32[]{:S(2)}) collective-permute-start(bf16[64,512]{1,0:T(8,128)(2,1)S(1)} %get-tuple-element.112), channel_id=1, source_target_pairs={{0,24},{4,28},{8,16},{12,20},{16,8},{20,12},{24,0},{28,4},{1,25},{... | collective-permute-start | bytes 196616 | tf_op jit(solution)/shard_map/ppermute | solution.py:33
  60.9 4.1 %collective-permute-done.15.refs_2_ = bf16[128,512]{1,0:T(8,128)(2,1)S(1)} collective-permute-done((bf16[128,512]{1,0:T(8,128)(2,1)S(1)}, bf16[128,512]{1,0:T(8,128)(2,1)S(1)}, u32[]{:S(2)}, u32[]{:S(2)}) %collective-permute-start.15) | collective-permute-done | bytes 131104 | tf_op jit(solution)/shard_map/ppermute | solution.py:33
  65.9 2.6 %collective-permute-start.21 = (bf16[144,512]{1,0:T(8,128)(2,1)S(1)}, bf16[144,512]{1,0:T(8,128)(2,1)S(1)}, u32[]{:S(2)}, u32[]{:S(2)}) collective-permute-start(bf16[144,512]{1,0:T(8,128)(2,1)S(1)} %get-tuple-element.119), channel_id=1, source_target_pairs={{0,1},{1,0},{2,3},{3,2},{4,5},{5,4},{6,7},{7,6},{8,9},{9,8},{10,11... | collective-permute-start | bytes 442376 | tf_op jit(solution)/shard_map/ppermute | solution.py:33
  68.4 2.2 %shard_map.105 = (bf16[128,2048]{1,0:T(8,128)(2,1)S(1)}, bf16[4,128,128]{2,1,0:T(8,128)(2,1)S(1)}, bf16[8,128,128]{2,1,0:T(8,128)(2,1)S(1)}, bf16[8,128,128]{2,1,0:T(8,128)(2,1)S(1)}, bf16[8,128,128]{2,1,0:T(8,128)(2,1)S(1)}) custom-call(s32[8,384]{1,0:T(8,128)S(1)} %shard_map.96.list_ref, s32[1]{0:T(128)} %bitcast.1.me_ref.mec_ref, s32[1]{0:T(128)} %bitcast.me_ref.mer_ref, ...), custom_call_target="tpu_custom_call" | custom-call | flops 1073741824 | bytes 8388608 | tf_op jit(solution)/shard_map/pallas_call | solution.py:21
  70.7 2.2 %collective-permute-start.24 = (bf16[8,128,128]{2,1,0:T(8,128)(2,1)S(1)}, bf16[8,128,128]{2,1,0:T(8,128)(2,1)S(1)}, u32[]{:S(2)}, u32[]{:S(2)}) collective-permute-start(bf16[8,128,128]{2,1,0:T(8,128)(2,1)S(1)} %get-tuple-element.123), channel_id=1, source_target_pairs={{0,8},{4,12},{8,0},{12,4},{16,24},{20,28},{24,16},{28,20},{1,9},{5... | collective-permute-start | bytes 786440 | tf_op jit(solution)/shard_map/ppermute | solution.py:33
  76.9 1.8 %shard_map.108.base_ref = f32[16,128,128]{2,1,0:T(8,128)S(1)} custom-call(s32[8,384]{1,0:T(8,128)S(1)} %shard_map.96.list_ref, bf16[256,128,128]{2,1,0:T(8,128)(2,1)S(1)} %shard_map.97.tiles_ref, bf16[128,2048]{1,0:T(8,128)(2,1)S(1)} %get-tuple-element.126.wide_ref), custom_call_target="tpu_custom_call" | custom-call | flops 1073741824 | bytes 8388608 | tf_op jit(solution)/shard_map/pallas_call | solution.py:21
  78.7 9.1 %collective-permute-done.22.refs_2_.refs_1_ = bf16[144,512]{1,0:T(8,128)(2,1)S(1)} collective-permute-done((bf16[144,512]{1,0:T(8,128)(2,1)S(1)}, bf16[144,512]{1,0:T(8,128)(2,1)S(1)}, u32[]{:S(2)}, u32[]{:S(2)}) %collective-permute-start.22) | collective-permute-done | bytes 147488 | tf_op jit(solution)/shard_map/ppermute | solution.py:33
  90.0 2.1 %collective-permute-start.32 = (f32[2,64,128]{2,1,0:T(8,128)S(1)}, f32[2,64,128]{2,1,0:T(8,128)S(1)}, u32[]{:S(2)}, u32[]{:S(2)}) collective-permute-start(f32[2,64,128]{2,1,0:T(8,128)S(1)} %shard_map.112.refs_0_), channel_id=1, source_target_pairs={{0,24},{4,28},{8,16},{12,20},{16,8},{20,12},{24,0},{28,4},{1,25},{... | collective-permute-start | bytes 196616 | tf_op jit(solution)/shard_map/ppermute | solution.py:33
  98.4 2.3 %shard_map.111 = bf16[128,2048]{1,0:T(8,128)(2,1)} custom-call(s32[1]{0:T(128)} %bitcast.me_ref.mer_ref, s32[64,128]{1,0:T(8,128)S(1)} %constant_dynamic-update-slice_fusion.table_ref, f32[16,128,128]{2,1,0:T(8,128)S(1)} %shard_map.108.base_ref, bf16[4,128,128]{2,1,0:T(8,128)(2,1)S(1)} %collective-permute-done.27.sib_ref, ...), custom_call_target="tpu_custom_call" | custom-call | bytes 2097152 | tf_op jit(solution)/shard_map/pallas_call | solution.py:21
  (81 shorter events, 27.7 us)
Async XLA Ops:
  0.6 12.8 %collective-permute-start.3 = (bf16[128,2048]{1,0:T(8,128)(2,1)}, bf16[128,2048]{1,0:T(8,128)(2,1)S(1)}, u32[]{:S(2)}, u32[]{:S(2)}) collective-permute-start(bf16[128,2048]{1,0:T(8,128)(2,1)} %feat_ref.1), channel_id=1, source_target_pairs={{0,4},{4,0},{8,12},{12,8},{16,20},{20,16},{24,28},{28,24},{1,5},{5... | collective-permute-start | bytes 1572872 | tf_op jit(solution)/shard_map/ppermute | solution.py:33
  2.8 10.9 %collective-permute-start.2 = (s32[8,128]{1,0:T(8,128)S(1)}, s32[8,128]{1,0:T(8,128)S(1)}, u32[]{:S(2)}, u32[]{:S(2)}) collective-permute-start(s32[8,128]{1,0:T(8,128)S(1)} %shard_map.94), channel_id=1, source_target_pairs={{0,24},{4,28},{8,16},{12,20},{16,8},{20,12},{24,0},{28,4},{1,25},{... | collective-permute-start | bytes 12296 | tf_op jit(solution)/shard_map/ppermute | solution.py:33
  13.7 8.4 %collective-permute-start.7 = (s32[32,128]{1,0:T(8,128)S(1)}, s32[32,128]{1,0:T(8,128)S(1)}, u32[]{:S(2)}, u32[]{:S(2)}) collective-permute-start(s32[32,128]{1,0:T(8,128)S(1)} %pad_add_fusion), channel_id=1, source_target_pairs={{0,4},{4,0},{8,12},{12,8},{16,20},{20,16},{24,28},{28,24},{1,5},{5... | collective-permute-start | bytes 49160 | tf_op jit(solution)/shard_map/ppermute | solution.py:33
  14.6 10.2 %collective-permute-start.4 = (bf16[8,128,128]{2,1,0:T(8,128)(2,1)S(1)}, bf16[8,128,128]{2,1,0:T(8,128)(2,1)S(1)}, u32[]{:S(2)}, u32[]{:S(2)}) collective-permute-start(bf16[8,128,128]{2,1,0:T(8,128)(2,1)S(1)} %get-tuple-element.82), channel_id=1, source_target_pairs={{0,8},{4,12},{8,0},{12,4},{16,24},{20,28},{24,16},{28,20},{1,9},{5... | collective-permute-start | bytes 786440 | tf_op jit(solution)/shard_map/ppermute | solution.py:33
  16.5 14.0 %collective-permute-start.5 = (bf16[8,128,128]{2,1,0:T(8,128)(2,1)S(1)}, bf16[8,128,128]{2,1,0:T(8,128)(2,1)S(1)}, u32[]{:S(2)}, u32[]{:S(2)}) collective-permute-start(bf16[8,128,128]{2,1,0:T(8,128)(2,1)S(1)} %get-tuple-element.83), channel_id=1, source_target_pairs={{0,16},{4,20},{8,24},{12,28},{16,0},{20,4},{24,8},{28,12},{1,17},{... | collective-permute-start | bytes 786440 | tf_op jit(solution)/shard_map/ppermute | solution.py:33
  18.1 12.5 %collective-permute-start.6 = (bf16[8,128,128]{2,1,0:T(8,128)(2,1)S(1)}, bf16[8,128,128]{2,1,0:T(8,128)(2,1)S(1)}, u32[]{:S(2)}, u32[]{:S(2)}) collective-permute-start(bf16[8,128,128]{2,1,0:T(8,128)(2,1)S(1)} %get-tuple-element.84), channel_id=1, source_target_pairs={{0,24},{4,28},{8,16},{12,20},{16,8},{20,12},{24,0},{28,4},{1,25},{... | collective-permute-start | bytes 786440 | tf_op jit(solution)/shard_map/ppermute | solution.py:33
  18.1 18.6 %collective-permute-start.11 = (bf16[128,512]{1,0:T(8,128)(2,1)S(1)}, bf16[128,512]{1,0:T(8,128)(2,1)S(1)}, u32[]{:S(2)}, u32[]{:S(2)}) collective-permute-start(bf16[128,512]{1,0:T(8,128)(2,1)S(1)} %get-tuple-element.94), channel_id=1, source_target_pairs={{0,1},{1,0},{2,3},{3,2},{4,5},{5,4},{6,7},{7,6},{8,9},{9,8},{10,11... | collective-permute-start | bytes 393224 | tf_op jit(solution)/shard_map/ppermute | solution.py:33
  22.1 14.8 %collective-permute-start.12 = (bf16[128,512]{1,0:T(8,128)(2,1)S(1)}, bf16[128,512]{1,0:T(8,128)(2,1)S(1)}, u32[]{:S(2)}, u32[]{:S(2)}) collective-permute-start(bf16[128,512]{1,0:T(8,128)(2,1)S(1)} %get-tuple-element.95), channel_id=1, source_target_pairs={{0,2},{1,3},{2,0},{3,1},{4,6},{5,7},{6,4},{7,5},{8,10},{9,11},{10,... | collective-permute-start | bytes 393224 | tf_op jit(solution)/shard_map/ppermute | solution.py:33
  24.8 12.1 %collective-permute-start.13 = (bf16[128,512]{1,0:T(8,128)(2,1)S(1)}, bf16[128,512]{1,0:T(8,128)(2,1)S(1)}, u32[]{:S(2)}, u32[]{:S(2)}) collective-permute-start(bf16[128,512]{1,0:T(8,128)(2,1)S(1)} %get-tuple-element.96), channel_id=1, source_target_pairs={{0,3},{1,2},{2,1},{3,0},{4,7},{5,6},{6,5},{7,4},{8,11},{9,10},{10,... | collective-permute-start | bytes 393224 | tf_op jit(solution)/shard_map/ppermute | solution.py:33
  34.1 12.9 %collective-permute-start.9 = (bf16[128,512]{1,0:T(8,128)(2,1)S(1)}, bf16[128,512]{1,0:T(8,128)(2,1)S(1)}, u32[]{:S(2)}, u32[]{:S(2)}) collective-permute-start(bf16[128,512]{1,0:T(8,128)(2,1)S(1)} %get-tuple-element.91), channel_id=1, source_target_pairs={{0,2},{1,3},{2,0},{3,1},{4,6},{5,7},{6,4},{7,5},{8,10},{9,11},{10,... | collective-permute-start | bytes 393224 | tf_op jit(solution)/shard_map/ppermute | solution.py:33
  36.7 10.3 %collective-permute-start.10 = (bf16[128,512]{1,0:T(8,128)(2,1)S(1)}, bf16[128,512]{1,0:T(8,128)(2,1)S(1)}, u32[]{:S(2)}, u32[]{:S(2)}) collective-permute-start(bf16[128,512]{1,0:T(8,128)(2,1)S(1)} %get-tuple-element.92), channel_id=1, source_target_pairs={{0,3},{1,2},{2,1},{3,0},{4,7},{5,6},{6,5},{7,4},{8,11},{9,10},{10,... | collective-permute-start | bytes 393224 | tf_op jit(solution)/shard_map/ppermute | solution.py:33
  49.7 8.7 %collective-permute-start.14 = (bf16[128,512]{1,0:T(8,128)(2,1)S(1)}, bf16[128,512]{1,0:T(8,128)(2,1)S(1)}, u32[]{:S(2)}, u32[]{:S(2)}) collective-permute-start(bf16[128,512]{1,0:T(8,128)(2,1)S(1)} %get-tuple-element.102), channel_id=1, source_target_pairs={{0,1},{1,0},{2,3},{3,2},{4,5},{5,4},{6,7},{7,6},{8,9},{9,8},{10,11... | collective-permute-start | bytes 393224 | tf_op jit(solution)/shard_map/ppermute | solution.py:33
  52.1 12.9 %collective-permute-start.15 = (bf16[128,512]{1,0:T(8,128)(2,1)S(1)}, bf16[128,512]{1,0:T(8,128)(2,1)S(1)}, u32[]{:S(2)}, u32[]{:S(2)}) collective-permute-start(bf16[128,512]{1,0:T(8,128)(2,1)S(1)} %get-tuple-element.103), channel_id=1, source_target_pairs={{0,2},{1,3},{2,0},{3,1},{4,6},{5,7},{6,4},{7,5},{8,10},{9,11},{10,... | collective-permute-start | bytes 393224 | tf_op jit(solution)/shard_map/ppermute | solution.py:33
  53.2 11.8 %collective-permute-start.16 = (bf16[128,512]{1,0:T(8,128)(2,1)S(1)}, bf16[128,512]{1,0:T(8,128)(2,1)S(1)}, u32[]{:S(2)}, u32[]{:S(2)}) collective-permute-start(bf16[128,512]{1,0:T(8,128)(2,1)S(1)} %get-tuple-element.104), channel_id=1, source_target_pairs={{0,3},{1,2},{2,1},{3,0},{4,7},{5,6},{6,5},{7,4},{8,11},{9,10},{10,... | collective-permute-start | bytes 393224 | tf_op jit(solution)/shard_map/ppermute | solution.py:33
  54.6 10.4 %collective-permute-start.18 = (bf16[64,512]{1,0:T(8,128)(2,1)S(1)}, bf16[64,512]{1,0:T(8,128)(2,1)S(1)}, u32[]{:S(2)}, u32[]{:S(2)}) collective-permute-start(bf16[64,512]{1,0:T(8,128)(2,1)S(1)} %get-tuple-element.110), channel_id=1, source_target_pairs={{0,8},{4,12},{8,0},{12,4},{16,24},{20,28},{24,16},{28,20},{1,9},{5... | collective-permute-start | bytes 196616 | tf_op jit(solution)/shard_map/ppermute | solution.py:33
  57.0 8.0 %collective-permute-start.19 = (bf16[64,512]{1,0:T(8,128)(2,1)S(1)}, bf16[64,512]{1,0:T(8,128)(2,1)S(1)}, u32[]{:S(2)}, u32[]{:S(2)}) collective-permute-start(bf16[64,512]{1,0:T(8,128)(2,1)S(1)} %get-tuple-element.111), channel_id=1, source_target_pairs={{0,16},{4,20},{8,24},{12,28},{16,0},{20,4},{24,8},{28,12},{1,17},{... | collective-permute-start | bytes 196616 | tf_op jit(solution)/shard_map/ppermute | solution.py:33
  65.9 9.6 %collective-permute-start.21 = (bf16[144,512]{1,0:T(8,128)(2,1)S(1)}, bf16[144,512]{1,0:T(8,128)(2,1)S(1)}, u32[]{:S(2)}, u32[]{:S(2)}) collective-permute-start(bf16[144,512]{1,0:T(8,128)(2,1)S(1)} %get-tuple-element.119), channel_id=1, source_target_pairs={{0,1},{1,0},{2,3},{3,2},{4,5},{5,4},{6,7},{7,6},{8,9},{9,8},{10,11... | collective-permute-start | bytes 442376 | tf_op jit(solution)/shard_map/ppermute | solution.py:33
  70.7 17.2 %collective-permute-start.24 = (bf16[8,128,128]{2,1,0:T(8,128)(2,1)S(1)}, bf16[8,128,128]{2,1,0:T(8,128)(2,1)S(1)}, u32[]{:S(2)}, u32[]{:S(2)}) collective-permute-start(bf16[8,128,128]{2,1,0:T(8,128)(2,1)S(1)} %get-tuple-element.123), channel_id=1, source_target_pairs={{0,8},{4,12},{8,0},{12,4},{16,24},{20,28},{24,16},{28,20},{1,9},{5... | collective-permute-start | bytes 786440 | tf_op jit(solution)/shard_map/ppermute | solution.py:33
  72.9 15.0 %collective-permute-start.25 = (bf16[8,128,128]{2,1,0:T(8,128)(2,1)S(1)}, bf16[8,128,128]{2,1,0:T(8,128)(2,1)S(1)}, u32[]{:S(2)}, u32[]{:S(2)}) collective-permute-start(bf16[8,128,128]{2,1,0:T(8,128)(2,1)S(1)} %get-tuple-element.124), channel_id=1, source_target_pairs={{0,16},{4,20},{8,24},{12,28},{16,0},{20,4},{24,8},{28,12},{1,17},{... | collective-permute-start | bytes 786440 | tf_op jit(solution)/shard_map/ppermute | solution.py:33
  74.3 13.6 %collective-permute-start.26 = (bf16[8,128,128]{2,1,0:T(8,128)(2,1)S(1)}, bf16[8,128,128]{2,1,0:T(8,128)(2,1)S(1)}, u32[]{:S(2)}, u32[]{:S(2)}) collective-permute-start(bf16[8,128,128]{2,1,0:T(8,128)(2,1)S(1)} %get-tuple-element.125), channel_id=1, source_target_pairs={{0,24},{4,28},{8,16},{12,20},{16,8},{20,12},{24,0},{28,4},{1,25},{... | collective-permute-start | bytes 786440 | tf_op jit(solution)/shard_map/ppermute | solution.py:33
  74.4 13.4 %collective-permute-start.22 = (bf16[144,512]{1,0:T(8,128)(2,1)S(1)}, bf16[144,512]{1,0:T(8,128)(2,1)S(1)}, u32[]{:S(2)}, u32[]{:S(2)}) collective-permute-start(bf16[144,512]{1,0:T(8,128)(2,1)S(1)} %get-tuple-element.120), channel_id=1, source_target_pairs={{0,2},{1,3},{2,0},{3,1},{4,6},{5,7},{6,4},{7,5},{8,10},{9,11},{10,... | collective-permute-start | bytes 442376 | tf_op jit(solution)/shard_map/ppermute | solution.py:33
  75.4 12.5 %collective-permute-start.23 = (bf16[144,512]{1,0:T(8,128)(2,1)S(1)}, bf16[144,512]{1,0:T(8,128)(2,1)S(1)}, u32[]{:S(2)}, u32[]{:S(2)}) collective-permute-start(bf16[144,512]{1,0:T(8,128)(2,1)S(1)} %get-tuple-element.121), channel_id=1, source_target_pairs={{0,3},{1,2},{2,1},{3,0},{4,7},{5,6},{6,5},{7,4},{8,11},{9,10},{10,... | collective-permute-start | bytes 442376 | tf_op jit(solution)/shard_map/ppermute | solution.py:33
  88.0 10.5 %collective-permute-start.28 = (bf16[12,128,128]{2,1,0:T(8,128)(2,1)S(1)}, bf16[12,128,128]{2,1,0:T(8,128)(2,1)S(1)}, u32[]{:S(2)}, u32[]{:S(2)}) collective-permute-start(bf16[12,128,128]{2,1,0:T(8,128)(2,1)S(1)} %shard_map.110), channel_id=1, source_target_pairs={{0,4},{4,0},{8,12},{12,8},{16,20},{20,16},{24,28},{28,24},{1,5},{5... | collective-permute-start | bytes 1179656 | tf_op jit(solution)/shard_map/ppermute | solution.py:33
  88.1 10.3 %collective-permute-start.27 = (bf16[4,128,128]{2,1,0:T(8,128)(2,1)S(1)}, bf16[4,128,128]{2,1,0:T(8,128)(2,1)S(1)}, u32[]{:S(2)}, u32[]{:S(2)}) collective-permute-start(bf16[4,128,128]{2,1,0:T(8,128)(2,1)S(1)} %get-tuple-element.117), channel_id=1, source_target_pairs={{0,4},{4,0},{8,12},{12,8},{16,20},{20,16},{24,28},{28,24},{1,5},{5... | collective-permute-start | bytes 393224 | tf_op jit(solution)/shard_map/ppermute | solution.py:33
  (15 other events, 96.0 us)

commit v3 on v2

--- a/solution.py
+++ b/solution.py
@@ -215,22 +215,18 @@
             out[:, i * TILE : (i + 1) * TILE] = acc_ref[block * per + i].astype(BF)
 
 
-def weight_kernel(me_ref, s_ref, z_ref, own_ref, sib_ref):
-    n_chip, per, _ = own_ref.shape
-    z = z_ref[...]
-    for q, out in enumerate((own_ref, sib_ref)):
-        core = (me_ref[0] & 1) ^ q
-        for c in range(n_chip):
-            rows = pl.ds(pl.multiple_of((2 * c + core) * per, per), per)
-            out[c] = lax.dot_general(
-                s_ref[rows, :], z, (((1,), (1,)), ((), ())), preferred_element_type=F32
-            ).astype(out.dtype)
-
-
-def weight_pair_kernel(me_ref, own_ref, got_ref, keep_ref, *outs):
+def weight_kernel(me_ref, own_ref, sib_ref, keep_ref, *outs):
+    n_f = own_ref.shape[0] - keep_ref.shape[1]
+    per = keep_ref.shape[0]
+    core = me_ref[0] & 1
+    pairs = [(r, r[n_f:, :]) for r in (own_ref, sib_ref)]
     for e in range(len(outs) + 1):
-        c = (me_ref[0] >> 1) ^ e
-        total = own_ref[c] + got_ref[c].astype(F32)
+        row = ((((me_ref[0] >> 1) ^ e) << 1) + core) * per
+        rows = pl.ds(pl.multiple_of(row, per), per)
+        total = sum(
+            lax.dot_general(r[rows, :], z, (((1,), (1,)), ((), ())), preferred_element_type=F32)
+            for r, z in pairs
+        )
         if e == 0:
             keep_ref[...] = total
         else:
@@ -297,8 +293,10 @@
 def dense_kernel(n_col, me_ref, wt_ref, w_ref, *refs):
     s_refs, g_refs = refs[:n_col], refs[n_col : 2 * n_col]
     o_refs, y_refs = refs[2 * n_col : 3 * n_col], refs[3 * n_col : 4 * n_col]
-    z_ref, s_ref = refs[4 * n_col], refs[4 * n_col + 1]
+    sz_ref = refs[4 * n_col]
     f_loc = s_refs[0].shape[0]
+    n_f = f_loc * n_col
+    s_ref, z_ref = sz_ref.at[pl.ds(0, n_f)], sz_ref.at[pl.ds(n_f, sz_ref.shape[0] - n_f)]
     me = me_ref[0]
     for k in range(n_col):
         s_ref[pl.ds(pl.multiple_of((me ^ k) * f_loc, f_loc), f_loc), :] = s_refs[k][...]
@@ -330,6 +328,10 @@
         wide_ref[:, pl.ds(at, width)] = r[: wide_ref.shape[0], :]
 
 
+def turn_kernel(x_ref, out_ref):
+    out_ref[...] = x_ref[...].T
+
+
 def split_kernel(me_ref, x_ref, *outs):
     width = outs[0].shape[1]
     for k, out in enumerate(outs):
@@ -390,9 +392,29 @@
     tile_flops = 2 * f_loc * TILE * TILE
     tile_bytes = slots * TILE * TILE * 2
 
-    tile_values, mer, mec, weight_t = lax.optimization_barrier(
-        (tile_values, mer, mec, weight.T)
-    )
+    def over_chips(x):
+        return swap(x, "row", n_row, 1)
+
+    sib_feat = over_chips(features)
+    need = call(
+        functools.partial(need_kernel, n_row, row_tiles),
+        sds((n_row, 128), jnp.int32),
+        [],
+        (tile_count,),
+        (tile_cols,),
+    )
+    mer, mec, need = lax.optimization_barrier((mer, mec, need))
+    needs = [need] + [swap(need, "row", n_row, 2 * e) for e in range(1, n_chip)]
+    length = -(-(slots + n_chip * per + 2 * UNROLL) // 128) * 128
+    x_near = call(
+        pack_kernel,
+        sds((2 * row_tiles + 1, f_loc, TILE), BF),
+        [],
+        (mer,),
+        (features, sib_feat),
+        nbytes=f_loc * nodes * 8,
+    )
+    tile_values, mer, mec = lax.optimization_barrier((tile_values, mer, mec))
     tile_values = pl.pallas_call(
         load_kernel,
         out_shape=sds(tile_values.shape, BF),
@@ -402,35 +424,30 @@
         compiler_params=pltpu.CompilerParams(vmem_limit_bytes=24 << 20),
         cost_estimate=pl.CostEstimate(flops=0, bytes_accessed=tile_bytes, transcendentals=0),
     )(pltpu.with_memory_space_constraint(tile_values, pltpu.HBM))
-
-    def over_chips(x):
-        return swap(x, "row", n_row, 1)
-
-    sib_feat = over_chips(features)
-    need = call(
-        functools.partial(need_kernel, n_row, row_tiles),
-        sds((n_row, 128), jnp.int32),
-        [],
-        (tile_count,),
-        (tile_cols,),
-    )
-    needs = [need] + [swap(need, "row", n_row, 2 * e) for e in range(1, n_chip)]
-    length = -(-(slots + n_chip * per + 2 * UNROLL) // 128) * 128
+    needs, x_near, tile_values = lax.optimization_barrier((needs, x_near, tile_values))
+    sends = call(
+        functools.partial(send_kernel, n_chip, row_tiles),
+        [sds((per, f_loc, TILE), BF)] * (n_chip - 1),
+        [],
+        (mer, *needs[1:]),
+        (x_near,),
+        nbytes=4 * n_chip * per * f_loc * TILE,
+    )
+    got = [swap(x, "row", n_row, 2 * (e + 1)) for e, x in enumerate(sends)]
+    needs, sends, lists_in, out_grad = lax.optimization_barrier(
+        (needs, sends, (tile_cols, tile_rows), out_grad)
+    )
     lists = call(
         functools.partial(lists_kernel, n_row, row_tiles),
         sds((8, length), jnp.int32),
         [],
         (tile_count, mer),
-        (tile_cols, tile_rows),
-    )
-    x_near = call(
-        pack_kernel,
-        sds((2 * row_tiles + 1, f_loc, TILE), BF),
-        [],
-        (mer,),
-        (features, sib_feat),
-        nbytes=f_loc * nodes * 8,
-    )
+        lists_in,
+    )
+    table = jnp.concatenate(needs, axis=0)
+    table = jnp.concatenate([table, over_chips(table)], axis=0)
+    got, table = lax.optimization_barrier((got, table))
+
     g_parts = call(
         split_kernel,
         [sds((h_loc, part), BF)] * n_col,
@@ -439,22 +456,6 @@
         (out_grad,),
         nbytes=h_loc * nodes * 4,
     )
-    needs, x_near, lists, tile_values, g_parts = lax.optimization_barrier(
-        (needs, x_near, lists, tile_values, g_parts)
-    )
-    sends = call(
-        functools.partial(send_kernel, n_chip, row_tiles),
-        [sds((per, f_loc, TILE), BF)] * (n_chip - 1),
-        [],
-        (mer, *needs[1:]),
-        (x_near,),
-        nbytes=4 * n_chip * per * f_loc * TILE,
-    )
-    got = [swap(x, "row", n_row, 2 * (e + 1)) for e, x in enumerate(sends)]
-    table = jnp.concatenate(needs, axis=0)
-    table = jnp.concatenate([table, over_chips(table)], axis=0)
-    got, table = lax.optimization_barrier((got, table))
-
     grads = [g if k == 0 else swap(g, "col", n_col, k) for k, g in enumerate(g_parts)]
 
     acc = call(
@@ -482,37 +483,31 @@
     )
     s_got = [s if k == 0 else swap(s, "col", n_col, k) for k, s in enumerate(s_parts)]
 
+    weight_t, _ = lax.optimization_barrier((weight, s_parts[0]))
+    weight_t = call(turn_kernel, sds((n_h, n_f), BF), [], (), (weight_t,), nbytes=n_f * n_h * 4)
     res = call(
         functools.partial(dense_kernel, n_col),
         [sds((h_loc, part), BF)] * n_col
         + [sds((f_loc, part), BF)] * n_col
-        + [sds((n_h, part), BF), sds((n_f, part), BF)],
+        + [sds((n_f + n_h, part), BF)],
         [],
         (mec,),
         (weight_t, weight, *s_got, *grads),
         flops=4 * n_f * n_h * part,
         nbytes=n_f * part * 8,
     )
-    o_parts, y_parts, z_all, s_all = res[:n_col], res[n_col : 2 * n_col], res[-2], res[-1]
+    o_parts, y_parts, sz = res[:n_col], res[n_col : 2 * n_col], res[-1]
     y_got = [y if k == 0 else swap(y, "col", n_col, k) for k, y in enumerate(y_parts)]
 
     w_rows = n_f // n_row
-    w_own, w_sib = call(
+    w_parts = call(
         weight_kernel,
-        [sds((n_chip, w_rows, n_h), F32), sds((n_chip, w_rows, n_h), BF)],
+        [sds((w_rows, n_h), F32)] + [sds((w_rows, n_h), BF)] * (n_chip - 1),
         [],
         (mer,),
-        (s_all, z_all),
+        (sz, over_chips(sz)),
         flops=2 * n_f * n_h * part,
         nbytes=n_f * part * 8,
-    )
-    w_parts = call(
-        weight_pair_kernel,
-        [sds((w_rows, n_h), F32)] + [sds((w_rows, n_h), BF)] * (n_chip - 1),
-        [],
-        (mer,),
-        (w_own, over_chips(w_sib)),
-        nbytes=n_f * n_h * 4,
     )
     w_chips = [w if e == 0 else swap(w, "row", n_row, 2 * e) for e, w in enumerate(w_parts)]
     more = -(-(w_rows * h_loc // part) // 16) * 16
@@ -586,14 +581,6 @@
         pair_kernel, sds((2, w_rows, h_loc), F32), [], (mer,), (w_mine, over_chips(w_mine))
     )
     w_chips = [w_pair] + [swap(w_pair, "row", n_row, 2 * e) for e in range(1, n_chip)]
-    weight_grad = call(
-        weight_place_kernel,
-        sds((n_f, h_loc), F32),
-        [],
-        (mer,),
-        tuple(w_chips),
-        nbytes=n_f * h_loc * 8,
-    )
 
     input_grad = call(
         functools.partial(join_kernel, n_chip),
@@ -602,6 +589,15 @@
         (mer, table),
         (acc_b, from_sib, over_chips(passed), *returned),
         nbytes=f_loc * nodes * 8,
+    )
+    w_chips, input_grad = lax.optimization_barrier((w_chips, input_grad))
+    weight_grad = call(
+        weight_place_kernel,
+        sds((n_f, h_loc), F32),
+        [],
+        (mer,),
+        tuple(w_chips),
+        nbytes=n_f * h_loc * 8,
     )
     output = call(
         place_kernel, sds((h_loc, nodes), BF), [], (mec,), (o_parts[0], *mixed[1:]), nbytes=h_loc * nodes * 4

time: 100 us -> 95.8 us (0.958); the launches traced: 101 us -> 95.2 us
  waiting for transfers between devices: 31.3 us -> 27.6 us
  starting transfers between devices: 44.1 us -> 42.5 us
  local copies, waits for them, and re-layouts: 1.97 us -> 0.72 us
  Pallas kernels: 21.7 us -> 22.9 us
    ppermute x33, waiting for transfers between devices: 31.3 us -> 27.6 us  [swap(): return lax.ppermute(x, axis, [(i, i ^ k) for i in range(n)])]
    ppermute x33, starting transfers between devices: 44.1 us -> 42.5 us  [swap(): return lax.ppermute(x, axis, [(i, i ^ k) for i in range(n)])]
    pallas_call x19, Pallas kernels: 18.1 us -> 19.4 us  [call(): pl.pallas_call(kernel, out_shape=outs, in_specs=[SM] * len(smem) + [VM] *...]
    unnamed x17 -> x16, local copies, waits for them, and re-layouts: 1.97 us -> 0.71 us
  transfers between devices with their start and end apart: 33 -> 33, of which waited for: 10 -> 8; matrix products, arithmetic and copies ran while one was open for 1% -> 0% of each run, Pallas kernels for 16% -> 20%
where the time goes in v3:
time: 95.8 us; the launch traced here: 95.2 us
  starting transfers between devices  42.5 us (44%)
  waiting for transfers between devices  27.6 us (29%)
  Pallas kernels  22.9 us (24%)
  between operations  1.59 us (2%)
    ppermute x33, starting transfers between devices, swap(): return lax.ppermute(x, axis, [(i, i ^ k) for i in range(n)])  42.5 us
    ppermute x33, waiting for transfers between devices, swap(): return lax.ppermute(x, axis, [(i, i ^ k) for i in range(n)])  27.6 us
    pallas_call x19, Pallas kernels, call(): pl.pallas_call(kernel, out_shape=outs, in_specs=[SM] * len(smem) + [VM] *...  19.4 us
    pallas_call x1, Pallas kernels, shards(): pl.pallas_call(load_kernel, out_shape=sds(tile_values.shape, BF), in_spec...  3.47 us
  transfers between devices with their start and end apart: 33, of which 8 were waited for; matrix products, arithmetic and copies ran while one was open for 0% of the time, Pallas kernels for 20%

profile of v3, /device:TPU:0, one launch (start us, length us, event | category | flops | bytes accessed | tf_op | source)
XLA Modules:
  0.0 95.2 jit_solution(9245307902406411104)
XLA Ops:
  2.8 3.5 %collective-permute-start.2 = (s32[8,128]{1,0:T(8,128)S(1)}, s32[8,128]{1,0:T(8,128)S(1)}, u32[]{:S(2)}, u32[]{:S(2)}) collective-permute-start(s32[8,128]{1,0:T(8,128)S(1)} %shard_map.94), channel_id=1, source_target_pairs={{0,24},{4,28},{8,16},{12,20},{16,8},{20,12},{24,0},{28,4},{1,25},{... | collective-permute-start | bytes 12296 | tf_op jit(solution)/shard_map/ppermute | solution.py:33
  7.0 3.5 %shard_map.96.tiles_ref = bf16[256,128,128]{2,1,0:T(8,128)(2,1)S(1)} custom-call(bf16[256,128,128]{2,1,0:T(8,128)(2,1)} %in_ref), custom_call_target="tpu_custom_call" | custom-call | bytes 8388608 | tf_op jit(solution)/shard_map/pallas_call | solution.py:418
  11.5 2.0 %collective-permute-start.4 = (bf16[8,128,128]{2,1,0:T(8,128)(2,1)S(1)}, bf16[8,128,128]{2,1,0:T(8,128)(2,1)S(1)}, u32[]{:S(2)}, u32[]{:S(2)}) collective-permute-start(bf16[8,128,128]{2,1,0:T(8,128)(2,1)S(1)} %get-tuple-element.86), channel_id=1, source_target_pairs={{0,8},{4,12},{8,0},{12,4},{16,24},{20,28},{24,16},{28,20},{1,9},{5... | collective-permute-start | bytes 786440 | tf_op jit(solution)/shard_map/ppermute | solution.py:33
  15.2 2.0 %collective-permute-start.11 = (bf16[128,512]{1,0:T(8,128)(2,1)S(1)}, bf16[128,512]{1,0:T(8,128)(2,1)S(1)}, u32[]{:S(2)}, u32[]{:S(2)}) collective-permute-start(bf16[128,512]{1,0:T(8,128)(2,1)S(1)} %get-tuple-element.106), channel_id=1, source_target_pairs={{0,1},{1,0},{2,3},{3,2},{4,5},{5,4},{6,7},{7,6},{8,9},{9,8},{10,11... | collective-permute-start | bytes 393224 | tf_op jit(solution)/shard_map/ppermute | solution.py:33
  17.2 1.5 %shard_map.98.list_ref = s32[8,384]{1,0:T(8,128)S(1)} custom-call(s32[1]{0:T(128)S(6)} %copy.14.count_ref, s32[1]{0:T(128)} %bitcast.me_ref.mer_ref, s32[1,256]{1,0:T(1,128)S(1)} %copy-done.4, s32[1,256]{1,0:T(1,128)S(1)} %copy-done.5), custom_call_target="tpu_custom_call" | custom-call | tf_op jit(solution)/shard_map/pallas_call | solution.py:21
  18.8 2.2 %shard_map.99.refs_3_ = f32[16,128,128]{2,1,0:T(8,128)S(1)} custom-call(s32[8,384]{1,0:T(8,128)S(1)} %shard_map.98.list_ref, bf16[256,128,128]{2,1,0:T(8,128)(2,1)S(1)} %shard_map.96.tiles_ref, bf16[33,128,128]{2,1,0:T(8,128)(2,1)S(1)} %shard_map.95.refs_3_.x_ref), custom_call_target="tpu_custom_call" | custom-call | flops 1073741824 | bytes 8388608 | tf_op jit(solution)/shard_map/pallas_call | solution.py:21
  21.0 2.7 %collective-permute-start.12 = (bf16[128,512]{1,0:T(8,128)(2,1)S(1)}, bf16[128,512]{1,0:T(8,128)(2,1)S(1)}, u32[]{:S(2)}, u32[]{:S(2)}) collective-permute-start(bf16[128,512]{1,0:T(8,128)(2,1)S(1)} %get-tuple-element.107), channel_id=1, source_target_pairs={{0,2},{1,3},{2,0},{3,1},{4,6},{5,7},{6,4},{7,5},{8,10},{9,11},{10,... | collective-permute-start | bytes 393224 | tf_op jit(solution)/shard_map/ppermute | solution.py:33
  24.8 1.9 %collective-permute-done.5.refs_1_ = bf16[8,128,128]{2,1,0:T(8,128)(2,1)S(1)} collective-permute-done((bf16[8,128,128]{2,1,0:T(8,128)(2,1)S(1)}, bf16[8,128,128]{2,1,0:T(8,128)(2,1)S(1)}, u32[]{:S(2)}, u32[]{:S(2)}) %collective-permute-start.5) | collective-permute-done | bytes 262176 | tf_op jit(solution)/shard_map/ppermute | solution.py:33
  26.7 2.4 %shard_map.100 = (bf16[128,512]{1,0:T(8,128)(2,1)S(1)}, bf16[128,512]{1,0:T(8,128)(2,1)S(1)}, bf16[128,512]{1,0:T(8,128)(2,1)S(1)}, bf16[128,512]{1,0:T(8,128)(2,1)S(1)}) custom-call(s32[8,384]{1,0:T(8,128)S(1)} %shard_map.98.list_ref, s32[1]{0:T(128)} %bitcast.1.me_ref.mec_ref, bf16[256,128,128]{2,1,0:T(8,128)(2,1)S(1)} %shard_map.96.tiles_ref, ...), custom_call_target="tpu_custom_call" | custom-call | flops 1073741824 | bytes 8388608 | tf_op jit(solution)/shard_map/pallas_call | solution.py:21
  29.0 1.6 %collective-permute-start.8 = (bf16[128,512]{1,0:T(8,128)(2,1)S(1)}, bf16[128,512]{1,0:T(8,128)(2,1)S(1)}, u32[]{:S(2)}, u32[]{:S(2)}) collective-permute-start(bf16[128,512]{1,0:T(8,128)(2,1)S(1)} %get-tuple-element.101), channel_id=1, source_target_pairs={{0,1},{1,0},{2,3},{3,2},{4,5},{5,4},{6,7},{7,6},{8,9},{9,8},{10,11... | collective-permute-start | bytes 393224 | tf_op jit(solution)/shard_map/ppermute | solution.py:33
  30.7 2.6 %collective-permute-start.9 = (bf16[128,512]{1,0:T(8,128)(2,1)S(1)}, bf16[128,512]{1,0:T(8,128)(2,1)S(1)}, u32[]{:S(2)}, u32[]{:S(2)}) collective-permute-start(bf16[128,512]{1,0:T(8,128)(2,1)S(1)} %get-tuple-element.102), channel_id=1, source_target_pairs={{0,2},{1,3},{2,0},{3,1},{4,6},{5,7},{6,4},{7,5},{8,10},{9,11},{10,... | collective-permute-start | bytes 393224 | tf_op jit(solution)/shard_map/ppermute | solution.py:33
  33.7 2.6 %collective-permute-done.8.refs_1_ = bf16[128,512]{1,0:T(8,128)(2,1)S(1)} collective-permute-done((bf16[128,512]{1,0:T(8,128)(2,1)S(1)}, bf16[128,512]{1,0:T(8,128)(2,1)S(1)}, u32[]{:S(2)}, u32[]{:S(2)}) %collective-permute-start.8) | collective-permute-done | bytes 131104 | tf_op jit(solution)/shard_map/ppermute | solution.py:33
  36.3 8.1 %collective-permute-done.9.refs_2_ = bf16[128,512]{1,0:T(8,128)(2,1)S(1)} collective-permute-done((bf16[128,512]{1,0:T(8,128)(2,1)S(1)}, bf16[128,512]{1,0:T(8,128)(2,1)S(1)}, u32[]{:S(2)}, u32[]{:S(2)}) %collective-permute-start.9) | collective-permute-done | bytes 131104 | tf_op jit(solution)/shard_map/ppermute | solution.py:33
  45.7 3.4 %collective-permute-start.14 = (bf16[128,512]{1,0:T(8,128)(2,1)S(1)}, bf16[128,512]{1,0:T(8,128)(2,1)S(1)}, u32[]{:S(2)}, u32[]{:S(2)}) collective-permute-start(bf16[128,512]{1,0:T(8,128)(2,1)S(1)} %get-tuple-element.114), channel_id=1, source_target_pairs={{0,1},{1,0},{2,3},{3,2},{4,5},{5,4},{6,7},{7,6},{8,9},{9,8},{10,11... | collective-permute-start | bytes 393224 | tf_op jit(solution)/shard_map/ppermute | solution.py:33
  54.3 2.5 %collective-permute-start.19 = (bf16[64,512]{1,0:T(8,128)(2,1)S(1)}, bf16[64,512]{1,0:T(8,128)(2,1)S(1)}, u32[]{:S(2)}, u32[]{:S(2)}) collective-permute-start(bf16[64,512]{1,0:T(8,128)(2,1)S(1)} %get-tuple-element.120), channel_id=1, source_target_pairs={{0,16},{4,20},{8,24},{12,28},{16,0},{20,4},{24,8},{28,12},{1,17},{... | collective-permute-start | bytes 196616 | tf_op jit(solution)/shard_map/ppermute | solution.py:33
  57.9 4.1 %collective-permute-done.15.refs_2_ = bf16[128,512]{1,0:T(8,128)(2,1)S(1)} collective-permute-done((bf16[128,512]{1,0:T(8,128)(2,1)S(1)}, bf16[128,512]{1,0:T(8,128)(2,1)S(1)}, u32[]{:S(2)}, u32[]{:S(2)}) %collective-permute-start.15) | collective-permute-done | bytes 131104 | tf_op jit(solution)/shard_map/ppermute | solution.py:33
  62.8 2.5 %collective-permute-start.21 = (bf16[144,512]{1,0:T(8,128)(2,1)S(1)}, bf16[144,512]{1,0:T(8,128)(2,1)S(1)}, u32[]{:S(2)}, u32[]{:S(2)}) collective-permute-start(bf16[144,512]{1,0:T(8,128)(2,1)S(1)} %get-tuple-element.128), channel_id=1, source_target_pairs={{0,1},{1,0},{2,3},{3,2},{4,5},{5,4},{6,7},{7,6},{8,9},{9,8},{10,11... | collective-permute-start | bytes 442376 | tf_op jit(solution)/shard_map/ppermute | solution.py:33
  65.4 2.5 %shard_map.105 = (bf16[128,2048]{1,0:T(8,128)(2,1)S(1)}, bf16[4,128,128]{2,1,0:T(8,128)(2,1)S(1)}, bf16[8,128,128]{2,1,0:T(8,128)(2,1)S(1)}, bf16[8,128,128]{2,1,0:T(8,128)(2,1)S(1)}, bf16[8,128,128]{2,1,0:T(8,128)(2,1)S(1)}) custom-call(s32[8,384]{1,0:T(8,128)S(1)} %shard_map.98.list_ref, s32[1]{0:T(128)} %bitcast.1.me_ref.mec_ref, s32[1]{0:T(128)} %bitcast.me_ref.mer_ref, ...), custom_call_target="tpu_custom_call" | custom-call | flops 1073741824 | bytes 8388608 | tf_op jit(solution)/shard_map/pallas_call | solution.py:21
  69.2 2.4 %collective-permute-start.25 = (bf16[8,128,128]{2,1,0:T(8,128)(2,1)S(1)}, bf16[8,128,128]{2,1,0:T(8,128)(2,1)S(1)}, u32[]{:S(2)}, u32[]{:S(2)}) collective-permute-start(bf16[8,128,128]{2,1,0:T(8,128)(2,1)S(1)} %get-tuple-element.132), channel_id=1, source_target_pairs={{0,16},{4,20},{8,24},{12,28},{16,0},{20,4},{24,8},{28,12},{1,17},{... | collective-permute-start | bytes 786440 | tf_op jit(solution)/shard_map/ppermute | solution.py:33
  72.7 1.5 %collective-permute-start.23 = (bf16[144,512]{1,0:T(8,128)(2,1)S(1)}, bf16[144,512]{1,0:T(8,128)(2,1)S(1)}, u32[]{:S(2)}, u32[]{:S(2)}) collective-permute-start(bf16[144,512]{1,0:T(8,128)(2,1)S(1)} %get-tuple-element.130), channel_id=1, source_target_pairs={{0,3},{1,2},{2,1},{3,0},{4,7},{5,6},{6,5},{7,4},{8,11},{9,10},{10,... | collective-permute-start | bytes 442376 | tf_op jit(solution)/shard_map/ppermute | solution.py:33
  74.2 2.0 %shard_map.108.base_ref = f32[16,128,128]{2,1,0:T(8,128)S(1)} custom-call(s32[8,384]{1,0:T(8,128)S(1)} %shard_map.98.list_ref, bf16[256,128,128]{2,1,0:T(8,128)(2,1)S(1)} %shard_map.96.tiles_ref, bf16[128,2048]{1,0:T(8,128)(2,1)S(1)} %get-tuple-element.134.wide_ref), custom_call_target="tpu_custom_call" | custom-call | flops 1073741824 | bytes 8388608 | tf_op jit(solution)/shard_map/pallas_call | solution.py:21
  76.2 8.9 %collective-permute-done.22.refs_2_.refs_1_ = bf16[144,512]{1,0:T(8,128)(2,1)S(1)} collective-permute-done((bf16[144,512]{1,0:T(8,128)(2,1)S(1)}, bf16[144,512]{1,0:T(8,128)(2,1)S(1)}, u32[]{:S(2)}, u32[]{:S(2)}) %collective-permute-start.22) | collective-permute-done | bytes 147488 | tf_op jit(solution)/shard_map/ppermute | solution.py:33
  87.3 3.0 %collective-permute-start.30 = (f32[2,64,128]{2,1,0:T(8,128)S(1)}, f32[2,64,128]{2,1,0:T(8,128)S(1)}, u32[]{:S(2)}, u32[]{:S(2)}) collective-permute-start(f32[2,64,128]{2,1,0:T(8,128)S(1)} %shard_map.110.refs_0_), channel_id=1, source_target_pairs={{0,24},{4,28},{8,16},{12,20},{16,8},{20,12},{24,0},{28,4},{1,25},{... | collective-permute-start | bytes 196616 | tf_op jit(solution)/shard_map/ppermute | solution.py:33
  91.7 2.3 %shard_map.112 = bf16[128,2048]{1,0:T(8,128)(2,1)} custom-call(s32[1]{0:T(128)} %bitcast.me_ref.mer_ref, s32[64,128]{1,0:T(8,128)S(1)} %constant_dynamic-update-slice_fusion.table_ref, f32[16,128,128]{2,1,0:T(8,128)S(1)} %shard_map.108.base_ref, bf16[4,128,128]{2,1,0:T(8,128)(2,1)S(1)} %collective-permute-done.31.sib_ref, ...), custom_call_target="tpu_custom_call" | custom-call | bytes 2097152 | tf_op jit(solution)/shard_map/pallas_call | solution.py:21
  (80 shorter events, 22.0 us)
Async XLA Ops:
  0.6 9.8 %collective-permute-start.3 = (bf16[128,2048]{1,0:T(8,128)(2,1)}, bf16[128,2048]{1,0:T(8,128)(2,1)S(1)}, u32[]{:S(2)}, u32[]{:S(2)}) collective-permute-start(bf16[128,2048]{1,0:T(8,128)(2,1)} %feat_ref.1), channel_id=1, source_target_pairs={{0,4},{4,0},{8,12},{12,8},{16,20},{20,16},{24,28},{28,24},{1,5},{5... | collective-permute-start | bytes 1572872 | tf_op jit(solution)/shard_map/ppermute | solution.py:33
  2.8 7.9 %collective-permute-start.2 = (s32[8,128]{1,0:T(8,128)S(1)}, s32[8,128]{1,0:T(8,128)S(1)}, u32[]{:S(2)}, u32[]{:S(2)}) collective-permute-start(s32[8,128]{1,0:T(8,128)S(1)} %shard_map.94), channel_id=1, source_target_pairs={{0,24},{4,28},{8,16},{12,20},{16,8},{20,12},{24,0},{28,4},{1,25},{... | collective-permute-start | bytes 12296 | tf_op jit(solution)/shard_map/ppermute | solution.py:33
  11.5 12.2 %collective-permute-start.4 = (bf16[8,128,128]{2,1,0:T(8,128)(2,1)S(1)}, bf16[8,128,128]{2,1,0:T(8,128)(2,1)S(1)}, u32[]{:S(2)}, u32[]{:S(2)}) collective-permute-start(bf16[8,128,128]{2,1,0:T(8,128)(2,1)S(1)} %get-tuple-element.86), channel_id=1, source_target_pairs={{0,8},{4,12},{8,0},{12,4},{16,24},{20,28},{24,16},{28,20},{1,9},{5... | collective-permute-start | bytes 786440 | tf_op jit(solution)/shard_map/ppermute | solution.py:33
  13.5 13.2 %collective-permute-start.5 = (bf16[8,128,128]{2,1,0:T(8,128)(2,1)S(1)}, bf16[8,128,128]{2,1,0:T(8,128)(2,1)S(1)}, u32[]{:S(2)}, u32[]{:S(2)}) collective-permute-start(bf16[8,128,128]{2,1,0:T(8,128)(2,1)S(1)} %get-tuple-element.87), channel_id=1, source_target_pairs={{0,16},{4,20},{8,24},{12,28},{16,0},{20,4},{24,8},{28,12},{1,17},{... | collective-permute-start | bytes 786440 | tf_op jit(solution)/shard_map/ppermute | solution.py:33
  15.0 11.7 %collective-permute-start.6 = (bf16[8,128,128]{2,1,0:T(8,128)(2,1)S(1)}, bf16[8,128,128]{2,1,0:T(8,128)(2,1)S(1)}, u32[]{:S(2)}, u32[]{:S(2)}) collective-permute-start(bf16[8,128,128]{2,1,0:T(8,128)(2,1)S(1)} %get-tuple-element.88), channel_id=1, source_target_pairs={{0,24},{4,28},{8,16},{12,20},{16,8},{20,12},{24,0},{28,4},{1,25},{... | collective-permute-start | bytes 786440 | tf_op jit(solution)/shard_map/ppermute | solution.py:33
  15.2 18.1 %collective-permute-start.11 = (bf16[128,512]{1,0:T(8,128)(2,1)S(1)}, bf16[128,512]{1,0:T(8,128)(2,1)S(1)}, u32[]{:S(2)}, u32[]{:S(2)}) collective-permute-start(bf16[128,512]{1,0:T(8,128)(2,1)S(1)} %get-tuple-element.106), channel_id=1, source_target_pairs={{0,1},{1,0},{2,3},{3,2},{4,5},{5,4},{6,7},{7,6},{8,9},{9,8},{10,11... | collective-permute-start | bytes 393224 | tf_op jit(solution)/shard_map/ppermute | solution.py:33
  21.0 12.7 %collective-permute-start.12 = (bf16[128,512]{1,0:T(8,128)(2,1)S(1)}, bf16[128,512]{1,0:T(8,128)(2,1)S(1)}, u32[]{:S(2)}, u32[]{:S(2)}) collective-permute-start(bf16[128,512]{1,0:T(8,128)(2,1)S(1)} %get-tuple-element.107), channel_id=1, source_target_pairs={{0,2},{1,3},{2,0},{3,1},{4,6},{5,7},{6,4},{7,5},{8,10},{9,11},{10,... | collective-permute-start | bytes 393224 | tf_op jit(solution)/shard_map/ppermute | solution.py:33
  23.7 10.0 %collective-permute-start.13 = (bf16[128,512]{1,0:T(8,128)(2,1)S(1)}, bf16[128,512]{1,0:T(8,128)(2,1)S(1)}, u32[]{:S(2)}, u32[]{:S(2)}) collective-permute-start(bf16[128,512]{1,0:T(8,128)(2,1)S(1)} %get-tuple-element.108), channel_id=1, source_target_pairs={{0,3},{1,2},{2,1},{3,0},{4,7},{5,6},{6,5},{7,4},{8,11},{9,10},{10,... | collective-permute-start | bytes 393224 | tf_op jit(solution)/shard_map/ppermute | solution.py:33
  29.0 7.3 %collective-permute-start.8 = (bf16[128,512]{1,0:T(8,128)(2,1)S(1)}, bf16[128,512]{1,0:T(8,128)(2,1)S(1)}, u32[]{:S(2)}, u32[]{:S(2)}) collective-permute-start(bf16[128,512]{1,0:T(8,128)(2,1)S(1)} %get-tuple-element.101), channel_id=1, source_target_pairs={{0,1},{1,0},{2,3},{3,2},{4,5},{5,4},{6,7},{7,6},{8,9},{9,8},{10,11... | collective-permute-start | bytes 393224 | tf_op jit(solution)/shard_map/ppermute | solution.py:33
  30.7 13.7 %collective-permute-start.9 = (bf16[128,512]{1,0:T(8,128)(2,1)S(1)}, bf16[128,512]{1,0:T(8,128)(2,1)S(1)}, u32[]{:S(2)}, u32[]{:S(2)}) collective-permute-start(bf16[128,512]{1,0:T(8,128)(2,1)S(1)} %get-tuple-element.102), channel_id=1, source_target_pairs={{0,2},{1,3},{2,0},{3,1},{4,6},{5,7},{6,4},{7,5},{8,10},{9,11},{10,... | collective-permute-start | bytes 393224 | tf_op jit(solution)/shard_map/ppermute | solution.py:33
  33.3 11.1 %collective-permute-start.10 = (bf16[128,512]{1,0:T(8,128)(2,1)S(1)}, bf16[128,512]{1,0:T(8,128)(2,1)S(1)}, u32[]{:S(2)}, u32[]{:S(2)}) collective-permute-start(bf16[128,512]{1,0:T(8,128)(2,1)S(1)} %get-tuple-element.103), channel_id=1, source_target_pairs={{0,3},{1,2},{2,1},{3,0},{4,7},{5,6},{6,5},{7,4},{8,11},{9,10},{10,... | collective-permute-start | bytes 393224 | tf_op jit(solution)/shard_map/ppermute | solution.py:33
  45.7 11.2 %collective-permute-start.14 = (bf16[128,512]{1,0:T(8,128)(2,1)S(1)}, bf16[128,512]{1,0:T(8,128)(2,1)S(1)}, u32[]{:S(2)}, u32[]{:S(2)}) collective-permute-start(bf16[128,512]{1,0:T(8,128)(2,1)S(1)} %get-tuple-element.114), channel_id=1, source_target_pairs={{0,1},{1,0},{2,3},{3,2},{4,5},{5,4},{6,7},{7,6},{8,9},{9,8},{10,11... | collective-permute-start | bytes 393224 | tf_op jit(solution)/shard_map/ppermute | solution.py:33
  49.0 12.9 %collective-permute-start.15 = (bf16[128,512]{1,0:T(8,128)(2,1)S(1)}, bf16[128,512]{1,0:T(8,128)(2,1)S(1)}, u32[]{:S(2)}, u32[]{:S(2)}) collective-permute-start(bf16[128,512]{1,0:T(8,128)(2,1)S(1)} %get-tuple-element.115), channel_id=1, source_target_pairs={{0,2},{1,3},{2,0},{3,1},{4,6},{5,7},{6,4},{7,5},{8,10},{9,11},{10,... | collective-permute-start | bytes 393224 | tf_op jit(solution)/shard_map/ppermute | solution.py:33
  50.2 11.7 %collective-permute-start.16 = (bf16[128,512]{1,0:T(8,128)(2,1)S(1)}, bf16[128,512]{1,0:T(8,128)(2,1)S(1)}, u32[]{:S(2)}, u32[]{:S(2)}) collective-permute-start(bf16[128,512]{1,0:T(8,128)(2,1)S(1)} %get-tuple-element.116), channel_id=1, source_target_pairs={{0,3},{1,2},{2,1},{3,0},{4,7},{5,6},{6,5},{7,4},{8,11},{9,10},{10,... | collective-permute-start | bytes 393224 | tf_op jit(solution)/shard_map/ppermute | solution.py:33
  53.0 8.9 %collective-permute-start.18 = (bf16[64,512]{1,0:T(8,128)(2,1)S(1)}, bf16[64,512]{1,0:T(8,128)(2,1)S(1)}, u32[]{:S(2)}, u32[]{:S(2)}) collective-permute-start(bf16[64,512]{1,0:T(8,128)(2,1)S(1)} %get-tuple-element.119), channel_id=1, source_target_pairs={{0,8},{4,12},{8,0},{12,4},{16,24},{20,28},{24,16},{28,20},{1,9},{5... | collective-permute-start | bytes 196616 | tf_op jit(solution)/shard_map/ppermute | solution.py:33
  54.3 7.6 %collective-permute-start.19 = (bf16[64,512]{1,0:T(8,128)(2,1)S(1)}, bf16[64,512]{1,0:T(8,128)(2,1)S(1)}, u32[]{:S(2)}, u32[]{:S(2)}) collective-permute-start(bf16[64,512]{1,0:T(8,128)(2,1)S(1)} %get-tuple-element.120), channel_id=1, source_target_pairs={{0,16},{4,20},{8,24},{12,28},{16,0},{20,4},{24,8},{28,12},{1,17},{... | collective-permute-start | bytes 196616 | tf_op jit(solution)/shard_map/ppermute | solution.py:33
  62.8 9.8 %collective-permute-start.21 = (bf16[144,512]{1,0:T(8,128)(2,1)S(1)}, bf16[144,512]{1,0:T(8,128)(2,1)S(1)}, u32[]{:S(2)}, u32[]{:S(2)}) collective-permute-start(bf16[144,512]{1,0:T(8,128)(2,1)S(1)} %get-tuple-element.128), channel_id=1, source_target_pairs={{0,1},{1,0},{2,3},{3,2},{4,5},{5,4},{6,7},{7,6},{8,9},{9,8},{10,11... | collective-permute-start | bytes 442376 | tf_op jit(solution)/shard_map/ppermute | solution.py:33
  67.9 17.3 %collective-permute-start.24 = (bf16[8,128,128]{2,1,0:T(8,128)(2,1)S(1)}, bf16[8,128,128]{2,1,0:T(8,128)(2,1)S(1)}, u32[]{:S(2)}, u32[]{:S(2)}) collective-permute-start(bf16[8,128,128]{2,1,0:T(8,128)(2,1)S(1)} %get-tuple-element.131), channel_id=1, source_target_pairs={{0,8},{4,12},{8,0},{12,4},{16,24},{20,28},{24,16},{28,20},{1,9},{5... | collective-permute-start | bytes 786440 | tf_op jit(solution)/shard_map/ppermute | solution.py:33
  69.2 16.0 %collective-permute-start.25 = (bf16[8,128,128]{2,1,0:T(8,128)(2,1)S(1)}, bf16[8,128,128]{2,1,0:T(8,128)(2,1)S(1)}, u32[]{:S(2)}, u32[]{:S(2)}) collective-permute-start(bf16[8,128,128]{2,1,0:T(8,128)(2,1)S(1)} %get-tuple-element.132), channel_id=1, source_target_pairs={{0,16},{4,20},{8,24},{12,28},{16,0},{20,4},{24,8},{28,12},{1,17},{... | collective-permute-start | bytes 786440 | tf_op jit(solution)/shard_map/ppermute | solution.py:33
  71.6 13.6 %collective-permute-start.26 = (bf16[8,128,128]{2,1,0:T(8,128)(2,1)S(1)}, bf16[8,128,128]{2,1,0:T(8,128)(2,1)S(1)}, u32[]{:S(2)}, u32[]{:S(2)}) collective-permute-start(bf16[8,128,128]{2,1,0:T(8,128)(2,1)S(1)} %get-tuple-element.133), channel_id=1, source_target_pairs={{0,24},{4,28},{8,16},{12,20},{16,8},{20,12},{24,0},{28,4},{1,25},{... | collective-permute-start | bytes 786440 | tf_op jit(solution)/shard_map/ppermute | solution.py:33
  71.6 13.6 %collective-permute-start.22 = (bf16[144,512]{1,0:T(8,128)(2,1)S(1)}, bf16[144,512]{1,0:T(8,128)(2,1)S(1)}, u32[]{:S(2)}, u32[]{:S(2)}) collective-permute-start(bf16[144,512]{1,0:T(8,128)(2,1)S(1)} %get-tuple-element.129), channel_id=1, source_target_pairs={{0,2},{1,3},{2,0},{3,1},{4,6},{5,7},{6,4},{7,5},{8,10},{9,11},{10,... | collective-permute-start | bytes 442376 | tf_op jit(solution)/shard_map/ppermute | solution.py:33
  72.7 12.5 %collective-permute-start.23 = (bf16[144,512]{1,0:T(8,128)(2,1)S(1)}, bf16[144,512]{1,0:T(8,128)(2,1)S(1)}, u32[]{:S(2)}, u32[]{:S(2)}) collective-permute-start(bf16[144,512]{1,0:T(8,128)(2,1)S(1)} %get-tuple-element.130), channel_id=1, source_target_pairs={{0,3},{1,2},{2,1},{3,0},{4,7},{5,6},{6,5},{7,4},{8,11},{9,10},{10,... | collective-permute-start | bytes 442376 | tf_op jit(solution)/shard_map/ppermute | solution.py:33
  85.3 6.5 %collective-permute-start.32 = (bf16[12,128,128]{2,1,0:T(8,128)(2,1)S(1)}, bf16[12,128,128]{2,1,0:T(8,128)(2,1)S(1)}, u32[]{:S(2)}, u32[]{:S(2)}) collective-permute-start(bf16[12,128,128]{2,1,0:T(8,128)(2,1)S(1)} %shard_map.111), channel_id=1, source_target_pairs={{0,4},{4,0},{8,12},{12,8},{16,20},{20,16},{24,28},{28,24},{1,5},{5... | collective-permute-start | bytes 1179656 | tf_op jit(solution)/shard_map/ppermute | solution.py:33
  87.3 6.7 %collective-permute-start.30 = (f32[2,64,128]{2,1,0:T(8,128)S(1)}, f32[2,64,128]{2,1,0:T(8,128)S(1)}, u32[]{:S(2)}, u32[]{:S(2)}) collective-permute-start(f32[2,64,128]{2,1,0:T(8,128)S(1)} %shard_map.110.refs_0_), channel_id=1, source_target_pairs={{0,24},{4,28},{8,16},{12,20},{16,8},{20,12},{24,0},{28,4},{1,25},{... | collective-permute-start | bytes 196616 | tf_op jit(solution)/shard_map/ppermute | solution.py:33
  (15 other events, 106.0 us)

commit v4 on v3

--- a/solution.py
+++ b/solution.py
@@ -200,7 +200,7 @@
 
 
 def far_fwd_kernel(n_in, list_ref, me_ref, tiles_ref, *refs):
-    ins, base_ref, rest = refs[:n_in], refs[n_in], refs[n_in + 1 :]
+    ins, base_ref, rest = refs[:n_in][::-1], refs[n_in], refs[n_in + 1 :]
     outs, (x_ref, acc_ref) = rest[:-2], rest[-2:]
     per = 2 * SLOT
     for d, r in enumerate(ins):
@@ -238,7 +238,7 @@
     wide_ref, sib_ref, (x_ref, acc_ref) = rest[0], rest[1], rest[-2:]
     outs = rest[2:-2]
     per = 2 * SLOT
-    gather_blocks(wide_ref, mec_ref[0], ins)
+    gather_blocks(wide_ref, mec_ref[0], ins[::-1])
     fill_from_wide(x_ref, wide_ref, x_ref.shape[0] - 1)
     acc_ref[...] = jnp.zeros_like(acc_ref)
     sparse_loop(list_ref, 2, x_ref, tiles_ref, acc_ref, False)
@@ -251,13 +251,13 @@
 
 def forward_kernel(me_ref, *refs):
     other = 1 - (me_ref[0] & 1)
-    for e, r in enumerate(refs[:-1]):
+    for e, r in enumerate(refs[:-1][::-1]):
         for j in range(SLOT):
             refs[-1][e * SLOT + j] = r[other * SLOT + j]
 
 
 def join_kernel(n_chip, me_ref, table_ref, base_ref, sib_ref, fwd_ref, *refs):
-    ins, (out_ref, acc_ref) = refs[:-2], refs[-2:]
+    ins, (out_ref, acc_ref) = refs[:-2][::-1], refs[-2:]
     me = me_ref[0]
     core = me & 1
     n_row = 2 * n_chip
@@ -291,7 +291,7 @@
 
 
 def dense_kernel(n_col, me_ref, wt_ref, w_ref, *refs):
-    s_refs, g_refs = refs[:n_col], refs[n_col : 2 * n_col]
+    s_refs, g_refs = refs[:n_col][::-1], refs[n_col : 2 * n_col][::-1]
     o_refs, y_refs = refs[2 * n_col : 3 * n_col], refs[3 * n_col : 4 * n_col]
     sz_ref = refs[4 * n_col]
     f_loc = s_refs[0].shape[0]
@@ -446,7 +446,7 @@
     )
     table = jnp.concatenate(needs, axis=0)
     table = jnp.concatenate([table, over_chips(table)], axis=0)
-    got, table = lax.optimization_barrier((got, table))
+    got, table = lax.optimization_barrier((got[::-1], table))
 
     g_parts = call(
         split_kernel,
@@ -492,7 +492,7 @@
         + [sds((n_f + n_h, part), BF)],
         [],
         (mec,),
-        (weight_t, weight, *s_got, *grads),
+        (weight_t, weight, *s_got[::-1], *grads[::-1]),
         flops=4 * n_f * n_h * part,
         nbytes=n_f * part * 8,
     )
@@ -522,7 +522,7 @@
     w_own_cols = mixed[-1]
     mixed = [m if k == 0 else swap(m, "col", n_col, k) for k, m in enumerate(mixed[:-1])]
 
-    y_got, w_chips = lax.optimization_barrier((y_got, w_chips))
+    y_got, w_chips = lax.optimization_barrier((y_got[::-1], w_chips))
     back = call(
         functools.partial(far_bwd_kernel, n_col),
         [sds((f_loc, nodes), BF), sds((SLOT, f_loc, TILE), BF)]
@@ -546,19 +546,9 @@
         sds((w_rows, h_loc), F32),
         [],
         (),
-        (w_own_cols, *mixed[1:]),
-    )
-
-    w_mine = call(
-        functools.partial(weight_scale_kernel, float(nodes * n_row) ** (-0.5)),
-        sds((w_rows, h_loc), F32),
-        [],
-        (),
-        (w_own_cols, *mixed[1:]),
-    )
-
-    o_parts, _ = lax.optimization_barrier((o_parts, to_sib))
-    o_got = [o if k == 0 else swap(o, "col", n_col, k) for k, o in enumerate(o_parts)]
+        (w_own_cols, *mixed[:0:-1]),
+    )
+
     acc_b = call(
         own_bwd_kernel,
         sds((row_tiles, f_loc, TILE), F32),
@@ -569,7 +559,7 @@
         flops=tile_flops * slots,
         nbytes=tile_bytes,
     )
-    returned, acc_b, w_mine = lax.optimization_barrier((returned, acc_b, w_mine))
+    returned, acc_b, w_mine = lax.optimization_barrier((returned[::-1], acc_b, w_mine))
     passed = call(
         forward_kernel,
         sds(((n_chip - 1) * SLOT, f_loc, TILE), BF),

time: 95.8 us -> 91.2 us (0.952)
  starting transfers between devices: 42.5 us -> 39.1 us
  waiting for transfers between devices: 27.6 us -> 25.5 us
  Pallas kernels: 22.9 us -> 24.3 us
    ppermute x33, starting transfers between devices: 42.5 us -> 39.1 us  [swap(): return lax.ppermute(x, axis, [(i, i ^ k) for i in range(n)])]
    ppermute x33, waiting for transfers between devices: 27.6 us -> 25.5 us  [swap(): return lax.ppermute(x, axis, [(i, i ^ k) for i in range(n)])]
    pallas_call x19, Pallas kernels: 19.4 us -> 20.8 us  [call(): pl.pallas_call(kernel, out_shape=outs, in_specs=[SM] * len(smem) + [VM] *...]
  transfers between devices with their start and end apart: 33 -> 33, of which waited for: 8 -> 8; matrix products, arithmetic and copies ran while one was open for 0% -> 0% of each run, Pallas kernels for 20% -> 23%
where the time goes in v4:
time: 91.2 us
  starting transfers between devices  39.1 us (43%)
  waiting for transfers between devices  25.5 us (28%)
  Pallas kernels  24.3 us (27%)
  between operations  1.62 us (2%)
    ppermute x33, starting transfers between devices, swap(): return lax.ppermute(x, axis, [(i, i ^ k) for i in range(n)])  39.1 us
    ppermute x33, waiting for transfers between devices, swap(): return lax.ppermute(x, axis, [(i, i ^ k) for i in range(n)])  25.5 us
    pallas_call x19, Pallas kernels, call(): pl.pallas_call(kernel, out_shape=outs, in_specs=[SM] * len(smem) + [VM] *...  20.8 us
    pallas_call x1, Pallas kernels, shards(): pl.pallas_call(load_kernel, out_shape=sds(tile_values.shape, BF), in_spec...  3.47 us
  transfers between devices with their start and end apart: 33, of which 8 were waited for; matrix products, arithmetic and copies ran while one was open for 0% of the time, Pallas kernels for 23%

profile of v4, /device:TPU:0, one launch (start us, length us, event | category | flops | bytes accessed | tf_op | source)
XLA Modules:
  0.0 91.2 jit_solution(1841290453556066054)
XLA Ops:
  2.8 3.5 %collective-permute-start.2 = (s32[8,128]{1,0:T(8,128)S(1)}, s32[8,128]{1,0:T(8,128)S(1)}, u32[]{:S(2)}, u32[]{:S(2)}) collective-permute-start(s32[8,128]{1,0:T(8,128)S(1)} %shard_map.94), channel_id=1, source_target_pairs={{0,24},{4,28},{8,16},{12,20},{16,8},{20,12},{24,0},{28,4},{1,25},{... | collective-permute-start | bytes 12296 | tf_op jit(solution)/shard_map/ppermute | solution.py:33
  7.0 3.5 %shard_map.96.tiles_ref = bf16[256,128,128]{2,1,0:T(8,128)(2,1)S(1)} custom-call(bf16[256,128,128]{2,1,0:T(8,128)(2,1)} %in_ref), custom_call_target="tpu_custom_call" | custom-call | bytes 8388608 | tf_op jit(solution)/shard_map/pallas_call | solution.py:418
  11.5 2.0 %collective-permute-start.6 = (bf16[8,128,128]{2,1,0:T(8,128)(2,1)S(1)}, bf16[8,128,128]{2,1,0:T(8,128)(2,1)S(1)}, u32[]{:S(2)}, u32[]{:S(2)}) collective-permute-start(bf16[8,128,128]{2,1,0:T(8,128)(2,1)S(1)} %get-tuple-element.85), channel_id=1, source_target_pairs={{0,8},{4,12},{8,0},{12,4},{16,24},{20,28},{24,16},{28,20},{1,9},{5... | collective-permute-start | bytes 786440 | tf_op jit(solution)/shard_map/ppermute | solution.py:33
  13.5 1.5 %collective-permute-start.5 = (bf16[8,128,128]{2,1,0:T(8,128)(2,1)S(1)}, bf16[8,128,128]{2,1,0:T(8,128)(2,1)S(1)}, u32[]{:S(2)}, u32[]{:S(2)}) collective-permute-start(bf16[8,128,128]{2,1,0:T(8,128)(2,1)S(1)} %get-tuple-element.86), channel_id=1, source_target_pairs={{0,16},{4,20},{8,24},{12,28},{16,0},{20,4},{24,8},{28,12},{1,17},{... | collective-permute-start | bytes 786440 | tf_op jit(solution)/shard_map/ppermute | solution.py:33
  15.2 4.1 %collective-permute-start.11 = (bf16[128,512]{1,0:T(8,128)(2,1)S(1)}, bf16[128,512]{1,0:T(8,128)(2,1)S(1)}, u32[]{:S(2)}, u32[]{:S(2)}) collective-permute-start(bf16[128,512]{1,0:T(8,128)(2,1)S(1)} %get-tuple-element.104), channel_id=1, source_target_pairs={{0,3},{1,2},{2,1},{3,0},{4,7},{5,6},{6,5},{7,4},{8,11},{9,10},{10,... | collective-permute-start | bytes 393224 | tf_op jit(solution)/shard_map/ppermute | solution.py:33
  19.2 1.5 %shard_map.98.list_ref = s32[8,384]{1,0:T(8,128)S(1)} custom-call(s32[1]{0:T(128)S(6)} %copy.14.count_ref, s32[1]{0:T(128)} %bitcast.me_ref.mer_ref, s32[1,256]{1,0:T(1,128)S(1)} %copy-done.4, s32[1,256]{1,0:T(1,128)S(1)} %copy-done.5), custom_call_target="tpu_custom_call" | custom-call | tf_op jit(solution)/shard_map/pallas_call | solution.py:21
  20.8 2.7 %shard_map.99.refs_3_ = f32[16,128,128]{2,1,0:T(8,128)S(1)} custom-call(s32[8,384]{1,0:T(8,128)S(1)} %shard_map.98.list_ref, bf16[256,128,128]{2,1,0:T(8,128)(2,1)S(1)} %shard_map.96.tiles_ref, bf16[33,128,128]{2,1,0:T(8,128)(2,1)S(1)} %shard_map.95.refs_3_.x_ref), custom_call_target="tpu_custom_call" | custom-call | flops 1073741824 | bytes 8388608 | tf_op jit(solution)/shard_map/pallas_call | solution.py:21
  24.2 2.5 %collective-permute-done.5.refs_1_ = bf16[8,128,128]{2,1,0:T(8,128)(2,1)S(1)} collective-permute-done((bf16[8,128,128]{2,1,0:T(8,128)(2,1)S(1)}, bf16[8,128,128]{2,1,0:T(8,128)(2,1)S(1)}, u32[]{:S(2)}, u32[]{:S(2)}) %collective-permute-start.5) | collective-permute-done | bytes 262176 | tf_op jit(solution)/shard_map/ppermute | solution.py:33
  26.7 2.4 %shard_map.100 = (bf16[128,512]{1,0:T(8,128)(2,1)S(1)}, bf16[128,512]{1,0:T(8,128)(2,1)S(1)}, bf16[128,512]{1,0:T(8,128)(2,1)S(1)}, bf16[128,512]{1,0:T(8,128)(2,1)S(1)}) custom-call(s32[8,384]{1,0:T(8,128)S(1)} %shard_map.98.list_ref, s32[1]{0:T(128)} %bitcast.1.me_ref.mec_ref, bf16[256,128,128]{2,1,0:T(8,128)(2,1)S(1)} %shard_map.96.tiles_ref, ...), custom_call_target="tpu_custom_call" | custom-call | flops 1073741824 | bytes 8388608 | tf_op jit(solution)/shard_map/pallas_call | solution.py:21
  29.0 3.7 %collective-permute-start.8 = (bf16[128,512]{1,0:T(8,128)(2,1)S(1)}, bf16[128,512]{1,0:T(8,128)(2,1)S(1)}, u32[]{:S(2)}, u32[]{:S(2)}) collective-permute-start(bf16[128,512]{1,0:T(8,128)(2,1)S(1)} %get-tuple-element.100), channel_id=1, source_target_pairs={{0,3},{1,2},{2,1},{3,0},{4,7},{5,6},{6,5},{7,4},{8,11},{9,10},{10,... | collective-permute-start | bytes 393224 | tf_op jit(solution)/shard_map/ppermute | solution.py:33
  33.7 3.5 %collective-permute-done.8.refs_0_ = bf16[128,512]{1,0:T(8,128)(2,1)S(1)} collective-permute-done((bf16[128,512]{1,0:T(8,128)(2,1)S(1)}, bf16[128,512]{1,0:T(8,128)(2,1)S(1)}, u32[]{:S(2)}, u32[]{:S(2)}) %collective-permute-start.8) | collective-permute-done | bytes 131104 | tf_op jit(solution)/shard_map/ppermute | solution.py:33
  37.2 5.9 %collective-permute-done.9.refs_1_ = bf16[128,512]{1,0:T(8,128)(2,1)S(1)} collective-permute-done((bf16[128,512]{1,0:T(8,128)(2,1)S(1)}, bf16[128,512]{1,0:T(8,128)(2,1)S(1)}, u32[]{:S(2)}, u32[]{:S(2)}) %collective-permute-start.9) | collective-permute-done | bytes 131104 | tf_op jit(solution)/shard_map/ppermute | solution.py:33
  44.5 2.1 %collective-permute-start.21 = (bf16[128,512]{1,0:T(8,128)(2,1)S(1)}, bf16[128,512]{1,0:T(8,128)(2,1)S(1)}, u32[]{:S(2)}, u32[]{:S(2)}) collective-permute-start(bf16[128,512]{1,0:T(8,128)(2,1)S(1)} %get-tuple-element.120), channel_id=1, source_target_pairs={{0,3},{1,2},{2,1},{3,0},{4,7},{5,6},{6,5},{7,4},{8,11},{9,10},{10,... | collective-permute-start | bytes 393224 | tf_op jit(solution)/shard_map/ppermute | solution.py:33
  46.6 2.4 %collective-permute-start.23 = (bf16[128,512]{1,0:T(8,128)(2,1)S(1)}, bf16[128,512]{1,0:T(8,128)(2,1)S(1)}, u32[]{:S(2)}, u32[]{:S(2)}) collective-permute-start(bf16[128,512]{1,0:T(8,128)(2,1)S(1)} %get-tuple-element.122), channel_id=1, source_target_pairs={{0,1},{1,0},{2,3},{3,2},{4,5},{5,4},{6,7},{7,6},{8,9},{9,8},{10,11... | collective-permute-start | bytes 393224 | tf_op jit(solution)/shard_map/ppermute | solution.py:33
  50.3 1.8 %collective-permute-start.15 = (bf16[64,512]{1,0:T(8,128)(2,1)S(1)}, bf16[64,512]{1,0:T(8,128)(2,1)S(1)}, u32[]{:S(2)}, u32[]{:S(2)}) collective-permute-start(bf16[64,512]{1,0:T(8,128)(2,1)S(1)} %get-tuple-element.111), channel_id=1, source_target_pairs={{0,8},{4,12},{8,0},{12,4},{16,24},{20,28},{24,16},{28,20},{1,9},{5... | collective-permute-start | bytes 196616 | tf_op jit(solution)/shard_map/ppermute | solution.py:33
  53.2 1.4 %collective-permute-start.17 = (bf16[64,512]{1,0:T(8,128)(2,1)S(1)}, bf16[64,512]{1,0:T(8,128)(2,1)S(1)}, u32[]{:S(2)}, u32[]{:S(2)}) collective-permute-start(bf16[64,512]{1,0:T(8,128)(2,1)S(1)} %get-tuple-element.113), channel_id=1, source_target_pairs={{0,24},{4,28},{8,16},{12,20},{16,8},{20,12},{24,0},{28,4},{1,25},{... | collective-permute-start | bytes 196616 | tf_op jit(solution)/shard_map/ppermute | solution.py:33
  54.6 3.2 %collective-permute-done.22.refs_1_ = bf16[128,512]{1,0:T(8,128)(2,1)S(1)} collective-permute-done((bf16[128,512]{1,0:T(8,128)(2,1)S(1)}, bf16[128,512]{1,0:T(8,128)(2,1)S(1)}, u32[]{:S(2)}, u32[]{:S(2)}) %collective-permute-start.22) | collective-permute-done | bytes 131104 | tf_op jit(solution)/shard_map/ppermute | solution.py:33
  59.3 2.9 %shard_map.107 = (bf16[128,2048]{1,0:T(8,128)(2,1)S(1)}, bf16[4,128,128]{2,1,0:T(8,128)(2,1)S(1)}, bf16[8,128,128]{2,1,0:T(8,128)(2,1)S(1)}, bf16[8,128,128]{2,1,0:T(8,128)(2,1)S(1)}, bf16[8,128,128]{2,1,0:T(8,128)(2,1)S(1)}) custom-call(s32[8,384]{1,0:T(8,128)S(1)} %shard_map.98.list_ref, s32[1]{0:T(128)} %bitcast.1.me_ref.mec_ref, s32[1]{0:T(128)} %bitcast.me_ref.mer_ref, ...), custom_call_target="tpu_custom_call" | custom-call | flops 1073741824 | bytes 8388608 | tf_op jit(solution)/shard_map/pallas_call | solution.py:21
  63.2 4.0 %collective-permute-start.25 = (bf16[8,128,128]{2,1,0:T(8,128)(2,1)S(1)}, bf16[8,128,128]{2,1,0:T(8,128)(2,1)S(1)}, u32[]{:S(2)}, u32[]{:S(2)}) collective-permute-start(bf16[8,128,128]{2,1,0:T(8,128)(2,1)S(1)} %get-tuple-element.129), channel_id=1, source_target_pairs={{0,16},{4,20},{8,24},{12,28},{16,0},{20,4},{24,8},{28,12},{1,17},{... | collective-permute-start | bytes 786440 | tf_op jit(solution)/shard_map/ppermute | solution.py:33
  68.8 2.0 %collective-permute-start.20 = (bf16[144,512]{1,0:T(8,128)(2,1)S(1)}, bf16[144,512]{1,0:T(8,128)(2,1)S(1)}, u32[]{:S(2)}, u32[]{:S(2)}) collective-permute-start(bf16[144,512]{1,0:T(8,128)(2,1)S(1)} %get-tuple-element.119), channel_id=1, source_target_pairs={{0,3},{1,2},{2,1},{3,0},{4,7},{5,6},{6,5},{7,4},{8,11},{9,10},{10,... | collective-permute-start | bytes 442376 | tf_op jit(solution)/shard_map/ppermute | solution.py:33
  70.9 2.5 %shard_map.108.base_ref = f32[16,128,128]{2,1,0:T(8,128)S(1)} custom-call(s32[8,384]{1,0:T(8,128)S(1)} %shard_map.98.list_ref, bf16[256,128,128]{2,1,0:T(8,128)(2,1)S(1)} %shard_map.96.tiles_ref, bf16[128,2048]{1,0:T(8,128)(2,1)S(1)} %get-tuple-element.131.wide_ref), custom_call_target="tpu_custom_call" | custom-call | flops 1073741824 | bytes 8388608 | tf_op jit(solution)/shard_map/pallas_call | solution.py:21
  73.4 8.2 %collective-permute-done.19.refs_2_.refs_1_ = bf16[144,512]{1,0:T(8,128)(2,1)S(1)} collective-permute-done((bf16[144,512]{1,0:T(8,128)(2,1)S(1)}, bf16[144,512]{1,0:T(8,128)(2,1)S(1)}, u32[]{:S(2)}, u32[]{:S(2)}) %collective-permute-start.19) | collective-permute-done | bytes 147488 | tf_op jit(solution)/shard_map/ppermute | solution.py:33
  83.7 1.5 %collective-permute-start.30 = (f32[2,64,128]{2,1,0:T(8,128)S(1)}, f32[2,64,128]{2,1,0:T(8,128)S(1)}, u32[]{:S(2)}, u32[]{:S(2)}) collective-permute-start(f32[2,64,128]{2,1,0:T(8,128)S(1)} %shard_map.110.refs_0_), channel_id=1, source_target_pairs={{0,24},{4,28},{8,16},{12,20},{16,8},{20,12},{24,0},{28,4},{1,25},{... | collective-permute-start | bytes 196616 | tf_op jit(solution)/shard_map/ppermute | solution.py:33
  88.1 2.3 %shard_map.112 = bf16[128,2048]{1,0:T(8,128)(2,1)} custom-call(s32[1]{0:T(128)} %bitcast.me_ref.mer_ref, s32[64,128]{1,0:T(8,128)S(1)} %constant_dynamic-update-slice_fusion.table_ref, f32[16,128,128]{2,1,0:T(8,128)S(1)} %shard_map.108.base_ref, bf16[4,128,128]{2,1,0:T(8,128)(2,1)S(1)} %collective-permute-done.31.sib_ref, ...), custom_call_target="tpu_custom_call" | custom-call | bytes 2097152 | tf_op jit(solution)/shard_map/pallas_call | solution.py:21
  (80 shorter events, 18.6 us)
Async XLA Ops:
  0.6 9.8 %collective-permute-start.3 = (bf16[128,2048]{1,0:T(8,128)(2,1)}, bf16[128,2048]{1,0:T(8,128)(2,1)S(1)}, u32[]{:S(2)}, u32[]{:S(2)}) collective-permute-start(bf16[128,2048]{1,0:T(8,128)(2,1)} %feat_ref.1), channel_id=1, source_target_pairs={{0,4},{4,0},{8,12},{12,8},{16,20},{20,16},{24,28},{28,24},{1,5},{5... | collective-permute-start | bytes 1572872 | tf_op jit(solution)/shard_map/ppermute | solution.py:33
  2.8 7.9 %collective-permute-start.2 = (s32[8,128]{1,0:T(8,128)S(1)}, s32[8,128]{1,0:T(8,128)S(1)}, u32[]{:S(2)}, u32[]{:S(2)}) collective-permute-start(s32[8,128]{1,0:T(8,128)S(1)} %shard_map.94), channel_id=1, source_target_pairs={{0,24},{4,28},{8,16},{12,20},{16,8},{20,12},{24,0},{28,4},{1,25},{... | collective-permute-start | bytes 12296 | tf_op jit(solution)/shard_map/ppermute | solution.py:33
  11.5 12.1 %collective-permute-start.6 = (bf16[8,128,128]{2,1,0:T(8,128)(2,1)S(1)}, bf16[8,128,128]{2,1,0:T(8,128)(2,1)S(1)}, u32[]{:S(2)}, u32[]{:S(2)}) collective-permute-start(bf16[8,128,128]{2,1,0:T(8,128)(2,1)S(1)} %get-tuple-element.85), channel_id=1, source_target_pairs={{0,8},{4,12},{8,0},{12,4},{16,24},{20,28},{24,16},{28,20},{1,9},{5... | collective-permute-start | bytes 786440 | tf_op jit(solution)/shard_map/ppermute | solution.py:33
  13.5 13.2 %collective-permute-start.5 = (bf16[8,128,128]{2,1,0:T(8,128)(2,1)S(1)}, bf16[8,128,128]{2,1,0:T(8,128)(2,1)S(1)}, u32[]{:S(2)}, u32[]{:S(2)}) collective-permute-start(bf16[8,128,128]{2,1,0:T(8,128)(2,1)S(1)} %get-tuple-element.86), channel_id=1, source_target_pairs={{0,16},{4,20},{8,24},{12,28},{16,0},{20,4},{24,8},{28,12},{1,17},{... | collective-permute-start | bytes 786440 | tf_op jit(solution)/shard_map/ppermute | solution.py:33
  15.0 11.7 %collective-permute-start.4 = (bf16[8,128,128]{2,1,0:T(8,128)(2,1)S(1)}, bf16[8,128,128]{2,1,0:T(8,128)(2,1)S(1)}, u32[]{:S(2)}, u32[]{:S(2)}) collective-permute-start(bf16[8,128,128]{2,1,0:T(8,128)(2,1)S(1)} %get-tuple-element.87), channel_id=1, source_target_pairs={{0,24},{4,28},{8,16},{12,20},{16,8},{20,12},{24,0},{28,4},{1,25},{... | collective-permute-start | bytes 786440 | tf_op jit(solution)/shard_map/ppermute | solution.py:33
  15.1 8.5 %collective-permute-start.7 = (s32[32,128]{1,0:T(8,128)S(1)}, s32[32,128]{1,0:T(8,128)S(1)}, u32[]{:S(2)}, u32[]{:S(2)}) collective-permute-start(s32[32,128]{1,0:T(8,128)S(1)} %pad_add_fusion), channel_id=1, source_target_pairs={{0,4},{4,0},{8,12},{12,8},{16,20},{20,16},{24,28},{28,24},{1,5},{5... | collective-permute-start | bytes 49160 | tf_op jit(solution)/shard_map/ppermute | solution.py:33
  15.2 17.5 %collective-permute-start.11 = (bf16[128,512]{1,0:T(8,128)(2,1)S(1)}, bf16[128,512]{1,0:T(8,128)(2,1)S(1)}, u32[]{:S(2)}, u32[]{:S(2)}) collective-permute-start(bf16[128,512]{1,0:T(8,128)(2,1)S(1)} %get-tuple-element.104), channel_id=1, source_target_pairs={{0,3},{1,2},{2,1},{3,0},{4,7},{5,6},{6,5},{7,4},{8,11},{9,10},{10,... | collective-permute-start | bytes 393224 | tf_op jit(solution)/shard_map/ppermute | solution.py:33
  23.5 10.2 %collective-permute-start.12 = (bf16[128,512]{1,0:T(8,128)(2,1)S(1)}, bf16[128,512]{1,0:T(8,128)(2,1)S(1)}, u32[]{:S(2)}, u32[]{:S(2)}) collective-permute-start(bf16[128,512]{1,0:T(8,128)(2,1)S(1)} %get-tuple-element.105), channel_id=1, source_target_pairs={{0,2},{1,3},{2,0},{3,1},{4,6},{5,7},{6,4},{7,5},{8,10},{9,11},{10,... | collective-permute-start | bytes 393224 | tf_op jit(solution)/shard_map/ppermute | solution.py:33
  23.6 10.1 %collective-permute-start.13 = (bf16[128,512]{1,0:T(8,128)(2,1)S(1)}, bf16[128,512]{1,0:T(8,128)(2,1)S(1)}, u32[]{:S(2)}, u32[]{:S(2)}) collective-permute-start(bf16[128,512]{1,0:T(8,128)(2,1)S(1)} %get-tuple-element.106), channel_id=1, source_target_pairs={{0,1},{1,0},{2,3},{3,2},{4,5},{5,4},{6,7},{7,6},{8,9},{9,8},{10,11... | collective-permute-start | bytes 393224 | tf_op jit(solution)/shard_map/ppermute | solution.py:33
  29.0 8.2 %collective-permute-start.8 = (bf16[128,512]{1,0:T(8,128)(2,1)S(1)}, bf16[128,512]{1,0:T(8,128)(2,1)S(1)}, u32[]{:S(2)}, u32[]{:S(2)}) collective-permute-start(bf16[128,512]{1,0:T(8,128)(2,1)S(1)} %get-tuple-element.100), channel_id=1, source_target_pairs={{0,3},{1,2},{2,1},{3,0},{4,7},{5,6},{6,5},{7,4},{8,11},{9,10},{10,... | collective-permute-start | bytes 393224 | tf_op jit(solution)/shard_map/ppermute | solution.py:33
  32.7 10.5 %collective-permute-start.9 = (bf16[128,512]{1,0:T(8,128)(2,1)S(1)}, bf16[128,512]{1,0:T(8,128)(2,1)S(1)}, u32[]{:S(2)}, u32[]{:S(2)}) collective-permute-start(bf16[128,512]{1,0:T(8,128)(2,1)S(1)} %get-tuple-element.101), channel_id=1, source_target_pairs={{0,2},{1,3},{2,0},{3,1},{4,6},{5,7},{6,4},{7,5},{8,10},{9,11},{10,... | collective-permute-start | bytes 393224 | tf_op jit(solution)/shard_map/ppermute | solution.py:33
  32.7 10.5 %collective-permute-start.10 = (bf16[128,512]{1,0:T(8,128)(2,1)S(1)}, bf16[128,512]{1,0:T(8,128)(2,1)S(1)}, u32[]{:S(2)}, u32[]{:S(2)}) collective-permute-start(bf16[128,512]{1,0:T(8,128)(2,1)S(1)} %get-tuple-element.102), channel_id=1, source_target_pairs={{0,1},{1,0},{2,3},{3,2},{4,5},{5,4},{6,7},{7,6},{8,9},{9,8},{10,11... | collective-permute-start | bytes 393224 | tf_op jit(solution)/shard_map/ppermute | solution.py:33
  44.5 8.8 %collective-permute-start.21 = (bf16[128,512]{1,0:T(8,128)(2,1)S(1)}, bf16[128,512]{1,0:T(8,128)(2,1)S(1)}, u32[]{:S(2)}, u32[]{:S(2)}) collective-permute-start(bf16[128,512]{1,0:T(8,128)(2,1)S(1)} %get-tuple-element.120), channel_id=1, source_target_pairs={{0,3},{1,2},{2,1},{3,0},{4,7},{5,6},{6,5},{7,4},{8,11},{9,10},{10,... | collective-permute-start | bytes 393224 | tf_op jit(solution)/shard_map/ppermute | solution.py:33
  46.5 11.3 %collective-permute-start.22 = (bf16[128,512]{1,0:T(8,128)(2,1)S(1)}, bf16[128,512]{1,0:T(8,128)(2,1)S(1)}, u32[]{:S(2)}, u32[]{:S(2)}) collective-permute-start(bf16[128,512]{1,0:T(8,128)(2,1)S(1)} %get-tuple-element.121), channel_id=1, source_target_pairs={{0,2},{1,3},{2,0},{3,1},{4,6},{5,7},{6,4},{7,5},{8,10},{9,11},{10,... | collective-permute-start | bytes 393224 | tf_op jit(solution)/shard_map/ppermute | solution.py:33
  46.6 11.3 %collective-permute-start.23 = (bf16[128,512]{1,0:T(8,128)(2,1)S(1)}, bf16[128,512]{1,0:T(8,128)(2,1)S(1)}, u32[]{:S(2)}, u32[]{:S(2)}) collective-permute-start(bf16[128,512]{1,0:T(8,128)(2,1)S(1)} %get-tuple-element.122), channel_id=1, source_target_pairs={{0,1},{1,0},{2,3},{3,2},{4,5},{5,4},{6,7},{7,6},{8,9},{9,8},{10,11... | collective-permute-start | bytes 393224 | tf_op jit(solution)/shard_map/ppermute | solution.py:33
  50.3 7.5 %collective-permute-start.15 = (bf16[64,512]{1,0:T(8,128)(2,1)S(1)}, bf16[64,512]{1,0:T(8,128)(2,1)S(1)}, u32[]{:S(2)}, u32[]{:S(2)}) collective-permute-start(bf16[64,512]{1,0:T(8,128)(2,1)S(1)} %get-tuple-element.111), channel_id=1, source_target_pairs={{0,8},{4,12},{8,0},{12,4},{16,24},{20,28},{24,16},{28,20},{1,9},{5... | collective-permute-start | bytes 196616 | tf_op jit(solution)/shard_map/ppermute | solution.py:33
  59.2 9.6 %collective-permute-start.18 = (bf16[144,512]{1,0:T(8,128)(2,1)S(1)}, bf16[144,512]{1,0:T(8,128)(2,1)S(1)}, u32[]{:S(2)}, u32[]{:S(2)}) collective-permute-start(bf16[144,512]{1,0:T(8,128)(2,1)S(1)} %get-tuple-element.117), channel_id=1, source_target_pairs={{0,1},{1,0},{2,3},{3,2},{4,5},{5,4},{6,7},{7,6},{8,9},{9,8},{10,11... | collective-permute-start | bytes 442376 | tf_op jit(solution)/shard_map/ppermute | solution.py:33
  62.3 19.4 %collective-permute-start.24 = (bf16[8,128,128]{2,1,0:T(8,128)(2,1)S(1)}, bf16[8,128,128]{2,1,0:T(8,128)(2,1)S(1)}, u32[]{:S(2)}, u32[]{:S(2)}) collective-permute-start(bf16[8,128,128]{2,1,0:T(8,128)(2,1)S(1)} %get-tuple-element.128), channel_id=1, source_target_pairs={{0,24},{4,28},{8,16},{12,20},{16,8},{20,12},{24,0},{28,4},{1,25},{... | collective-permute-start | bytes 786440 | tf_op jit(solution)/shard_map/ppermute | solution.py:33
  63.2 18.5 %collective-permute-start.25 = (bf16[8,128,128]{2,1,0:T(8,128)(2,1)S(1)}, bf16[8,128,128]{2,1,0:T(8,128)(2,1)S(1)}, u32[]{:S(2)}, u32[]{:S(2)}) collective-permute-start(bf16[8,128,128]{2,1,0:T(8,128)(2,1)S(1)} %get-tuple-element.129), channel_id=1, source_target_pairs={{0,16},{4,20},{8,24},{12,28},{16,0},{20,4},{24,8},{28,12},{1,17},{... | collective-permute-start | bytes 786440 | tf_op jit(solution)/shard_map/ppermute | solution.py:33
  67.1 14.5 %collective-permute-start.26 = (bf16[8,128,128]{2,1,0:T(8,128)(2,1)S(1)}, bf16[8,128,128]{2,1,0:T(8,128)(2,1)S(1)}, u32[]{:S(2)}, u32[]{:S(2)}) collective-permute-start(bf16[8,128,128]{2,1,0:T(8,128)(2,1)S(1)} %get-tuple-element.130), channel_id=1, source_target_pairs={{0,8},{4,12},{8,0},{12,4},{16,24},{20,28},{24,16},{28,20},{1,9},{5... | collective-permute-start | bytes 786440 | tf_op jit(solution)/shard_map/ppermute | solution.py:33
  68.5 13.1 %collective-permute-start.19 = (bf16[144,512]{1,0:T(8,128)(2,1)S(1)}, bf16[144,512]{1,0:T(8,128)(2,1)S(1)}, u32[]{:S(2)}, u32[]{:S(2)}) collective-permute-start(bf16[144,512]{1,0:T(8,128)(2,1)S(1)} %get-tuple-element.118), channel_id=1, source_target_pairs={{0,2},{1,3},{2,0},{3,1},{4,6},{5,7},{6,4},{7,5},{8,10},{9,11},{10,... | collective-permute-start | bytes 442376 | tf_op jit(solution)/shard_map/ppermute | solution.py:33
  68.8 12.8 %collective-permute-start.20 = (bf16[144,512]{1,0:T(8,128)(2,1)S(1)}, bf16[144,512]{1,0:T(8,128)(2,1)S(1)}, u32[]{:S(2)}, u32[]{:S(2)}) collective-permute-start(bf16[144,512]{1,0:T(8,128)(2,1)S(1)} %get-tuple-element.119), channel_id=1, source_target_pairs={{0,3},{1,2},{2,1},{3,0},{4,7},{5,6},{6,5},{7,4},{8,11},{9,10},{10,... | collective-permute-start | bytes 442376 | tf_op jit(solution)/shard_map/ppermute | solution.py:33
  81.7 6.4 %collective-permute-start.32 = (bf16[12,128,128]{2,1,0:T(8,128)(2,1)S(1)}, bf16[12,128,128]{2,1,0:T(8,128)(2,1)S(1)}, u32[]{:S(2)}, u32[]{:S(2)}) collective-permute-start(bf16[12,128,128]{2,1,0:T(8,128)(2,1)S(1)} %shard_map.111), channel_id=1, source_target_pairs={{0,4},{4,0},{8,12},{12,8},{16,20},{20,16},{24,28},{28,24},{1,5},{5... | collective-permute-start | bytes 1179656 | tf_op jit(solution)/shard_map/ppermute | solution.py:33
  83.7 6.6 %collective-permute-start.30 = (f32[2,64,128]{2,1,0:T(8,128)S(1)}, f32[2,64,128]{2,1,0:T(8,128)S(1)}, u32[]{:S(2)}, u32[]{:S(2)}) collective-permute-start(f32[2,64,128]{2,1,0:T(8,128)S(1)} %shard_map.110.refs_0_), channel_id=1, source_target_pairs={{0,24},{4,28},{8,16},{12,20},{16,8},{20,12},{24,0},{28,4},{1,25},{... | collective-permute-start | bytes 196616 | tf_op jit(solution)/shard_map/ppermute | solution.py:33
  (15 other events, 107.4 us)

commit v5 on v4

--- a/solution.py
+++ b/solution.py
@@ -9,7 +9,7 @@
 
 TILE = 128
 SLOT = 4
-UNROLL = 4
+UNROLL = 8
 LOADS = 8
 BF = jnp.bfloat16
 F32 = jnp.float32
@@ -249,6 +249,11 @@
         sib_ref[j] = acc_ref[other * SLOT + j].astype(BF)
 
 
+def table_kernel(n_row, me_ref, all_ref, out_ref):
+    for p in range(out_ref.shape[0]):
+        out_ref[p : p + 1, :] = all_ref[pl.ds(p * n_row + me_ref[0], 1), :]
+
+
 def forward_kernel(me_ref, *refs):
     other = 1 - (me_ref[0] & 1)
     for e, r in enumerate(refs[:-1][::-1]):
@@ -258,12 +263,10 @@
 
 def join_kernel(n_chip, me_ref, table_ref, base_ref, sib_ref, fwd_ref, *refs):
     ins, (out_ref, acc_ref) = refs[:-2][::-1], refs[-2:]
-    me = me_ref[0]
-    core = me & 1
-    n_row = 2 * n_chip
+    core = me_ref[0] & 1
 
     def tile(e, j, other):
-        return table_ref[(other * n_chip + e) * n_row + me, j]
+        return table_ref[other * n_chip + e, j]
 
     acc_ref[...] = base_ref[...]
     for j in range(SLOT):
@@ -323,7 +326,8 @@
 def place_kernel(me_ref, *refs):
     wide_ref = refs[-1]
     width = refs[0].shape[1]
-    for k, r in enumerate(refs[:-1]):
+    parts = [refs[0], *refs[-2:0:-1]]
+    for k, r in enumerate(parts):
         at = pl.multiple_of((me_ref[0] ^ k) * width, width)
         wide_ref[:, pl.ds(at, width)] = r[: wide_ref.shape[0], :]
 
@@ -446,7 +450,10 @@
     )
     table = jnp.concatenate(needs, axis=0)
     table = jnp.concatenate([table, over_chips(table)], axis=0)
-    got, table = lax.optimization_barrier((got[::-1], table))
+    table = call(
+        functools.partial(table_kernel, n_row), sds((n_row, 128), jnp.int32), [], (mer,), (table,)
+    )
+    got, table = lax.optimization_barrier((got, table))
 
     g_parts = call(
         split_kernel,
@@ -476,7 +483,7 @@
             pltpu.VMEM((row_tiles, f_loc, TILE), F32),
         ],
         (lists, mec),
-        (*got, acc),
+        (*got[::-1], acc),
         (tile_values,),
         flops=tile_flops * slots,
         nbytes=tile_bytes,
@@ -516,13 +523,13 @@
         [sds((h_loc + more, part), BF)] * n_col + [sds((w_rows, h_loc), F32)],
         [pltpu.VMEM((w_rows, n_h), F32)],
         (mec,),
-        (*w_chips, *o_parts),
+        (w_chips[0], *w_chips[:0:-1], *o_parts),
         nbytes=n_h * part * 4,
     )
     w_own_cols = mixed[-1]
     mixed = [m if k == 0 else swap(m, "col", n_col, k) for k, m in enumerate(mixed[:-1])]
 
-    y_got, w_chips = lax.optimization_barrier((y_got[::-1], w_chips))
+    y_got, _ = lax.optimization_barrier((y_got[::-1], w_chips[::-1]))
     back = call(
         functools.partial(far_bwd_kernel, n_col),
         [sds((f_loc, nodes), BF), sds((SLOT, f_loc, TILE), BF)]
@@ -567,9 +574,11 @@
         (mer,),
         tuple(returned),
     )
-    w_pair = call(
-        pair_kernel, sds((2, w_rows, h_loc), F32), [], (mer,), (w_mine, over_chips(w_mine))
-    )
+    output = call(
+        place_kernel, sds((h_loc, nodes), BF), [], (mec,), (o_parts[0], *mixed[:0:-1]), nbytes=h_loc * nodes * 4
+    )
+    w_hop, output = lax.optimization_barrier((over_chips(w_mine), output))
+    w_pair = call(pair_kernel, sds((2, w_rows, h_loc), F32), [], (mer,), (w_mine, w_hop))
     w_chips = [w_pair] + [swap(w_pair, "row", n_row, 2 * e) for e in range(1, n_chip)]
 
     input_grad = call(
@@ -588,9 +597,6 @@
         (mer,),
         tuple(w_chips),
         nbytes=n_f * h_loc * 8,
-    )
-    output = call(
-        place_kernel, sds((h_loc, nodes), BF), [], (mec,), (o_parts[0], *mixed[1:]), nbytes=h_loc * nodes * 4
     )
     return output, input_grad, weight_grad
 

time: 91.2 us -> 88.1 us (0.966)
  waiting for transfers between devices: 25.5 us -> 23.2 us
  Pallas kernels: 24.3 us -> 22.2 us
    ppermute x33, waiting for transfers between devices: 25.5 us -> 23.2 us  [swap(): return lax.ppermute(x, axis, [(i, i ^ k) for i in range(n)])]
    pallas_call x19 -> x20, Pallas kernels: 20.8 us -> 18.7 us  [call(): pl.pallas_call(kernel, out_shape=outs, in_specs=[SM] * len(smem) + [VM] *...]
  transfers between devices with their start and end apart: 33 -> 33, of which waited for: 8 -> 11; matrix products, arithmetic and copies ran while one was open for 0% -> 0% of each run, Pallas kernels for 23% -> 21%
where the time goes in v5:
time: 88.1 us; the launch traced here: 87.5 us
  starting transfers between devices  39.8 us (45%)
  waiting for transfers between devices  23.2 us (26%)
  Pallas kernels  22.2 us (25%)
  between operations  1.6 us (2%)
    ppermute x33, starting transfers between devices, swap(): return lax.ppermute(x, axis, [(i, i ^ k) for i in range(n)])  39.8 us
    ppermute x33, waiting for transfers between devices, swap(): return lax.ppermute(x, axis, [(i, i ^ k) for i in range(n)])  23.2 us
    pallas_call x20, Pallas kernels, call(): pl.pallas_call(kernel, out_shape=outs, in_specs=[SM] * len(smem) + [VM] *...  18.7 us
    pallas_call x1, Pallas kernels, shards(): pl.pallas_call(load_kernel, out_shape=sds(tile_values.shape, BF), in_spec...  3.47 us
  transfers between devices with their start and end apart: 33, of which 11 were waited for; matrix products, arithmetic and copies ran while one was open for 0% of the time, Pallas kernels for 21%

profile of v5, /device:TPU:0, one launch (start us, length us, event | category | flops | bytes accessed | tf_op | source)
XLA Modules:
  0.0 87.5 jit_solution(751406097790812045)
XLA Ops:
  2.8 3.5 %collective-permute-start.2 = (s32[8,128]{1,0:T(8,128)S(1)}, s32[8,128]{1,0:T(8,128)S(1)}, u32[]{:S(2)}, u32[]{:S(2)}) collective-permute-start(s32[8,128]{1,0:T(8,128)S(1)} %shard_map.94), channel_id=1, source_target_pairs={{0,24},{4,28},{8,16},{12,20},{16,8},{20,12},{24,0},{28,4},{1,25},{... | collective-permute-start | bytes 12296 | tf_op jit(solution)/shard_map/ppermute | solution.py:33
  7.0 3.5 %shard_map.96.tiles_ref = bf16[256,128,128]{2,1,0:T(8,128)(2,1)S(1)} custom-call(bf16[256,128,128]{2,1,0:T(8,128)(2,1)} %in_ref), custom_call_target="tpu_custom_call" | custom-call | bytes 8388608 | tf_op jit(solution)/shard_map/pallas_call | solution.py:422
  11.5 2.0 %collective-permute-start.4 = (bf16[8,128,128]{2,1,0:T(8,128)(2,1)S(1)}, bf16[8,128,128]{2,1,0:T(8,128)(2,1)S(1)}, u32[]{:S(2)}, u32[]{:S(2)}) collective-permute-start(bf16[8,128,128]{2,1,0:T(8,128)(2,1)S(1)} %get-tuple-element.86), channel_id=1, source_target_pairs={{0,8},{4,12},{8,0},{12,4},{16,24},{20,28},{24,16},{28,20},{1,9},{5... | collective-permute-start | bytes 786440 | tf_op jit(solution)/shard_map/ppermute | solution.py:33
  15.2 4.1 %collective-permute-start.11 = (bf16[128,512]{1,0:T(8,128)(2,1)S(1)}, bf16[128,512]{1,0:T(8,128)(2,1)S(1)}, u32[]{:S(2)}, u32[]{:S(2)}) collective-permute-start(bf16[128,512]{1,0:T(8,128)(2,1)S(1)} %get-tuple-element.106), channel_id=1, source_target_pairs={{0,3},{1,2},{2,1},{3,0},{4,7},{5,6},{6,5},{7,4},{8,11},{9,10},{10,... | collective-permute-start | bytes 393224 | tf_op jit(solution)/shard_map/ppermute | solution.py:33
  19.2 1.5 %shard_map.98.list_ref = s32[8,384]{1,0:T(8,128)S(1)} custom-call(s32[1]{0:T(128)S(6)} %copy.14.count_ref, s32[1]{0:T(128)} %bitcast.me_ref.mer_ref, s32[1,256]{1,0:T(1,128)S(1)} %copy-done.4, s32[1,256]{1,0:T(1,128)S(1)} %copy-done.5), custom_call_target="tpu_custom_call" | custom-call | tf_op jit(solution)/shard_map/pallas_call | solution.py:21
  20.8 2.0 %shard_map.100.refs_3_ = f32[16,128,128]{2,1,0:T(8,128)S(1)} custom-call(s32[8,384]{1,0:T(8,128)S(1)} %shard_map.98.list_ref, bf16[256,128,128]{2,1,0:T(8,128)(2,1)S(1)} %shard_map.96.tiles_ref, bf16[33,128,128]{2,1,0:T(8,128)(2,1)S(1)} %shard_map.95.refs_3_.x_ref), custom_call_target="tpu_custom_call" | custom-call | flops 1073741824 | bytes 8388608 | tf_op jit(solution)/shard_map/pallas_call | solution.py:21
  23.6 3.1 %collective-permute-done.5.refs_1_ = bf16[8,128,128]{2,1,0:T(8,128)(2,1)S(1)} collective-permute-done((bf16[8,128,128]{2,1,0:T(8,128)(2,1)S(1)}, bf16[8,128,128]{2,1,0:T(8,128)(2,1)S(1)}, u32[]{:S(2)}, u32[]{:S(2)}) %collective-permute-start.5) | collective-permute-done | bytes 262176 | tf_op jit(solution)/shard_map/ppermute | solution.py:33
  26.7 2.2 %shard_map.101 = (bf16[128,512]{1,0:T(8,128)(2,1)S(1)}, bf16[128,512]{1,0:T(8,128)(2,1)S(1)}, bf16[128,512]{1,0:T(8,128)(2,1)S(1)}, bf16[128,512]{1,0:T(8,128)(2,1)S(1)}) custom-call(s32[8,384]{1,0:T(8,128)S(1)} %shard_map.98.list_ref, s32[1]{0:T(128)} %bitcast.1.me_ref.mec_ref, bf16[256,128,128]{2,1,0:T(8,128)(2,1)S(1)} %shard_map.96.tiles_ref, ...), custom_call_target="tpu_custom_call" | custom-call | flops 1073741824 | bytes 8388608 | tf_op jit(solution)/shard_map/pallas_call | solution.py:21
  28.9 3.7 %collective-permute-start.8 = (bf16[128,512]{1,0:T(8,128)(2,1)S(1)}, bf16[128,512]{1,0:T(8,128)(2,1)S(1)}, u32[]{:S(2)}, u32[]{:S(2)}) collective-permute-start(bf16[128,512]{1,0:T(8,128)(2,1)S(1)} %get-tuple-element.102), channel_id=1, source_target_pairs={{0,3},{1,2},{2,1},{3,0},{4,7},{5,6},{6,5},{7,4},{8,11},{9,10},{10,... | collective-permute-start | bytes 393224 | tf_op jit(solution)/shard_map/ppermute | solution.py:33
  33.5 3.1 %collective-permute-done.8.refs_0_ = bf16[128,512]{1,0:T(8,128)(2,1)S(1)} collective-permute-done((bf16[128,512]{1,0:T(8,128)(2,1)S(1)}, bf16[128,512]{1,0:T(8,128)(2,1)S(1)}, u32[]{:S(2)}, u32[]{:S(2)}) %collective-permute-start.8) | collective-permute-done | bytes 131104 | tf_op jit(solution)/shard_map/ppermute | solution.py:33
  36.6 5.6 %collective-permute-done.9.refs_1_ = bf16[128,512]{1,0:T(8,128)(2,1)S(1)} collective-permute-done((bf16[128,512]{1,0:T(8,128)(2,1)S(1)}, bf16[128,512]{1,0:T(8,128)(2,1)S(1)}, u32[]{:S(2)}, u32[]{:S(2)}) %collective-permute-start.9) | collective-permute-done | bytes 131104 | tf_op jit(solution)/shard_map/ppermute | solution.py:33
  43.5 2.5 %collective-permute-start.14 = (bf16[128,512]{1,0:T(8,128)(2,1)S(1)}, bf16[128,512]{1,0:T(8,128)(2,1)S(1)}, u32[]{:S(2)}, u32[]{:S(2)}) collective-permute-start(bf16[128,512]{1,0:T(8,128)(2,1)S(1)} %get-tuple-element.110), channel_id=1, source_target_pairs={{0,3},{1,2},{2,1},{3,0},{4,7},{5,6},{6,5},{7,4},{8,11},{9,10},{10,... | collective-permute-start | bytes 393224 | tf_op jit(solution)/shard_map/ppermute | solution.py:33
  46.0 2.0 %collective-permute-start.16 = (bf16[128,512]{1,0:T(8,128)(2,1)S(1)}, bf16[128,512]{1,0:T(8,128)(2,1)S(1)}, u32[]{:S(2)}, u32[]{:S(2)}) collective-permute-start(bf16[128,512]{1,0:T(8,128)(2,1)S(1)} %get-tuple-element.112), channel_id=1, source_target_pairs={{0,1},{1,0},{2,3},{3,2},{4,5},{5,4},{6,7},{7,6},{8,9},{9,8},{10,11... | collective-permute-start | bytes 393224 | tf_op jit(solution)/shard_map/ppermute | solution.py:33
  49.3 3.1 %collective-permute-start.18 = (bf16[64,512]{1,0:T(8,128)(2,1)S(1)}, bf16[64,512]{1,0:T(8,128)(2,1)S(1)}, u32[]{:S(2)}, u32[]{:S(2)}) collective-permute-start(bf16[64,512]{1,0:T(8,128)(2,1)S(1)} %get-tuple-element.115), channel_id=1, source_target_pairs={{0,24},{4,28},{8,16},{12,20},{16,8},{20,12},{24,0},{28,4},{1,25},{... | collective-permute-start | bytes 196616 | tf_op jit(solution)/shard_map/ppermute | solution.py:33
  53.7 3.2 %collective-permute-done.15.refs_1_ = bf16[128,512]{1,0:T(8,128)(2,1)S(1)} collective-permute-done((bf16[128,512]{1,0:T(8,128)(2,1)S(1)}, bf16[128,512]{1,0:T(8,128)(2,1)S(1)}, u32[]{:S(2)}, u32[]{:S(2)}) %collective-permute-start.15) | collective-permute-done | bytes 131104 | tf_op jit(solution)/shard_map/ppermute | solution.py:33
  57.9 2.3 %collective-permute-start.24 = (bf16[144,512]{1,0:T(8,128)(2,1)S(1)}, bf16[144,512]{1,0:T(8,128)(2,1)S(1)}, u32[]{:S(2)}, u32[]{:S(2)}) collective-permute-start(bf16[144,512]{1,0:T(8,128)(2,1)S(1)} %get-tuple-element.132), channel_id=1, source_target_pairs={{0,3},{1,2},{2,1},{3,0},{4,7},{5,6},{6,5},{7,4},{8,11},{9,10},{10,... | collective-permute-start | bytes 442376 | tf_op jit(solution)/shard_map/ppermute | solution.py:33
  60.2 2.6 %shard_map.106 = (bf16[128,2048]{1,0:T(8,128)(2,1)S(1)}, bf16[4,128,128]{2,1,0:T(8,128)(2,1)S(1)}, bf16[8,128,128]{2,1,0:T(8,128)(2,1)S(1)}, bf16[8,128,128]{2,1,0:T(8,128)(2,1)S(1)}, bf16[8,128,128]{2,1,0:T(8,128)(2,1)S(1)}) custom-call(s32[8,384]{1,0:T(8,128)S(1)} %shard_map.98.list_ref, s32[1]{0:T(128)} %bitcast.1.me_ref.mec_ref, s32[1]{0:T(128)} %bitcast.me_ref.mer_ref, ...), custom_call_target="tpu_custom_call" | custom-call | flops 1073741824 | bytes 8388608 | tf_op jit(solution)/shard_map/pallas_call | solution.py:21
  62.8 2.3 %collective-permute-start.21 = (bf16[8,128,128]{2,1,0:T(8,128)(2,1)S(1)}, bf16[8,128,128]{2,1,0:T(8,128)(2,1)S(1)}, u32[]{:S(2)}, u32[]{:S(2)}) collective-permute-start(bf16[8,128,128]{2,1,0:T(8,128)(2,1)S(1)} %get-tuple-element.123), channel_id=1, source_target_pairs={{0,24},{4,28},{8,16},{12,20},{16,8},{20,12},{24,0},{28,4},{1,25},{... | collective-permute-start | bytes 786440 | tf_op jit(solution)/shard_map/ppermute | solution.py:33
  67.4 2.4 %collective-permute-start.26 = (bf16[144,512]{1,0:T(8,128)(2,1)S(1)}, bf16[144,512]{1,0:T(8,128)(2,1)S(1)}, u32[]{:S(2)}, u32[]{:S(2)}) collective-permute-start(bf16[144,512]{1,0:T(8,128)(2,1)S(1)} %get-tuple-element.134), channel_id=1, source_target_pairs={{0,1},{1,0},{2,3},{3,2},{4,5},{5,4},{6,7},{7,6},{8,9},{9,8},{10,11... | collective-permute-start | bytes 442376 | tf_op jit(solution)/shard_map/ppermute | solution.py:33
  69.8 2.1 %shard_map.107.base_ref = f32[16,128,128]{2,1,0:T(8,128)S(1)} custom-call(s32[8,384]{1,0:T(8,128)S(1)} %shard_map.98.list_ref, bf16[256,128,128]{2,1,0:T(8,128)(2,1)S(1)} %shard_map.96.tiles_ref, bf16[128,2048]{1,0:T(8,128)(2,1)S(1)} %get-tuple-element.126.wide_ref), custom_call_target="tpu_custom_call" | custom-call | flops 1073741824 | bytes 8388608 | tf_op jit(solution)/shard_map/pallas_call | solution.py:21
  71.9 2.7 %collective-permute-done.25.refs_1_.refs_2_ = bf16[144,512]{1,0:T(8,128)(2,1)S(1)} collective-permute-done((bf16[144,512]{1,0:T(8,128)(2,1)S(1)}, bf16[144,512]{1,0:T(8,128)(2,1)S(1)}, u32[]{:S(2)}, u32[]{:S(2)}) %collective-permute-start.25) | collective-permute-done | bytes 147488 | tf_op jit(solution)/shard_map/ppermute | solution.py:33
  74.6 2.6 %collective-permute-done.22.refs_1_ = bf16[8,128,128]{2,1,0:T(8,128)(2,1)S(1)} collective-permute-done((bf16[8,128,128]{2,1,0:T(8,128)(2,1)S(1)}, bf16[8,128,128]{2,1,0:T(8,128)(2,1)S(1)}, u32[]{:S(2)}, u32[]{:S(2)}) %collective-permute-start.22) | collective-permute-done | bytes 262176 | tf_op jit(solution)/shard_map/ppermute | solution.py:33
  79.2 1.8 %collective-permute-start.30 = (f32[2,64,128]{2,1,0:T(8,128)S(1)}, f32[2,64,128]{2,1,0:T(8,128)S(1)}, u32[]{:S(2)}, u32[]{:S(2)}) collective-permute-start(f32[2,64,128]{2,1,0:T(8,128)S(1)} %shard_map.111.refs_0_), channel_id=1, source_target_pairs={{0,24},{4,28},{8,16},{12,20},{16,8},{20,12},{24,0},{28,4},{1,25},{... | collective-permute-start | bytes 196616 | tf_op jit(solution)/shard_map/ppermute | solution.py:33
  82.7 1.8 %shard_map.113 = bf16[128,2048]{1,0:T(8,128)(2,1)} custom-call(s32[1]{0:T(128)} %bitcast.me_ref.mer_ref, s32[8,128]{1,0:T(8,128)S(1)} %shard_map.99.table_ref, f32[16,128,128]{2,1,0:T(8,128)S(1)} %shard_map.107.base_ref, bf16[4,128,128]{2,1,0:T(8,128)(2,1)S(1)} %collective-permute-done.31.sib_ref, bf16[12,128,128]{2,1,0:T(8,128)(2,1)S(1)} %collective-permute-done.32.fwd_ref, ...), custom_call_target="tpu_custom_call" | custom-call | bytes 2097152 | tf_op jit(solution)/shard_map/pallas_call | solution.py:21
  (81 shorter events, 20.5 us)
Async XLA Ops:
  0.6 9.8 %collective-permute-start.3 = (bf16[128,2048]{1,0:T(8,128)(2,1)}, bf16[128,2048]{1,0:T(8,128)(2,1)S(1)}, u32[]{:S(2)}, u32[]{:S(2)}) collective-permute-start(bf16[128,2048]{1,0:T(8,128)(2,1)} %feat_ref.1), channel_id=1, source_target_pairs={{0,4},{4,0},{8,12},{12,8},{16,20},{20,16},{24,28},{28,24},{1,5},{5... | collective-permute-start | bytes 1572872 | tf_op jit(solution)/shard_map/ppermute | solution.py:33
  2.8 7.9 %collective-permute-start.2 = (s32[8,128]{1,0:T(8,128)S(1)}, s32[8,128]{1,0:T(8,128)S(1)}, u32[]{:S(2)}, u32[]{:S(2)}) collective-permute-start(s32[8,128]{1,0:T(8,128)S(1)} %shard_map.94), channel_id=1, source_target_pairs={{0,24},{4,28},{8,16},{12,20},{16,8},{20,12},{24,0},{28,4},{1,25},{... | collective-permute-start | bytes 12296 | tf_op jit(solution)/shard_map/ppermute | solution.py:33
  11.5 11.4 %collective-permute-start.4 = (bf16[8,128,128]{2,1,0:T(8,128)(2,1)S(1)}, bf16[8,128,128]{2,1,0:T(8,128)(2,1)S(1)}, u32[]{:S(2)}, u32[]{:S(2)}) collective-permute-start(bf16[8,128,128]{2,1,0:T(8,128)(2,1)S(1)} %get-tuple-element.86), channel_id=1, source_target_pairs={{0,8},{4,12},{8,0},{12,4},{16,24},{20,28},{24,16},{28,20},{1,9},{5... | collective-permute-start | bytes 786440 | tf_op jit(solution)/shard_map/ppermute | solution.py:33
  13.5 13.2 %collective-permute-start.5 = (bf16[8,128,128]{2,1,0:T(8,128)(2,1)S(1)}, bf16[8,128,128]{2,1,0:T(8,128)(2,1)S(1)}, u32[]{:S(2)}, u32[]{:S(2)}) collective-permute-start(bf16[8,128,128]{2,1,0:T(8,128)(2,1)S(1)} %get-tuple-element.87), channel_id=1, source_target_pairs={{0,16},{4,20},{8,24},{12,28},{16,0},{20,4},{24,8},{28,12},{1,17},{... | collective-permute-start | bytes 786440 | tf_op jit(solution)/shard_map/ppermute | solution.py:33
  15.0 11.7 %collective-permute-start.6 = (bf16[8,128,128]{2,1,0:T(8,128)(2,1)S(1)}, bf16[8,128,128]{2,1,0:T(8,128)(2,1)S(1)}, u32[]{:S(2)}, u32[]{:S(2)}) collective-permute-start(bf16[8,128,128]{2,1,0:T(8,128)(2,1)S(1)} %get-tuple-element.88), channel_id=1, source_target_pairs={{0,24},{4,28},{8,16},{12,20},{16,8},{20,12},{24,0},{28,4},{1,25},{... | collective-permute-start | bytes 786440 | tf_op jit(solution)/shard_map/ppermute | solution.py:33
  15.1 7.8 %collective-permute-start.7 = (s32[32,128]{1,0:T(8,128)S(1)}, s32[32,128]{1,0:T(8,128)S(1)}, u32[]{:S(2)}, u32[]{:S(2)}) collective-permute-start(s32[32,128]{1,0:T(8,128)S(1)} %pad_add_fusion), channel_id=1, source_target_pairs={{0,4},{4,0},{8,12},{12,8},{16,20},{20,16},{24,28},{28,24},{1,5},{5... | collective-permute-start | bytes 49160 | tf_op jit(solution)/shard_map/ppermute | solution.py:33
  15.2 17.4 %collective-permute-start.11 = (bf16[128,512]{1,0:T(8,128)(2,1)S(1)}, bf16[128,512]{1,0:T(8,128)(2,1)S(1)}, u32[]{:S(2)}, u32[]{:S(2)}) collective-permute-start(bf16[128,512]{1,0:T(8,128)(2,1)S(1)} %get-tuple-element.106), channel_id=1, source_target_pairs={{0,3},{1,2},{2,1},{3,0},{4,7},{5,6},{6,5},{7,4},{8,11},{9,10},{10,... | collective-permute-start | bytes 393224 | tf_op jit(solution)/shard_map/ppermute | solution.py:33
  22.8 10.7 %collective-permute-start.12 = (bf16[128,512]{1,0:T(8,128)(2,1)S(1)}, bf16[128,512]{1,0:T(8,128)(2,1)S(1)}, u32[]{:S(2)}, u32[]{:S(2)}) collective-permute-start(bf16[128,512]{1,0:T(8,128)(2,1)S(1)} %get-tuple-element.107), channel_id=1, source_target_pairs={{0,2},{1,3},{2,0},{3,1},{4,6},{5,7},{6,4},{7,5},{8,10},{9,11},{10,... | collective-permute-start | bytes 393224 | tf_op jit(solution)/shard_map/ppermute | solution.py:33
  23.0 10.6 %collective-permute-start.13 = (bf16[128,512]{1,0:T(8,128)(2,1)S(1)}, bf16[128,512]{1,0:T(8,128)(2,1)S(1)}, u32[]{:S(2)}, u32[]{:S(2)}) collective-permute-start(bf16[128,512]{1,0:T(8,128)(2,1)S(1)} %get-tuple-element.108), channel_id=1, source_target_pairs={{0,1},{1,0},{2,3},{3,2},{4,5},{5,4},{6,7},{7,6},{8,9},{9,8},{10,11... | collective-permute-start | bytes 393224 | tf_op jit(solution)/shard_map/ppermute | solution.py:33
  28.9 7.7 %collective-permute-start.8 = (bf16[128,512]{1,0:T(8,128)(2,1)S(1)}, bf16[128,512]{1,0:T(8,128)(2,1)S(1)}, u32[]{:S(2)}, u32[]{:S(2)}) collective-permute-start(bf16[128,512]{1,0:T(8,128)(2,1)S(1)} %get-tuple-element.102), channel_id=1, source_target_pairs={{0,3},{1,2},{2,1},{3,0},{4,7},{5,6},{6,5},{7,4},{8,11},{9,10},{10,... | collective-permute-start | bytes 393224 | tf_op jit(solution)/shard_map/ppermute | solution.py:33
  32.5 9.7 %collective-permute-start.9 = (bf16[128,512]{1,0:T(8,128)(2,1)S(1)}, bf16[128,512]{1,0:T(8,128)(2,1)S(1)}, u32[]{:S(2)}, u32[]{:S(2)}) collective-permute-start(bf16[128,512]{1,0:T(8,128)(2,1)S(1)} %get-tuple-element.103), channel_id=1, source_target_pairs={{0,2},{1,3},{2,0},{3,1},{4,6},{5,7},{6,4},{7,5},{8,10},{9,11},{10,... | collective-permute-start | bytes 393224 | tf_op jit(solution)/shard_map/ppermute | solution.py:33
  32.5 9.7 %collective-permute-start.10 = (bf16[128,512]{1,0:T(8,128)(2,1)S(1)}, bf16[128,512]{1,0:T(8,128)(2,1)S(1)}, u32[]{:S(2)}, u32[]{:S(2)}) collective-permute-start(bf16[128,512]{1,0:T(8,128)(2,1)S(1)} %get-tuple-element.104), channel_id=1, source_target_pairs={{0,1},{1,0},{2,3},{3,2},{4,5},{5,4},{6,7},{7,6},{8,9},{9,8},{10,11... | collective-permute-start | bytes 393224 | tf_op jit(solution)/shard_map/ppermute | solution.py:33
  43.5 9.3 %collective-permute-start.14 = (bf16[128,512]{1,0:T(8,128)(2,1)S(1)}, bf16[128,512]{1,0:T(8,128)(2,1)S(1)}, u32[]{:S(2)}, u32[]{:S(2)}) collective-permute-start(bf16[128,512]{1,0:T(8,128)(2,1)S(1)} %get-tuple-element.110), channel_id=1, source_target_pairs={{0,3},{1,2},{2,1},{3,0},{4,7},{5,6},{6,5},{7,4},{8,11},{9,10},{10,... | collective-permute-start | bytes 393224 | tf_op jit(solution)/shard_map/ppermute | solution.py:33
  46.0 10.9 %collective-permute-start.15 = (bf16[128,512]{1,0:T(8,128)(2,1)S(1)}, bf16[128,512]{1,0:T(8,128)(2,1)S(1)}, u32[]{:S(2)}, u32[]{:S(2)}) collective-permute-start(bf16[128,512]{1,0:T(8,128)(2,1)S(1)} %get-tuple-element.111), channel_id=1, source_target_pairs={{0,2},{1,3},{2,0},{3,1},{4,6},{5,7},{6,4},{7,5},{8,10},{9,11},{10,... | collective-permute-start | bytes 393224 | tf_op jit(solution)/shard_map/ppermute | solution.py:33
  46.0 10.9 %collective-permute-start.16 = (bf16[128,512]{1,0:T(8,128)(2,1)S(1)}, bf16[128,512]{1,0:T(8,128)(2,1)S(1)}, u32[]{:S(2)}, u32[]{:S(2)}) collective-permute-start(bf16[128,512]{1,0:T(8,128)(2,1)S(1)} %get-tuple-element.112), channel_id=1, source_target_pairs={{0,1},{1,0},{2,3},{3,2},{4,5},{5,4},{6,7},{7,6},{8,9},{9,8},{10,11... | collective-permute-start | bytes 393224 | tf_op jit(solution)/shard_map/ppermute | solution.py:33
  49.3 7.6 %collective-permute-start.18 = (bf16[64,512]{1,0:T(8,128)(2,1)S(1)}, bf16[64,512]{1,0:T(8,128)(2,1)S(1)}, u32[]{:S(2)}, u32[]{:S(2)}) collective-permute-start(bf16[64,512]{1,0:T(8,128)(2,1)S(1)} %get-tuple-element.115), channel_id=1, source_target_pairs={{0,24},{4,28},{8,16},{12,20},{16,8},{20,12},{24,0},{28,4},{1,25},{... | collective-permute-start | bytes 196616 | tf_op jit(solution)/shard_map/ppermute | solution.py:33
  57.9 9.5 %collective-permute-start.24 = (bf16[144,512]{1,0:T(8,128)(2,1)S(1)}, bf16[144,512]{1,0:T(8,128)(2,1)S(1)}, u32[]{:S(2)}, u32[]{:S(2)}) collective-permute-start(bf16[144,512]{1,0:T(8,128)(2,1)S(1)} %get-tuple-element.132), channel_id=1, source_target_pairs={{0,3},{1,2},{2,1},{3,0},{4,7},{5,6},{6,5},{7,4},{8,11},{9,10},{10,... | collective-permute-start | bytes 442376 | tf_op jit(solution)/shard_map/ppermute | solution.py:33
  62.8 11.8 %collective-permute-start.21 = (bf16[8,128,128]{2,1,0:T(8,128)(2,1)S(1)}, bf16[8,128,128]{2,1,0:T(8,128)(2,1)S(1)}, u32[]{:S(2)}, u32[]{:S(2)}) collective-permute-start(bf16[8,128,128]{2,1,0:T(8,128)(2,1)S(1)} %get-tuple-element.123), channel_id=1, source_target_pairs={{0,24},{4,28},{8,16},{12,20},{16,8},{20,12},{24,0},{28,4},{1,25},{... | collective-permute-start | bytes 786440 | tf_op jit(solution)/shard_map/ppermute | solution.py:33
  65.0 12.1 %collective-permute-start.22 = (bf16[8,128,128]{2,1,0:T(8,128)(2,1)S(1)}, bf16[8,128,128]{2,1,0:T(8,128)(2,1)S(1)}, u32[]{:S(2)}, u32[]{:S(2)}) collective-permute-start(bf16[8,128,128]{2,1,0:T(8,128)(2,1)S(1)} %get-tuple-element.124), channel_id=1, source_target_pairs={{0,16},{4,20},{8,24},{12,28},{16,0},{20,4},{24,8},{28,12},{1,17},{... | collective-permute-start | bytes 786440 | tf_op jit(solution)/shard_map/ppermute | solution.py:33
  66.0 11.2 %collective-permute-start.23 = (bf16[8,128,128]{2,1,0:T(8,128)(2,1)S(1)}, bf16[8,128,128]{2,1,0:T(8,128)(2,1)S(1)}, u32[]{:S(2)}, u32[]{:S(2)}) collective-permute-start(bf16[8,128,128]{2,1,0:T(8,128)(2,1)S(1)} %get-tuple-element.125), channel_id=1, source_target_pairs={{0,8},{4,12},{8,0},{12,4},{16,24},{20,28},{24,16},{28,20},{1,9},{5... | collective-permute-start | bytes 786440 | tf_op jit(solution)/shard_map/ppermute | solution.py:33
  67.4 7.2 %collective-permute-start.25 = (bf16[144,512]{1,0:T(8,128)(2,1)S(1)}, bf16[144,512]{1,0:T(8,128)(2,1)S(1)}, u32[]{:S(2)}, u32[]{:S(2)}) collective-permute-start(bf16[144,512]{1,0:T(8,128)(2,1)S(1)} %get-tuple-element.133), channel_id=1, source_target_pairs={{0,2},{1,3},{2,0},{3,1},{4,6},{5,7},{6,4},{7,5},{8,10},{9,11},{10,... | collective-permute-start | bytes 442376 | tf_op jit(solution)/shard_map/ppermute | solution.py:33
  67.4 7.2 %collective-permute-start.26 = (bf16[144,512]{1,0:T(8,128)(2,1)S(1)}, bf16[144,512]{1,0:T(8,128)(2,1)S(1)}, u32[]{:S(2)}, u32[]{:S(2)}) collective-permute-start(bf16[144,512]{1,0:T(8,128)(2,1)S(1)} %get-tuple-element.134), channel_id=1, source_target_pairs={{0,1},{1,0},{2,3},{3,2},{4,5},{5,4},{6,7},{7,6},{8,9},{9,8},{10,11... | collective-permute-start | bytes 442376 | tf_op jit(solution)/shard_map/ppermute | solution.py:33
  77.2 5.5 %collective-permute-start.32 = (bf16[12,128,128]{2,1,0:T(8,128)(2,1)S(1)}, bf16[12,128,128]{2,1,0:T(8,128)(2,1)S(1)}, u32[]{:S(2)}, u32[]{:S(2)}) collective-permute-start(bf16[12,128,128]{2,1,0:T(8,128)(2,1)S(1)} %shard_map.112), channel_id=1, source_target_pairs={{0,4},{4,0},{8,12},{12,8},{16,20},{20,16},{24,28},{28,24},{1,5},{5... | collective-permute-start | bytes 1179656 | tf_op jit(solution)/shard_map/ppermute | solution.py:33
  77.3 5.4 %collective-permute-start.31 = (bf16[4,128,128]{2,1,0:T(8,128)(2,1)S(1)}, bf16[4,128,128]{2,1,0:T(8,128)(2,1)S(1)}, u32[]{:S(2)}, u32[]{:S(2)}) collective-permute-start(bf16[4,128,128]{2,1,0:T(8,128)(2,1)S(1)} %get-tuple-element.140), channel_id=1, source_target_pairs={{0,4},{4,0},{8,12},{12,8},{16,20},{20,16},{24,28},{28,24},{1,5},{5... | collective-permute-start | bytes 393224 | tf_op jit(solution)/shard_map/ppermute | solution.py:33
  (15 other events, 103.3 us)

commit v6 on v5

--- a/solution.py
+++ b/solution.py
@@ -9,7 +9,7 @@
 
 TILE = 128
 SLOT = 4
-UNROLL = 8
+UNROLL = 16
 LOADS = 8
 BF = jnp.bfloat16
 F32 = jnp.float32

time: 88.1 us -> 88 us (level)
  waiting for transfers between devices: 23.2 us -> 25.6 us
  starting transfers between devices: 39.8 us -> 38 us
    ppermute x33, waiting for transfers between devices: 23.2 us -> 25.6 us  [swap(): return lax.ppermute(x, axis, [(i, i ^ k) for i in range(n)])]
    ppermute x33, starting transfers between devices: 39.8 us -> 38 us  [swap(): return lax.ppermute(x, axis, [(i, i ^ k) for i in range(n)])]
  transfers between devices with their start and end apart: 33 -> 33, of which waited for: 11 -> 10; matrix products, arithmetic and copies ran while one was open for 0% -> 0% of each run, Pallas kernels for 21% -> 21%
where the time goes in v6:
time: 88 us; the launch traced here: 87.9 us
  starting transfers between devices  38 us (43%)
  waiting for transfers between devices  25.6 us (29%)
  Pallas kernels  22 us (25%)
  between operations  1.61 us (2%)
    ppermute x33, starting transfers between devices, swap(): return lax.ppermute(x, axis, [(i, i ^ k) for i in range(n)])  38 us
    ppermute x33, waiting for transfers between devices, swap(): return lax.ppermute(x, axis, [(i, i ^ k) for i in range(n)])  25.6 us
    pallas_call x20, Pallas kernels, call(): pl.pallas_call(kernel, out_shape=outs, in_specs=[SM] * len(smem) + [VM] *...  18.5 us
    pallas_call x1, Pallas kernels, shards(): pl.pallas_call(load_kernel, out_shape=sds(tile_values.shape, BF), in_spec...  3.47 us
  transfers between devices with their start and end apart: 33, of which 10 were waited for; matrix products, arithmetic and copies ran while one was open for 0% of the time, Pallas kernels for 21%

profile of v6, /device:TPU:0, one launch (start us, length us, event | category | flops | bytes accessed | tf_op | source)
XLA Modules:
  0.0 87.9 jit_solution(2930949232744854999)
XLA Ops:
  2.8 3.5 %collective-permute-start.2 = (s32[8,128]{1,0:T(8,128)S(1)}, s32[8,128]{1,0:T(8,128)S(1)}, u32[]{:S(2)}, u32[]{:S(2)}) collective-permute-start(s32[8,128]{1,0:T(8,128)S(1)} %shard_map.94), channel_id=1, source_target_pairs={{0,24},{4,28},{8,16},{12,20},{16,8},{20,12},{24,0},{28,4},{1,25},{... | collective-permute-start | bytes 12296 | tf_op jit(solution)/shard_map/ppermute | solution.py:33
  7.0 3.5 %shard_map.96.tiles_ref = bf16[256,128,128]{2,1,0:T(8,128)(2,1)S(1)} custom-call(bf16[256,128,128]{2,1,0:T(8,128)(2,1)} %in_ref), custom_call_target="tpu_custom_call" | custom-call | bytes 8388608 | tf_op jit(solution)/shard_map/pallas_call | solution.py:422
  11.5 2.0 %collective-permute-start.4 = (bf16[8,128,128]{2,1,0:T(8,128)(2,1)S(1)}, bf16[8,128,128]{2,1,0:T(8,128)(2,1)S(1)}, u32[]{:S(2)}, u32[]{:S(2)}) collective-permute-start(bf16[8,128,128]{2,1,0:T(8,128)(2,1)S(1)} %get-tuple-element.86), channel_id=1, source_target_pairs={{0,8},{4,12},{8,0},{12,4},{16,24},{20,28},{24,16},{28,20},{1,9},{5... | collective-permute-start | bytes 786440 | tf_op jit(solution)/shard_map/ppermute | solution.py:33
  15.2 4.1 %collective-permute-start.11 = (bf16[128,512]{1,0:T(8,128)(2,1)S(1)}, bf16[128,512]{1,0:T(8,128)(2,1)S(1)}, u32[]{:S(2)}, u32[]{:S(2)}) collective-permute-start(bf16[128,512]{1,0:T(8,128)(2,1)S(1)} %get-tuple-element.106), channel_id=1, source_target_pairs={{0,3},{1,2},{2,1},{3,0},{4,7},{5,6},{6,5},{7,4},{8,11},{9,10},{10,... | collective-permute-start | bytes 393224 | tf_op jit(solution)/shard_map/ppermute | solution.py:33
  19.2 1.5 %shard_map.98.list_ref = s32[8,384]{1,0:T(8,128)S(1)} custom-call(s32[1]{0:T(128)S(6)} %copy.14.count_ref, s32[1]{0:T(128)} %bitcast.me_ref.mer_ref, s32[1,256]{1,0:T(1,128)S(1)} %copy-done.4, s32[1,256]{1,0:T(1,128)S(1)} %copy-done.5), custom_call_target="tpu_custom_call" | custom-call | tf_op jit(solution)/shard_map/pallas_call | solution.py:21
  20.8 2.2 %shard_map.100.refs_3_ = f32[16,128,128]{2,1,0:T(8,128)S(1)} custom-call(s32[8,384]{1,0:T(8,128)S(1)} %shard_map.98.list_ref, bf16[256,128,128]{2,1,0:T(8,128)(2,1)S(1)} %shard_map.96.tiles_ref, bf16[33,128,128]{2,1,0:T(8,128)(2,1)S(1)} %shard_map.95.refs_3_.x_ref), custom_call_target="tpu_custom_call" | custom-call | flops 1073741824 | bytes 8388608 | tf_op jit(solution)/shard_map/pallas_call | solution.py:21
  23.7 3.0 %collective-permute-done.5.refs_1_ = bf16[8,128,128]{2,1,0:T(8,128)(2,1)S(1)} collective-permute-done((bf16[8,128,128]{2,1,0:T(8,128)(2,1)S(1)}, bf16[8,128,128]{2,1,0:T(8,128)(2,1)S(1)}, u32[]{:S(2)}, u32[]{:S(2)}) %collective-permute-start.5) | collective-permute-done | bytes 262176 | tf_op jit(solution)/shard_map/ppermute | solution.py:33
  26.7 1.8 %shard_map.101 = (bf16[128,512]{1,0:T(8,128)(2,1)S(1)}, bf16[128,512]{1,0:T(8,128)(2,1)S(1)}, bf16[128,512]{1,0:T(8,128)(2,1)S(1)}, bf16[128,512]{1,0:T(8,128)(2,1)S(1)}) custom-call(s32[8,384]{1,0:T(8,128)S(1)} %shard_map.98.list_ref, s32[1]{0:T(128)} %bitcast.1.me_ref.mec_ref, bf16[256,128,128]{2,1,0:T(8,128)(2,1)S(1)} %shard_map.96.tiles_ref, ...), custom_call_target="tpu_custom_call" | custom-call | flops 1073741824 | bytes 8388608 | tf_op jit(solution)/shard_map/pallas_call | solution.py:21
  28.5 3.7 %collective-permute-start.8 = (bf16[128,512]{1,0:T(8,128)(2,1)S(1)}, bf16[128,512]{1,0:T(8,128)(2,1)S(1)}, u32[]{:S(2)}, u32[]{:S(2)}) collective-permute-start(bf16[128,512]{1,0:T(8,128)(2,1)S(1)} %get-tuple-element.102), channel_id=1, source_target_pairs={{0,3},{1,2},{2,1},{3,0},{4,7},{5,6},{6,5},{7,4},{8,11},{9,10},{10,... | collective-permute-start | bytes 393224 | tf_op jit(solution)/shard_map/ppermute | solution.py:33
  33.2 3.3 %collective-permute-done.8.refs_0_ = bf16[128,512]{1,0:T(8,128)(2,1)S(1)} collective-permute-done((bf16[128,512]{1,0:T(8,128)(2,1)S(1)}, bf16[128,512]{1,0:T(8,128)(2,1)S(1)}, u32[]{:S(2)}, u32[]{:S(2)}) %collective-permute-start.8) | collective-permute-done | bytes 131104 | tf_op jit(solution)/shard_map/ppermute | solution.py:33
  36.5 5.7 %collective-permute-done.9.refs_1_ = bf16[128,512]{1,0:T(8,128)(2,1)S(1)} collective-permute-done((bf16[128,512]{1,0:T(8,128)(2,1)S(1)}, bf16[128,512]{1,0:T(8,128)(2,1)S(1)}, u32[]{:S(2)}, u32[]{:S(2)}) %collective-permute-start.9) | collective-permute-done | bytes 131104 | tf_op jit(solution)/shard_map/ppermute | solution.py:33
  43.5 2.5 %collective-permute-start.14 = (bf16[128,512]{1,0:T(8,128)(2,1)S(1)}, bf16[128,512]{1,0:T(8,128)(2,1)S(1)}, u32[]{:S(2)}, u32[]{:S(2)}) collective-permute-start(bf16[128,512]{1,0:T(8,128)(2,1)S(1)} %get-tuple-element.110), channel_id=1, source_target_pairs={{0,3},{1,2},{2,1},{3,0},{4,7},{5,6},{6,5},{7,4},{8,11},{9,10},{10,... | collective-permute-start | bytes 393224 | tf_op jit(solution)/shard_map/ppermute | solution.py:33
  46.0 1.9 %collective-permute-start.16 = (bf16[128,512]{1,0:T(8,128)(2,1)S(1)}, bf16[128,512]{1,0:T(8,128)(2,1)S(1)}, u32[]{:S(2)}, u32[]{:S(2)}) collective-permute-start(bf16[128,512]{1,0:T(8,128)(2,1)S(1)} %get-tuple-element.112), channel_id=1, source_target_pairs={{0,1},{1,0},{2,3},{3,2},{4,5},{5,4},{6,7},{7,6},{8,9},{9,8},{10,11... | collective-permute-start | bytes 393224 | tf_op jit(solution)/shard_map/ppermute | solution.py:33
  49.3 3.2 %collective-permute-start.18 = (bf16[64,512]{1,0:T(8,128)(2,1)S(1)}, bf16[64,512]{1,0:T(8,128)(2,1)S(1)}, u32[]{:S(2)}, u32[]{:S(2)}) collective-permute-start(bf16[64,512]{1,0:T(8,128)(2,1)S(1)} %get-tuple-element.115), channel_id=1, source_target_pairs={{0,24},{4,28},{8,16},{12,20},{16,8},{20,12},{24,0},{28,4},{1,25},{... | collective-permute-start | bytes 196616 | tf_op jit(solution)/shard_map/ppermute | solution.py:33
  53.3 3.6 %collective-permute-done.15.refs_1_ = bf16[128,512]{1,0:T(8,128)(2,1)S(1)} collective-permute-done((bf16[128,512]{1,0:T(8,128)(2,1)S(1)}, bf16[128,512]{1,0:T(8,128)(2,1)S(1)}, u32[]{:S(2)}, u32[]{:S(2)}) %collective-permute-start.15) | collective-permute-done | bytes 131104 | tf_op jit(solution)/shard_map/ppermute | solution.py:33
  57.8 2.4 %collective-permute-start.24 = (bf16[144,512]{1,0:T(8,128)(2,1)S(1)}, bf16[144,512]{1,0:T(8,128)(2,1)S(1)}, u32[]{:S(2)}, u32[]{:S(2)}) collective-permute-start(bf16[144,512]{1,0:T(8,128)(2,1)S(1)} %get-tuple-element.132), channel_id=1, source_target_pairs={{0,3},{1,2},{2,1},{3,0},{4,7},{5,6},{6,5},{7,4},{8,11},{9,10},{10,... | collective-permute-start | bytes 442376 | tf_op jit(solution)/shard_map/ppermute | solution.py:33
  60.2 2.4 %shard_map.106 = (bf16[128,2048]{1,0:T(8,128)(2,1)S(1)}, bf16[4,128,128]{2,1,0:T(8,128)(2,1)S(1)}, bf16[8,128,128]{2,1,0:T(8,128)(2,1)S(1)}, bf16[8,128,128]{2,1,0:T(8,128)(2,1)S(1)}, bf16[8,128,128]{2,1,0:T(8,128)(2,1)S(1)}) custom-call(s32[8,384]{1,0:T(8,128)S(1)} %shard_map.98.list_ref, s32[1]{0:T(128)} %bitcast.1.me_ref.mec_ref, s32[1]{0:T(128)} %bitcast.me_ref.mer_ref, ...), custom_call_target="tpu_custom_call" | custom-call | flops 1073741824 | bytes 8388608 | tf_op jit(solution)/shard_map/pallas_call | solution.py:21
  62.6 2.1 %collective-permute-start.21 = (bf16[8,128,128]{2,1,0:T(8,128)(2,1)S(1)}, bf16[8,128,128]{2,1,0:T(8,128)(2,1)S(1)}, u32[]{:S(2)}, u32[]{:S(2)}) collective-permute-start(bf16[8,128,128]{2,1,0:T(8,128)(2,1)S(1)} %get-tuple-element.123), channel_id=1, source_target_pairs={{0,24},{4,28},{8,16},{12,20},{16,8},{20,12},{24,0},{28,4},{1,25},{... | collective-permute-start | bytes 786440 | tf_op jit(solution)/shard_map/ppermute | solution.py:33
  66.2 2.0 %collective-permute-start.26 = (bf16[144,512]{1,0:T(8,128)(2,1)S(1)}, bf16[144,512]{1,0:T(8,128)(2,1)S(1)}, u32[]{:S(2)}, u32[]{:S(2)}) collective-permute-start(bf16[144,512]{1,0:T(8,128)(2,1)S(1)} %get-tuple-element.134), channel_id=1, source_target_pairs={{0,1},{1,0},{2,3},{3,2},{4,5},{5,4},{6,7},{7,6},{8,9},{9,8},{10,11... | collective-permute-start | bytes 442376 | tf_op jit(solution)/shard_map/ppermute | solution.py:33
  68.2 2.3 %shard_map.107.base_ref = f32[16,128,128]{2,1,0:T(8,128)S(1)} custom-call(s32[8,384]{1,0:T(8,128)S(1)} %shard_map.98.list_ref, bf16[256,128,128]{2,1,0:T(8,128)(2,1)S(1)} %shard_map.96.tiles_ref, bf16[128,2048]{1,0:T(8,128)(2,1)S(1)} %get-tuple-element.126.wide_ref), custom_call_target="tpu_custom_call" | custom-call | flops 1073741824 | bytes 8388608 | tf_op jit(solution)/shard_map/pallas_call | solution.py:21
  70.4 4.8 %collective-permute-done.25.refs_1_.refs_2_ = bf16[144,512]{1,0:T(8,128)(2,1)S(1)} collective-permute-done((bf16[144,512]{1,0:T(8,128)(2,1)S(1)}, bf16[144,512]{1,0:T(8,128)(2,1)S(1)}, u32[]{:S(2)}, u32[]{:S(2)}) %collective-permute-start.25) | collective-permute-done | bytes 147488 | tf_op jit(solution)/shard_map/ppermute | solution.py:33
  75.4 2.5 %collective-permute-done.22.refs_1_ = bf16[8,128,128]{2,1,0:T(8,128)(2,1)S(1)} collective-permute-done((bf16[8,128,128]{2,1,0:T(8,128)(2,1)S(1)}, bf16[8,128,128]{2,1,0:T(8,128)(2,1)S(1)}, u32[]{:S(2)}, u32[]{:S(2)}) %collective-permute-start.22) | collective-permute-done | bytes 262176 | tf_op jit(solution)/shard_map/ppermute | solution.py:33
  80.0 1.8 %collective-permute-start.30 = (f32[2,64,128]{2,1,0:T(8,128)S(1)}, f32[2,64,128]{2,1,0:T(8,128)S(1)}, u32[]{:S(2)}, u32[]{:S(2)}) collective-permute-start(f32[2,64,128]{2,1,0:T(8,128)S(1)} %shard_map.111.refs_0_), channel_id=1, source_target_pairs={{0,24},{4,28},{8,16},{12,20},{16,8},{20,12},{24,0},{28,4},{1,25},{... | collective-permute-start | bytes 196616 | tf_op jit(solution)/shard_map/ppermute | solution.py:33
  83.5 1.8 %shard_map.113 = bf16[128,2048]{1,0:T(8,128)(2,1)} custom-call(s32[1]{0:T(128)} %bitcast.me_ref.mer_ref, s32[8,128]{1,0:T(8,128)S(1)} %shard_map.99.table_ref, f32[16,128,128]{2,1,0:T(8,128)S(1)} %shard_map.107.base_ref, bf16[4,128,128]{2,1,0:T(8,128)(2,1)S(1)} %collective-permute-done.31.sib_ref, bf16[12,128,128]{2,1,0:T(8,128)(2,1)S(1)} %collective-permute-done.32.fwd_ref, ...), custom_call_target="tpu_custom_call" | custom-call | bytes 2097152 | tf_op jit(solution)/shard_map/pallas_call | solution.py:21
  (81 shorter events, 18.8 us)
Async XLA Ops:
  0.6 9.8 %collective-permute-start.3 = (bf16[128,2048]{1,0:T(8,128)(2,1)}, bf16[128,2048]{1,0:T(8,128)(2,1)S(1)}, u32[]{:S(2)}, u32[]{:S(2)}) collective-permute-start(bf16[128,2048]{1,0:T(8,128)(2,1)} %feat_ref.1), channel_id=1, source_target_pairs={{0,4},{4,0},{8,12},{12,8},{16,20},{20,16},{24,28},{28,24},{1,5},{5... | collective-permute-start | bytes 1572872 | tf_op jit(solution)/shard_map/ppermute | solution.py:33
  2.8 7.9 %collective-permute-start.2 = (s32[8,128]{1,0:T(8,128)S(1)}, s32[8,128]{1,0:T(8,128)S(1)}, u32[]{:S(2)}, u32[]{:S(2)}) collective-permute-start(s32[8,128]{1,0:T(8,128)S(1)} %shard_map.94), channel_id=1, source_target_pairs={{0,24},{4,28},{8,16},{12,20},{16,8},{20,12},{24,0},{28,4},{1,25},{... | collective-permute-start | bytes 12296 | tf_op jit(solution)/shard_map/ppermute | solution.py:33
  11.5 11.6 %collective-permute-start.4 = (bf16[8,128,128]{2,1,0:T(8,128)(2,1)S(1)}, bf16[8,128,128]{2,1,0:T(8,128)(2,1)S(1)}, u32[]{:S(2)}, u32[]{:S(2)}) collective-permute-start(bf16[8,128,128]{2,1,0:T(8,128)(2,1)S(1)} %get-tuple-element.86), channel_id=1, source_target_pairs={{0,8},{4,12},{8,0},{12,4},{16,24},{20,28},{24,16},{28,20},{1,9},{5... | collective-permute-start | bytes 786440 | tf_op jit(solution)/shard_map/ppermute | solution.py:33
  13.5 13.2 %collective-permute-start.5 = (bf16[8,128,128]{2,1,0:T(8,128)(2,1)S(1)}, bf16[8,128,128]{2,1,0:T(8,128)(2,1)S(1)}, u32[]{:S(2)}, u32[]{:S(2)}) collective-permute-start(bf16[8,128,128]{2,1,0:T(8,128)(2,1)S(1)} %get-tuple-element.87), channel_id=1, source_target_pairs={{0,16},{4,20},{8,24},{12,28},{16,0},{20,4},{24,8},{28,12},{1,17},{... | collective-permute-start | bytes 786440 | tf_op jit(solution)/shard_map/ppermute | solution.py:33
  15.0 11.7 %collective-permute-start.6 = (bf16[8,128,128]{2,1,0:T(8,128)(2,1)S(1)}, bf16[8,128,128]{2,1,0:T(8,128)(2,1)S(1)}, u32[]{:S(2)}, u32[]{:S(2)}) collective-permute-start(bf16[8,128,128]{2,1,0:T(8,128)(2,1)S(1)} %get-tuple-element.88), channel_id=1, source_target_pairs={{0,24},{4,28},{8,16},{12,20},{16,8},{20,12},{24,0},{28,4},{1,25},{... | collective-permute-start | bytes 786440 | tf_op jit(solution)/shard_map/ppermute | solution.py:33
  15.1 7.9 %collective-permute-start.7 = (s32[32,128]{1,0:T(8,128)S(1)}, s32[32,128]{1,0:T(8,128)S(1)}, u32[]{:S(2)}, u32[]{:S(2)}) collective-permute-start(s32[32,128]{1,0:T(8,128)S(1)} %pad_add_fusion), channel_id=1, source_target_pairs={{0,4},{4,0},{8,12},{12,8},{16,20},{20,16},{24,28},{28,24},{1,5},{5... | collective-permute-start | bytes 49160 | tf_op jit(solution)/shard_map/ppermute | solution.py:33
  15.2 17.0 %collective-permute-start.11 = (bf16[128,512]{1,0:T(8,128)(2,1)S(1)}, bf16[128,512]{1,0:T(8,128)(2,1)S(1)}, u32[]{:S(2)}, u32[]{:S(2)}) collective-permute-start(bf16[128,512]{1,0:T(8,128)(2,1)S(1)} %get-tuple-element.106), channel_id=1, source_target_pairs={{0,3},{1,2},{2,1},{3,0},{4,7},{5,6},{6,5},{7,4},{8,11},{9,10},{10,... | collective-permute-start | bytes 393224 | tf_op jit(solution)/shard_map/ppermute | solution.py:33
  23.0 10.2 %collective-permute-start.12 = (bf16[128,512]{1,0:T(8,128)(2,1)S(1)}, bf16[128,512]{1,0:T(8,128)(2,1)S(1)}, u32[]{:S(2)}, u32[]{:S(2)}) collective-permute-start(bf16[128,512]{1,0:T(8,128)(2,1)S(1)} %get-tuple-element.107), channel_id=1, source_target_pairs={{0,2},{1,3},{2,0},{3,1},{4,6},{5,7},{6,4},{7,5},{8,10},{9,11},{10,... | collective-permute-start | bytes 393224 | tf_op jit(solution)/shard_map/ppermute | solution.py:33
  23.1 10.1 %collective-permute-start.13 = (bf16[128,512]{1,0:T(8,128)(2,1)S(1)}, bf16[128,512]{1,0:T(8,128)(2,1)S(1)}, u32[]{:S(2)}, u32[]{:S(2)}) collective-permute-start(bf16[128,512]{1,0:T(8,128)(2,1)S(1)} %get-tuple-element.108), channel_id=1, source_target_pairs={{0,1},{1,0},{2,3},{3,2},{4,5},{5,4},{6,7},{7,6},{8,9},{9,8},{10,11... | collective-permute-start | bytes 393224 | tf_op jit(solution)/shard_map/ppermute | solution.py:33
  28.5 8.0 %collective-permute-start.8 = (bf16[128,512]{1,0:T(8,128)(2,1)S(1)}, bf16[128,512]{1,0:T(8,128)(2,1)S(1)}, u32[]{:S(2)}, u32[]{:S(2)}) collective-permute-start(bf16[128,512]{1,0:T(8,128)(2,1)S(1)} %get-tuple-element.102), channel_id=1, source_target_pairs={{0,3},{1,2},{2,1},{3,0},{4,7},{5,6},{6,5},{7,4},{8,11},{9,10},{10,... | collective-permute-start | bytes 393224 | tf_op jit(solution)/shard_map/ppermute | solution.py:33
  32.2 10.0 %collective-permute-start.9 = (bf16[128,512]{1,0:T(8,128)(2,1)S(1)}, bf16[128,512]{1,0:T(8,128)(2,1)S(1)}, u32[]{:S(2)}, u32[]{:S(2)}) collective-permute-start(bf16[128,512]{1,0:T(8,128)(2,1)S(1)} %get-tuple-element.103), channel_id=1, source_target_pairs={{0,2},{1,3},{2,0},{3,1},{4,6},{5,7},{6,4},{7,5},{8,10},{9,11},{10,... | collective-permute-start | bytes 393224 | tf_op jit(solution)/shard_map/ppermute | solution.py:33
  32.2 10.0 %collective-permute-start.10 = (bf16[128,512]{1,0:T(8,128)(2,1)S(1)}, bf16[128,512]{1,0:T(8,128)(2,1)S(1)}, u32[]{:S(2)}, u32[]{:S(2)}) collective-permute-start(bf16[128,512]{1,0:T(8,128)(2,1)S(1)} %get-tuple-element.104), channel_id=1, source_target_pairs={{0,1},{1,0},{2,3},{3,2},{4,5},{5,4},{6,7},{7,6},{8,9},{9,8},{10,11... | collective-permute-start | bytes 393224 | tf_op jit(solution)/shard_map/ppermute | solution.py:33
  43.5 9.1 %collective-permute-start.14 = (bf16[128,512]{1,0:T(8,128)(2,1)S(1)}, bf16[128,512]{1,0:T(8,128)(2,1)S(1)}, u32[]{:S(2)}, u32[]{:S(2)}) collective-permute-start(bf16[128,512]{1,0:T(8,128)(2,1)S(1)} %get-tuple-element.110), channel_id=1, source_target_pairs={{0,3},{1,2},{2,1},{3,0},{4,7},{5,6},{6,5},{7,4},{8,11},{9,10},{10,... | collective-permute-start | bytes 393224 | tf_op jit(solution)/shard_map/ppermute | solution.py:33
  46.0 10.9 %collective-permute-start.15 = (bf16[128,512]{1,0:T(8,128)(2,1)S(1)}, bf16[128,512]{1,0:T(8,128)(2,1)S(1)}, u32[]{:S(2)}, u32[]{:S(2)}) collective-permute-start(bf16[128,512]{1,0:T(8,128)(2,1)S(1)} %get-tuple-element.111), channel_id=1, source_target_pairs={{0,2},{1,3},{2,0},{3,1},{4,6},{5,7},{6,4},{7,5},{8,10},{9,11},{10,... | collective-permute-start | bytes 393224 | tf_op jit(solution)/shard_map/ppermute | solution.py:33
  46.0 10.9 %collective-permute-start.16 = (bf16[128,512]{1,0:T(8,128)(2,1)S(1)}, bf16[128,512]{1,0:T(8,128)(2,1)S(1)}, u32[]{:S(2)}, u32[]{:S(2)}) collective-permute-start(bf16[128,512]{1,0:T(8,128)(2,1)S(1)} %get-tuple-element.112), channel_id=1, source_target_pairs={{0,1},{1,0},{2,3},{3,2},{4,5},{5,4},{6,7},{7,6},{8,9},{9,8},{10,11... | collective-permute-start | bytes 393224 | tf_op jit(solution)/shard_map/ppermute | solution.py:33
  49.3 7.6 %collective-permute-start.18 = (bf16[64,512]{1,0:T(8,128)(2,1)S(1)}, bf16[64,512]{1,0:T(8,128)(2,1)S(1)}, u32[]{:S(2)}, u32[]{:S(2)}) collective-permute-start(bf16[64,512]{1,0:T(8,128)(2,1)S(1)} %get-tuple-element.115), channel_id=1, source_target_pairs={{0,24},{4,28},{8,16},{12,20},{16,8},{20,12},{24,0},{28,4},{1,25},{... | collective-permute-start | bytes 196616 | tf_op jit(solution)/shard_map/ppermute | solution.py:33
  57.8 8.4 %collective-permute-start.24 = (bf16[144,512]{1,0:T(8,128)(2,1)S(1)}, bf16[144,512]{1,0:T(8,128)(2,1)S(1)}, u32[]{:S(2)}, u32[]{:S(2)}) collective-permute-start(bf16[144,512]{1,0:T(8,128)(2,1)S(1)} %get-tuple-element.132), channel_id=1, source_target_pairs={{0,3},{1,2},{2,1},{3,0},{4,7},{5,6},{6,5},{7,4},{8,11},{9,10},{10,... | collective-permute-start | bytes 442376 | tf_op jit(solution)/shard_map/ppermute | solution.py:33
  62.6 12.8 %collective-permute-start.21 = (bf16[8,128,128]{2,1,0:T(8,128)(2,1)S(1)}, bf16[8,128,128]{2,1,0:T(8,128)(2,1)S(1)}, u32[]{:S(2)}, u32[]{:S(2)}) collective-permute-start(bf16[8,128,128]{2,1,0:T(8,128)(2,1)S(1)} %get-tuple-element.123), channel_id=1, source_target_pairs={{0,24},{4,28},{8,16},{12,20},{16,8},{20,12},{24,0},{28,4},{1,25},{... | collective-permute-start | bytes 786440 | tf_op jit(solution)/shard_map/ppermute | solution.py:33
  64.7 13.2 %collective-permute-start.22 = (bf16[8,128,128]{2,1,0:T(8,128)(2,1)S(1)}, bf16[8,128,128]{2,1,0:T(8,128)(2,1)S(1)}, u32[]{:S(2)}, u32[]{:S(2)}) collective-permute-start(bf16[8,128,128]{2,1,0:T(8,128)(2,1)S(1)} %get-tuple-element.124), channel_id=1, source_target_pairs={{0,16},{4,20},{8,24},{12,28},{16,0},{20,4},{24,8},{28,12},{1,17},{... | collective-permute-start | bytes 786440 | tf_op jit(solution)/shard_map/ppermute | solution.py:33
  65.2 12.7 %collective-permute-start.23 = (bf16[8,128,128]{2,1,0:T(8,128)(2,1)S(1)}, bf16[8,128,128]{2,1,0:T(8,128)(2,1)S(1)}, u32[]{:S(2)}, u32[]{:S(2)}) collective-permute-start(bf16[8,128,128]{2,1,0:T(8,128)(2,1)S(1)} %get-tuple-element.125), channel_id=1, source_target_pairs={{0,8},{4,12},{8,0},{12,4},{16,24},{20,28},{24,16},{28,20},{1,9},{5... | collective-permute-start | bytes 786440 | tf_op jit(solution)/shard_map/ppermute | solution.py:33
  66.2 9.1 %collective-permute-start.25 = (bf16[144,512]{1,0:T(8,128)(2,1)S(1)}, bf16[144,512]{1,0:T(8,128)(2,1)S(1)}, u32[]{:S(2)}, u32[]{:S(2)}) collective-permute-start(bf16[144,512]{1,0:T(8,128)(2,1)S(1)} %get-tuple-element.133), channel_id=1, source_target_pairs={{0,2},{1,3},{2,0},{3,1},{4,6},{5,7},{6,4},{7,5},{8,10},{9,11},{10,... | collective-permute-start | bytes 442376 | tf_op jit(solution)/shard_map/ppermute | solution.py:33
  66.2 9.2 %collective-permute-start.26 = (bf16[144,512]{1,0:T(8,128)(2,1)S(1)}, bf16[144,512]{1,0:T(8,128)(2,1)S(1)}, u32[]{:S(2)}, u32[]{:S(2)}) collective-permute-start(bf16[144,512]{1,0:T(8,128)(2,1)S(1)} %get-tuple-element.134), channel_id=1, source_target_pairs={{0,1},{1,0},{2,3},{3,2},{4,5},{5,4},{6,7},{7,6},{8,9},{9,8},{10,11... | collective-permute-start | bytes 442376 | tf_op jit(solution)/shard_map/ppermute | solution.py:33
  77.9 5.5 %collective-permute-start.32 = (bf16[12,128,128]{2,1,0:T(8,128)(2,1)S(1)}, bf16[12,128,128]{2,1,0:T(8,128)(2,1)S(1)}, u32[]{:S(2)}, u32[]{:S(2)}) collective-permute-start(bf16[12,128,128]{2,1,0:T(8,128)(2,1)S(1)} %shard_map.112), channel_id=1, source_target_pairs={{0,4},{4,0},{8,12},{12,8},{16,20},{20,16},{24,28},{28,24},{1,5},{5... | collective-permute-start | bytes 1179656 | tf_op jit(solution)/shard_map/ppermute | solution.py:33
  78.1 5.4 %collective-permute-start.31 = (bf16[4,128,128]{2,1,0:T(8,128)(2,1)S(1)}, bf16[4,128,128]{2,1,0:T(8,128)(2,1)S(1)}, u32[]{:S(2)}, u32[]{:S(2)}) collective-permute-start(bf16[4,128,128]{2,1,0:T(8,128)(2,1)S(1)} %get-tuple-element.140), channel_id=1, source_target_pairs={{0,4},{4,0},{8,12},{12,8},{16,20},{20,16},{24,28},{28,24},{1,5},{5... | collective-permute-start | bytes 393224 | tf_op jit(solution)/shard_map/ppermute | solution.py:33
  (15 other events, 102.9 us)

commit v7 on v6

--- a/solution.py
+++ b/solution.py
@@ -149,7 +149,7 @@
     lax.fori_loop(0, list_ref[4 + which, 0], step, 0)
 
 
-def load_kernel(in_ref, out_ref, sems):
+def load_kernel(in_ref, after_ref, out_ref, sems):
     n = in_ref.shape[0] // LOADS
     copies = [
         pltpu.make_async_copy(
@@ -418,36 +418,36 @@
         (features, sib_feat),
         nbytes=f_loc * nodes * 8,
     )
-    tile_values, mer, mec = lax.optimization_barrier((tile_values, mer, mec))
+    needs, x_near, mer, mec = lax.optimization_barrier((needs, x_near, mer, mec))
+    sends = call(
+        functools.partial(send_kernel, n_chip, row_tiles),
+        [sds((per, f_loc, TILE), BF)] * (n_chip - 1),
+        [],
+        (mer, *needs[1:]),
+        (x_near,),
+        nbytes=4 * n_chip * per * f_loc * TILE,
+    )
+    got = [swap(x, "row", n_row, 2 * (e + 1)) for e, x in enumerate(sends)]
+    needs, sends, lists_in, out_grad = lax.optimization_barrier(
+        (needs, sends, (tile_cols, tile_rows), out_grad)
+    )
+    lists = call(
+        functools.partial(lists_kernel, n_row, row_tiles),
+        sds((8, length), jnp.int32),
+        [],
+        (tile_count, mer),
+        lists_in,
+    )
+    tile_values, sends = lax.optimization_barrier((tile_values, sends))
     tile_values = pl.pallas_call(
         load_kernel,
         out_shape=sds(tile_values.shape, BF),
-        in_specs=[pl.BlockSpec(memory_space=pltpu.HBM)],
+        in_specs=[pl.BlockSpec(memory_space=pltpu.HBM), VM],
         out_specs=VM,
         scratch_shapes=[pltpu.SemaphoreType.DMA((LOADS,))],
         compiler_params=pltpu.CompilerParams(vmem_limit_bytes=24 << 20),
         cost_estimate=pl.CostEstimate(flops=0, bytes_accessed=tile_bytes, transcendentals=0),
-    )(pltpu.with_memory_space_constraint(tile_values, pltpu.HBM))
-    needs, x_near, tile_values = lax.optimization_barrier((needs, x_near, tile_values))
-    sends = call(
-        functools.partial(send_kernel, n_chip, row_tiles),
-        [sds((per, f_loc, TILE), BF)] * (n_chip - 1),
-        [],
-        (mer, *needs[1:]),
-        (x_near,),
-        nbytes=4 * n_chip * per * f_loc * TILE,
-    )
-    got = [swap(x, "row", n_row, 2 * (e + 1)) for e, x in enumerate(sends)]
-    needs, sends, lists_in, out_grad = lax.optimization_barrier(
-        (needs, sends, (tile_cols, tile_rows), out_grad)
-    )
-    lists = call(
-        functools.partial(lists_kernel, n_row, row_tiles),
-        sds((8, length), jnp.int32),
-        [],
-        (tile_count, mer),
-        lists_in,
-    )
+    )(pltpu.with_memory_space_constraint(tile_values, pltpu.HBM), sends[0])
     table = jnp.concatenate(needs, axis=0)
     table = jnp.concatenate([table, over_chips(table)], axis=0)
     table = call(

time: 88 us -> 90.7 us (1.031)
  local copies, waits for them, and re-layouts: 0.72 us -> 4.13 us
    unnamed x16, local copies, waits for them, and re-layouts: 0.71 us -> 4.12 us
  transfers between devices with their start and end apart: 33 -> 33, of which waited for: 10 -> 14; matrix products, arithmetic and copies ran while one was open for 0% -> 0% of each run, Pallas kernels for 21% -> 20%
where the time goes in v7:
time: 90.7 us; the launch traced here: 90.4 us
  starting transfers between devices  37.3 us (41%)
  waiting for transfers between devices  25.8 us (28%)
  Pallas kernels  21.5 us (24%)
  local copies, waits for them, and re-layouts  4.13 us (5%)
  between operations  1.53 us (2%)
    ppermute x33, starting transfers between devices, swap(): return lax.ppermute(x, axis, [(i, i ^ k) for i in range(n)])  37.3 us
    ppermute x33, waiting for transfers between devices, swap(): return lax.ppermute(x, axis, [(i, i ^ k) for i in range(n)])  25.8 us
    pallas_call x20, Pallas kernels, call(): pl.pallas_call(kernel, out_shape=outs, in_specs=[SM] * len(smem) + [VM] *...  18 us
    unnamed x16, local copies, waits for them, and re-layouts  4.12 us
    pallas_call x1, Pallas kernels, shards(): pl.pallas_call(load_kernel, out_shape=sds(tile_values.shape, BF), in_spec...  3.48 us
  transfers between devices with their start and end apart: 33, of which 14 were waited for; matrix products, arithmetic and copies ran while one was open for 0% of the time, Pallas kernels for 20%

profile of v7, /device:TPU:0, one launch (start us, length us, event | category | flops | bytes accessed | tf_op | source)
XLA Modules:
  0.0 90.4 jit_solution(7685787787703626796)
XLA Ops:
  2.8 3.5 %collective-permute-start.2 = (s32[8,128]{1,0:T(8,128)S(1)}, s32[8,128]{1,0:T(8,128)S(1)}, u32[]{:S(2)}, u32[]{:S(2)}) collective-permute-start(s32[8,128]{1,0:T(8,128)S(1)} %shard_map.94), channel_id=1, source_target_pairs={{0,24},{4,28},{8,16},{12,20},{16,8},{20,12},{24,0},{28,4},{1,25},{... | collective-permute-start | bytes 12296 | tf_op jit(solution)/shard_map/ppermute | solution.py:33
  8.2 1.7 %collective-permute-done.1.refs_1_ = s32[8,128]{1,0:T(8,128)S(1)} collective-permute-done((s32[8,128]{1,0:T(8,128)S(1)}, s32[8,128]{1,0:T(8,128)S(1)}, u32[]{:S(2)}, u32[]{:S(2)}) %collective-permute-start.1) | collective-permute-done | bytes 4128 | tf_op jit(solution)/shard_map/ppermute | solution.py:33
  11.4 1.9 %collective-permute-start.5 = (bf16[8,128,128]{2,1,0:T(8,128)(2,1)S(1)}, bf16[8,128,128]{2,1,0:T(8,128)(2,1)S(1)}, u32[]{:S(2)}, u32[]{:S(2)}) collective-permute-start(bf16[8,128,128]{2,1,0:T(8,128)(2,1)S(1)} %get-tuple-element.87), channel_id=1, source_target_pairs={{0,16},{4,20},{8,24},{12,28},{16,0},{20,4},{24,8},{28,12},{1,17},{... | collective-permute-start | bytes 786440 | tf_op jit(solution)/shard_map/ppermute | solution.py:33
  13.3 1.4 %collective-permute-start.6 = (bf16[8,128,128]{2,1,0:T(8,128)(2,1)S(1)}, bf16[8,128,128]{2,1,0:T(8,128)(2,1)S(1)}, u32[]{:S(2)}, u32[]{:S(2)}) collective-permute-start(bf16[8,128,128]{2,1,0:T(8,128)(2,1)S(1)} %get-tuple-element.88), channel_id=1, source_target_pairs={{0,24},{4,28},{8,16},{12,20},{16,8},{20,12},{24,0},{28,4},{1,25},{... | collective-permute-start | bytes 786440 | tf_op jit(solution)/shard_map/ppermute | solution.py:33
  15.9 3.7 %collective-permute-start.11 = (bf16[128,512]{1,0:T(8,128)(2,1)S(1)}, bf16[128,512]{1,0:T(8,128)(2,1)S(1)}, u32[]{:S(2)}, u32[]{:S(2)}) collective-permute-start(bf16[128,512]{1,0:T(8,128)(2,1)S(1)} %get-tuple-element.108), channel_id=1, source_target_pairs={{0,3},{1,2},{2,1},{3,0},{4,7},{5,6},{6,5},{7,4},{8,11},{9,10},{10,... | collective-permute-start | bytes 393224 | tf_op jit(solution)/shard_map/ppermute | solution.py:33
  21.0 1.5 %shard_map.97.list_ref = s32[8,384]{1,0:T(8,128)S(1)} custom-call(s32[1]{0:T(128)S(6)} %copy.14.count_ref, s32[1]{0:T(128)} %bitcast.me_ref.mer_ref, s32[1,256]{1,0:T(1,128)S(1)} %copy-done.4, s32[1,256]{1,0:T(1,128)S(1)} %copy-done.5), custom_call_target="tpu_custom_call" | custom-call | tf_op jit(solution)/shard_map/pallas_call | solution.py:21
  22.5 3.5 %shard_map.98.tiles_ref = bf16[256,128,128]{2,1,0:T(8,128)(2,1)S(1)} custom-call(bf16[256,128,128]{2,1,0:T(8,128)(2,1)} %in_ref, bf16[8,128,128]{2,1,0:T(8,128)(2,1)S(1)} %get-tuple-element.94.after_ref), custom_call_target="tpu_custom_call" | custom-call | bytes 8388608 | tf_op jit(solution)/shard_map/pallas_call | solution.py:442
  26.0 2.2 %shard_map.100.refs_3_ = f32[16,128,128]{2,1,0:T(8,128)S(1)} custom-call(s32[8,384]{1,0:T(8,128)S(1)} %shard_map.97.list_ref, bf16[256,128,128]{2,1,0:T(8,128)(2,1)S(1)} %shard_map.98.tiles_ref, bf16[33,128,128]{2,1,0:T(8,128)(2,1)S(1)} %shard_map.95.refs_3_.x_ref), custom_call_target="tpu_custom_call" | custom-call | flops 1073741824 | bytes 8388608 | tf_op jit(solution)/shard_map/pallas_call | solution.py:21
  29.1 1.8 %shard_map.101 = (bf16[128,512]{1,0:T(8,128)(2,1)S(1)}, bf16[128,512]{1,0:T(8,128)(2,1)S(1)}, bf16[128,512]{1,0:T(8,128)(2,1)S(1)}, bf16[128,512]{1,0:T(8,128)(2,1)S(1)}) custom-call(s32[8,384]{1,0:T(8,128)S(1)} %shard_map.97.list_ref, s32[1]{0:T(128)} %bitcast.1.me_ref.mec_ref, bf16[256,128,128]{2,1,0:T(8,128)(2,1)S(1)} %shard_map.98.tiles_ref, ...), custom_call_target="tpu_custom_call" | custom-call | flops 1073741824 | bytes 8388608 | tf_op jit(solution)/shard_map/pallas_call | solution.py:21
  31.0 3.7 %collective-permute-start.8 = (bf16[128,512]{1,0:T(8,128)(2,1)S(1)}, bf16[128,512]{1,0:T(8,128)(2,1)S(1)}, u32[]{:S(2)}, u32[]{:S(2)}) collective-permute-start(bf16[128,512]{1,0:T(8,128)(2,1)S(1)} %get-tuple-element.104), channel_id=1, source_target_pairs={{0,3},{1,2},{2,1},{3,0},{4,7},{5,6},{6,5},{7,4},{8,11},{9,10},{10,... | collective-permute-start | bytes 393224 | tf_op jit(solution)/shard_map/ppermute | solution.py:33
  35.6 5.3 %collective-permute-done.12.refs_5_ = bf16[128,512]{1,0:T(8,128)(2,1)S(1)} collective-permute-done((bf16[128,512]{1,0:T(8,128)(2,1)S(1)}, bf16[128,512]{1,0:T(8,128)(2,1)S(1)}, u32[]{:S(2)}, u32[]{:S(2)}) %collective-permute-start.12) | collective-permute-done | bytes 131104 | tf_op jit(solution)/shard_map/ppermute | solution.py:33
  40.9 6.4 %collective-permute-done.9.refs_1_ = bf16[128,512]{1,0:T(8,128)(2,1)S(1)} collective-permute-done((bf16[128,512]{1,0:T(8,128)(2,1)S(1)}, bf16[128,512]{1,0:T(8,128)(2,1)S(1)}, u32[]{:S(2)}, u32[]{:S(2)}) %collective-permute-start.9) | collective-permute-done | bytes 131104 | tf_op jit(solution)/shard_map/ppermute | solution.py:33
  50.0 3.1 %collective-permute-start.16 = (bf16[128,512]{1,0:T(8,128)(2,1)S(1)}, bf16[128,512]{1,0:T(8,128)(2,1)S(1)}, u32[]{:S(2)}, u32[]{:S(2)}) collective-permute-start(bf16[128,512]{1,0:T(8,128)(2,1)S(1)} %get-tuple-element.114), channel_id=1, source_target_pairs={{0,1},{1,0},{2,3},{3,2},{4,5},{5,4},{6,7},{7,6},{8,9},{9,8},{10,11... | collective-permute-start | bytes 393224 | tf_op jit(solution)/shard_map/ppermute | solution.py:33
  54.5 1.6 %collective-permute-start.18 = (bf16[64,512]{1,0:T(8,128)(2,1)S(1)}, bf16[64,512]{1,0:T(8,128)(2,1)S(1)}, u32[]{:S(2)}, u32[]{:S(2)}) collective-permute-start(bf16[64,512]{1,0:T(8,128)(2,1)S(1)} %get-tuple-element.117), channel_id=1, source_target_pairs={{0,24},{4,28},{8,16},{12,20},{16,8},{20,12},{24,0},{28,4},{1,25},{... | collective-permute-start | bytes 196616 | tf_op jit(solution)/shard_map/ppermute | solution.py:33
  58.1 4.0 %collective-permute-done.15.refs_1_ = bf16[128,512]{1,0:T(8,128)(2,1)S(1)} collective-permute-done((bf16[128,512]{1,0:T(8,128)(2,1)S(1)}, bf16[128,512]{1,0:T(8,128)(2,1)S(1)}, u32[]{:S(2)}, u32[]{:S(2)}) %collective-permute-start.15) | collective-permute-done | bytes 131104 | tf_op jit(solution)/shard_map/ppermute | solution.py:33
  62.9 1.4 %collective-permute-start.24 = (bf16[144,512]{1,0:T(8,128)(2,1)S(1)}, bf16[144,512]{1,0:T(8,128)(2,1)S(1)}, u32[]{:S(2)}, u32[]{:S(2)}) collective-permute-start(bf16[144,512]{1,0:T(8,128)(2,1)S(1)} %get-tuple-element.134), channel_id=1, source_target_pairs={{0,3},{1,2},{2,1},{3,0},{4,7},{5,6},{6,5},{7,4},{8,11},{9,10},{10,... | collective-permute-start | bytes 442376 | tf_op jit(solution)/shard_map/ppermute | solution.py:33
  64.3 2.4 %shard_map.106 = (bf16[128,2048]{1,0:T(8,128)(2,1)S(1)}, bf16[4,128,128]{2,1,0:T(8,128)(2,1)S(1)}, bf16[8,128,128]{2,1,0:T(8,128)(2,1)S(1)}, bf16[8,128,128]{2,1,0:T(8,128)(2,1)S(1)}, bf16[8,128,128]{2,1,0:T(8,128)(2,1)S(1)}) custom-call(s32[8,384]{1,0:T(8,128)S(1)} %shard_map.97.list_ref, s32[1]{0:T(128)} %bitcast.1.me_ref.mec_ref, s32[1]{0:T(128)} %bitcast.me_ref.mer_ref, ...), custom_call_target="tpu_custom_call" | custom-call | flops 1073741824 | bytes 8388608 | tf_op jit(solution)/shard_map/pallas_call | solution.py:21
  66.7 1.6 %collective-permute-start.21 = (bf16[8,128,128]{2,1,0:T(8,128)(2,1)S(1)}, bf16[8,128,128]{2,1,0:T(8,128)(2,1)S(1)}, u32[]{:S(2)}, u32[]{:S(2)}) collective-permute-start(bf16[8,128,128]{2,1,0:T(8,128)(2,1)S(1)} %get-tuple-element.125), channel_id=1, source_target_pairs={{0,24},{4,28},{8,16},{12,20},{16,8},{20,12},{24,0},{28,4},{1,25},{... | collective-permute-start | bytes 786440 | tf_op jit(solution)/shard_map/ppermute | solution.py:33
  68.3 1.8 %collective-permute-start.22 = (bf16[8,128,128]{2,1,0:T(8,128)(2,1)S(1)}, bf16[8,128,128]{2,1,0:T(8,128)(2,1)S(1)}, u32[]{:S(2)}, u32[]{:S(2)}) collective-permute-start(bf16[8,128,128]{2,1,0:T(8,128)(2,1)S(1)} %get-tuple-element.126), channel_id=1, source_target_pairs={{0,16},{4,20},{8,24},{12,28},{16,0},{20,4},{24,8},{28,12},{1,17},{... | collective-permute-start | bytes 786440 | tf_op jit(solution)/shard_map/ppermute | solution.py:33
  70.6 2.7 %collective-permute-start.26 = (bf16[144,512]{1,0:T(8,128)(2,1)S(1)}, bf16[144,512]{1,0:T(8,128)(2,1)S(1)}, u32[]{:S(2)}, u32[]{:S(2)}) collective-permute-start(bf16[144,512]{1,0:T(8,128)(2,1)S(1)} %get-tuple-element.136), channel_id=1, source_target_pairs={{0,1},{1,0},{2,3},{3,2},{4,5},{5,4},{6,7},{7,6},{8,9},{9,8},{10,11... | collective-permute-start | bytes 442376 | tf_op jit(solution)/shard_map/ppermute | solution.py:33
  73.3 1.8 %shard_map.107.base_ref = f32[16,128,128]{2,1,0:T(8,128)S(1)} custom-call(s32[8,384]{1,0:T(8,128)S(1)} %shard_map.97.list_ref, bf16[256,128,128]{2,1,0:T(8,128)(2,1)S(1)} %shard_map.98.tiles_ref, bf16[128,2048]{1,0:T(8,128)(2,1)S(1)} %get-tuple-element.128.wide_ref), custom_call_target="tpu_custom_call" | custom-call | flops 1073741824 | bytes 8388608 | tf_op jit(solution)/shard_map/pallas_call | solution.py:21
  75.1 3.2 %collective-permute-done.25.refs_1_.refs_2_ = bf16[144,512]{1,0:T(8,128)(2,1)S(1)} collective-permute-done((bf16[144,512]{1,0:T(8,128)(2,1)S(1)}, bf16[144,512]{1,0:T(8,128)(2,1)S(1)}, u32[]{:S(2)}, u32[]{:S(2)}) %collective-permute-start.25) | collective-permute-done | bytes 147488 | tf_op jit(solution)/shard_map/ppermute | solution.py:33
  78.7 1.8 %collective-permute-done.22.refs_1_ = bf16[8,128,128]{2,1,0:T(8,128)(2,1)S(1)} collective-permute-done((bf16[8,128,128]{2,1,0:T(8,128)(2,1)S(1)}, bf16[8,128,128]{2,1,0:T(8,128)(2,1)S(1)}, u32[]{:S(2)}, u32[]{:S(2)}) %collective-permute-start.22) | collective-permute-done | bytes 262176 | tf_op jit(solution)/shard_map/ppermute | solution.py:33
  86.6 1.8 %shard_map.113 = bf16[128,2048]{1,0:T(8,128)(2,1)} custom-call(s32[1]{0:T(128)} %bitcast.me_ref.mer_ref, s32[8,128]{1,0:T(8,128)S(1)} %shard_map.99.table_ref, f32[16,128,128]{2,1,0:T(8,128)S(1)} %shard_map.107.base_ref, bf16[4,128,128]{2,1,0:T(8,128)(2,1)S(1)} %collective-permute-done.31.sib_ref, bf16[12,128,128]{2,1,0:T(8,128)(2,1)S(1)} %collective-permute-done.32.fwd_ref, ...), custom_call_target="tpu_custom_call" | custom-call | bytes 2097152 | tf_op jit(solution)/shard_map/pallas_call | solution.py:21
  (81 shorter events, 25.0 us)
Async XLA Ops:
  0.6 6.3 %collective-permute-start.3 = (bf16[128,2048]{1,0:T(8,128)(2,1)}, bf16[128,2048]{1,0:T(8,128)(2,1)S(1)}, u32[]{:S(2)}, u32[]{:S(2)}) collective-permute-start(bf16[128,2048]{1,0:T(8,128)(2,1)} %feat_ref.1), channel_id=1, source_target_pairs={{0,4},{4,0},{8,12},{12,8},{16,20},{20,16},{24,28},{28,24},{1,5},{5... | collective-permute-start | bytes 1572872 | tf_op jit(solution)/shard_map/ppermute | solution.py:33
  11.2 17.1 %collective-permute-start.4 = (bf16[8,128,128]{2,1,0:T(8,128)(2,1)S(1)}, bf16[8,128,128]{2,1,0:T(8,128)(2,1)S(1)}, u32[]{:S(2)}, u32[]{:S(2)}) collective-permute-start(bf16[8,128,128]{2,1,0:T(8,128)(2,1)S(1)} %get-tuple-element.94.after_ref), channel_id=1, source_target_pairs={{0,8},{4,12},{8,0},{12,4},{16,24},{20,28},{24,16},{28,20},{1,9},{5... | collective-permute-start | bytes 786440 | tf_op jit(solution)/shard_map/ppermute | solution.py:33
  11.4 17.7 %collective-permute-start.5 = (bf16[8,128,128]{2,1,0:T(8,128)(2,1)S(1)}, bf16[8,128,128]{2,1,0:T(8,128)(2,1)S(1)}, u32[]{:S(2)}, u32[]{:S(2)}) collective-permute-start(bf16[8,128,128]{2,1,0:T(8,128)(2,1)S(1)} %get-tuple-element.87), channel_id=1, source_target_pairs={{0,16},{4,20},{8,24},{12,28},{16,0},{20,4},{24,8},{28,12},{1,17},{... | collective-permute-start | bytes 786440 | tf_op jit(solution)/shard_map/ppermute | solution.py:33
  13.3 15.8 %collective-permute-start.6 = (bf16[8,128,128]{2,1,0:T(8,128)(2,1)S(1)}, bf16[8,128,128]{2,1,0:T(8,128)(2,1)S(1)}, u32[]{:S(2)}, u32[]{:S(2)}) collective-permute-start(bf16[8,128,128]{2,1,0:T(8,128)(2,1)S(1)} %get-tuple-element.88), channel_id=1, source_target_pairs={{0,24},{4,28},{8,16},{12,20},{16,8},{20,12},{24,0},{28,4},{1,25},{... | collective-permute-start | bytes 786440 | tf_op jit(solution)/shard_map/ppermute | solution.py:33
  14.8 13.4 %collective-permute-start.7 = (s32[32,128]{1,0:T(8,128)S(1)}, s32[32,128]{1,0:T(8,128)S(1)}, u32[]{:S(2)}, u32[]{:S(2)}) collective-permute-start(s32[32,128]{1,0:T(8,128)S(1)} %pad_add_fusion), channel_id=1, source_target_pairs={{0,4},{4,0},{8,12},{12,8},{16,20},{20,16},{24,28},{28,24},{1,5},{5... | collective-permute-start | bytes 49160 | tf_op jit(solution)/shard_map/ppermute | solution.py:33
  15.9 18.7 %collective-permute-start.11 = (bf16[128,512]{1,0:T(8,128)(2,1)S(1)}, bf16[128,512]{1,0:T(8,128)(2,1)S(1)}, u32[]{:S(2)}, u32[]{:S(2)}) collective-permute-start(bf16[128,512]{1,0:T(8,128)(2,1)S(1)} %get-tuple-element.108), channel_id=1, source_target_pairs={{0,3},{1,2},{2,1},{3,0},{4,7},{5,6},{6,5},{7,4},{8,11},{9,10},{10,... | collective-permute-start | bytes 393224 | tf_op jit(solution)/shard_map/ppermute | solution.py:33
  28.2 12.8 %collective-permute-start.12 = (bf16[128,512]{1,0:T(8,128)(2,1)S(1)}, bf16[128,512]{1,0:T(8,128)(2,1)S(1)}, u32[]{:S(2)}, u32[]{:S(2)}) collective-permute-start(bf16[128,512]{1,0:T(8,128)(2,1)S(1)} %get-tuple-element.109), channel_id=1, source_target_pairs={{0,2},{1,3},{2,0},{3,1},{4,6},{5,7},{6,4},{7,5},{8,10},{9,11},{10,... | collective-permute-start | bytes 393224 | tf_op jit(solution)/shard_map/ppermute | solution.py:33
  28.3 12.6 %collective-permute-start.13 = (bf16[128,512]{1,0:T(8,128)(2,1)S(1)}, bf16[128,512]{1,0:T(8,128)(2,1)S(1)}, u32[]{:S(2)}, u32[]{:S(2)}) collective-permute-start(bf16[128,512]{1,0:T(8,128)(2,1)S(1)} %get-tuple-element.110), channel_id=1, source_target_pairs={{0,1},{1,0},{2,3},{3,2},{4,5},{5,4},{6,7},{7,6},{8,9},{9,8},{10,11... | collective-permute-start | bytes 393224 | tf_op jit(solution)/shard_map/ppermute | solution.py:33
  31.0 10.0 %collective-permute-start.8 = (bf16[128,512]{1,0:T(8,128)(2,1)S(1)}, bf16[128,512]{1,0:T(8,128)(2,1)S(1)}, u32[]{:S(2)}, u32[]{:S(2)}) collective-permute-start(bf16[128,512]{1,0:T(8,128)(2,1)S(1)} %get-tuple-element.104), channel_id=1, source_target_pairs={{0,3},{1,2},{2,1},{3,0},{4,7},{5,6},{6,5},{7,4},{8,11},{9,10},{10,... | collective-permute-start | bytes 393224 | tf_op jit(solution)/shard_map/ppermute | solution.py:33
  34.6 12.8 %collective-permute-start.9 = (bf16[128,512]{1,0:T(8,128)(2,1)S(1)}, bf16[128,512]{1,0:T(8,128)(2,1)S(1)}, u32[]{:S(2)}, u32[]{:S(2)}) collective-permute-start(bf16[128,512]{1,0:T(8,128)(2,1)S(1)} %get-tuple-element.105), channel_id=1, source_target_pairs={{0,2},{1,3},{2,0},{3,1},{4,6},{5,7},{6,4},{7,5},{8,10},{9,11},{10,... | collective-permute-start | bytes 393224 | tf_op jit(solution)/shard_map/ppermute | solution.py:33
  34.6 12.8 %collective-permute-start.10 = (bf16[128,512]{1,0:T(8,128)(2,1)S(1)}, bf16[128,512]{1,0:T(8,128)(2,1)S(1)}, u32[]{:S(2)}, u32[]{:S(2)}) collective-permute-start(bf16[128,512]{1,0:T(8,128)(2,1)S(1)} %get-tuple-element.106), channel_id=1, source_target_pairs={{0,1},{1,0},{2,3},{3,2},{4,5},{5,4},{6,7},{7,6},{8,9},{9,8},{10,11... | collective-permute-start | bytes 393224 | tf_op jit(solution)/shard_map/ppermute | solution.py:33
  48.7 8.3 %collective-permute-start.14 = (bf16[128,512]{1,0:T(8,128)(2,1)S(1)}, bf16[128,512]{1,0:T(8,128)(2,1)S(1)}, u32[]{:S(2)}, u32[]{:S(2)}) collective-permute-start(bf16[128,512]{1,0:T(8,128)(2,1)S(1)} %get-tuple-element.112), channel_id=1, source_target_pairs={{0,3},{1,2},{2,1},{3,0},{4,7},{5,6},{6,5},{7,4},{8,11},{9,10},{10,... | collective-permute-start | bytes 393224 | tf_op jit(solution)/shard_map/ppermute | solution.py:33
  50.0 12.0 %collective-permute-start.15 = (bf16[128,512]{1,0:T(8,128)(2,1)S(1)}, bf16[128,512]{1,0:T(8,128)(2,1)S(1)}, u32[]{:S(2)}, u32[]{:S(2)}) collective-permute-start(bf16[128,512]{1,0:T(8,128)(2,1)S(1)} %get-tuple-element.113), channel_id=1, source_target_pairs={{0,2},{1,3},{2,0},{3,1},{4,6},{5,7},{6,4},{7,5},{8,10},{9,11},{10,... | collective-permute-start | bytes 393224 | tf_op jit(solution)/shard_map/ppermute | solution.py:33
  50.0 12.0 %collective-permute-start.16 = (bf16[128,512]{1,0:T(8,128)(2,1)S(1)}, bf16[128,512]{1,0:T(8,128)(2,1)S(1)}, u32[]{:S(2)}, u32[]{:S(2)}) collective-permute-start(bf16[128,512]{1,0:T(8,128)(2,1)S(1)} %get-tuple-element.114), channel_id=1, source_target_pairs={{0,1},{1,0},{2,3},{3,2},{4,5},{5,4},{6,7},{7,6},{8,9},{9,8},{10,11... | collective-permute-start | bytes 393224 | tf_op jit(solution)/shard_map/ppermute | solution.py:33
  54.5 7.5 %collective-permute-start.18 = (bf16[64,512]{1,0:T(8,128)(2,1)S(1)}, bf16[64,512]{1,0:T(8,128)(2,1)S(1)}, u32[]{:S(2)}, u32[]{:S(2)}) collective-permute-start(bf16[64,512]{1,0:T(8,128)(2,1)S(1)} %get-tuple-element.117), channel_id=1, source_target_pairs={{0,24},{4,28},{8,16},{12,20},{16,8},{20,12},{24,0},{28,4},{1,25},{... | collective-permute-start | bytes 196616 | tf_op jit(solution)/shard_map/ppermute | solution.py:33
  56.1 6.0 %collective-permute-start.19 = (bf16[64,512]{1,0:T(8,128)(2,1)S(1)}, bf16[64,512]{1,0:T(8,128)(2,1)S(1)}, u32[]{:S(2)}, u32[]{:S(2)}) collective-permute-start(bf16[64,512]{1,0:T(8,128)(2,1)S(1)} %get-tuple-element.118), channel_id=1, source_target_pairs={{0,16},{4,20},{8,24},{12,28},{16,0},{20,4},{24,8},{28,12},{1,17},{... | collective-permute-start | bytes 196616 | tf_op jit(solution)/shard_map/ppermute | solution.py:33
  62.9 7.7 %collective-permute-start.24 = (bf16[144,512]{1,0:T(8,128)(2,1)S(1)}, bf16[144,512]{1,0:T(8,128)(2,1)S(1)}, u32[]{:S(2)}, u32[]{:S(2)}) collective-permute-start(bf16[144,512]{1,0:T(8,128)(2,1)S(1)} %get-tuple-element.134), channel_id=1, source_target_pairs={{0,3},{1,2},{2,1},{3,0},{4,7},{5,6},{6,5},{7,4},{8,11},{9,10},{10,... | collective-permute-start | bytes 442376 | tf_op jit(solution)/shard_map/ppermute | solution.py:33
  66.7 11.9 %collective-permute-start.21 = (bf16[8,128,128]{2,1,0:T(8,128)(2,1)S(1)}, bf16[8,128,128]{2,1,0:T(8,128)(2,1)S(1)}, u32[]{:S(2)}, u32[]{:S(2)}) collective-permute-start(bf16[8,128,128]{2,1,0:T(8,128)(2,1)S(1)} %get-tuple-element.125), channel_id=1, source_target_pairs={{0,24},{4,28},{8,16},{12,20},{16,8},{20,12},{24,0},{28,4},{1,25},{... | collective-permute-start | bytes 786440 | tf_op jit(solution)/shard_map/ppermute | solution.py:33
  68.3 12.1 %collective-permute-start.22 = (bf16[8,128,128]{2,1,0:T(8,128)(2,1)S(1)}, bf16[8,128,128]{2,1,0:T(8,128)(2,1)S(1)}, u32[]{:S(2)}, u32[]{:S(2)}) collective-permute-start(bf16[8,128,128]{2,1,0:T(8,128)(2,1)S(1)} %get-tuple-element.126), channel_id=1, source_target_pairs={{0,16},{4,20},{8,24},{12,28},{16,0},{20,4},{24,8},{28,12},{1,17},{... | collective-permute-start | bytes 786440 | tf_op jit(solution)/shard_map/ppermute | solution.py:33
  70.1 10.9 %collective-permute-start.23 = (bf16[8,128,128]{2,1,0:T(8,128)(2,1)S(1)}, bf16[8,128,128]{2,1,0:T(8,128)(2,1)S(1)}, u32[]{:S(2)}, u32[]{:S(2)}) collective-permute-start(bf16[8,128,128]{2,1,0:T(8,128)(2,1)S(1)} %get-tuple-element.127), channel_id=1, source_target_pairs={{0,8},{4,12},{8,0},{12,4},{16,24},{20,28},{24,16},{28,20},{1,9},{5... | collective-permute-start | bytes 786440 | tf_op jit(solution)/shard_map/ppermute | solution.py:33
  70.3 8.0 %collective-permute-start.25 = (bf16[144,512]{1,0:T(8,128)(2,1)S(1)}, bf16[144,512]{1,0:T(8,128)(2,1)S(1)}, u32[]{:S(2)}, u32[]{:S(2)}) collective-permute-start(bf16[144,512]{1,0:T(8,128)(2,1)S(1)} %get-tuple-element.135), channel_id=1, source_target_pairs={{0,2},{1,3},{2,0},{3,1},{4,6},{5,7},{6,4},{7,5},{8,10},{9,11},{10,... | collective-permute-start | bytes 442376 | tf_op jit(solution)/shard_map/ppermute | solution.py:33
  70.6 8.0 %collective-permute-start.26 = (bf16[144,512]{1,0:T(8,128)(2,1)S(1)}, bf16[144,512]{1,0:T(8,128)(2,1)S(1)}, u32[]{:S(2)}, u32[]{:S(2)}) collective-permute-start(bf16[144,512]{1,0:T(8,128)(2,1)S(1)} %get-tuple-element.136), channel_id=1, source_target_pairs={{0,1},{1,0},{2,3},{3,2},{4,5},{5,4},{6,7},{7,6},{8,9},{9,8},{10,11... | collective-permute-start | bytes 442376 | tf_op jit(solution)/shard_map/ppermute | solution.py:33
  81.0 5.5 %collective-permute-start.32 = (bf16[12,128,128]{2,1,0:T(8,128)(2,1)S(1)}, bf16[12,128,128]{2,1,0:T(8,128)(2,1)S(1)}, u32[]{:S(2)}, u32[]{:S(2)}) collective-permute-start(bf16[12,128,128]{2,1,0:T(8,128)(2,1)S(1)} %shard_map.112), channel_id=1, source_target_pairs={{0,4},{4,0},{8,12},{12,8},{16,20},{20,16},{24,28},{28,24},{1,5},{5... | collective-permute-start | bytes 1179656 | tf_op jit(solution)/shard_map/ppermute | solution.py:33
  81.1 5.4 %collective-permute-start.31 = (bf16[4,128,128]{2,1,0:T(8,128)(2,1)S(1)}, bf16[4,128,128]{2,1,0:T(8,128)(2,1)S(1)}, u32[]{:S(2)}, u32[]{:S(2)}) collective-permute-start(bf16[4,128,128]{2,1,0:T(8,128)(2,1)S(1)} %get-tuple-element.142), channel_id=1, source_target_pairs={{0,4},{4,0},{8,12},{12,8},{16,20},{20,16},{24,28},{28,24},{1,5},{5... | collective-permute-start | bytes 393224 | tf_op jit(solution)/shard_map/ppermute | solution.py:33
  (15 other events, 52.0 us)
